TPU v7x, 512 devices: a whole 4x4x16 slice. The times are simulated.
512 devices in a mesh: gy: 32 (over z, core), gx: 16 (over x, y).
Axes of the slice: x: 4, y: 4, z: 16, core: 2. Of those that a mesh axis runs over, the one named last changes fastest.
Arguments:
- level_in: bfloat16 [256, 1024, 128], P('gy', 'gx'), may hold values from -6 to 6
- w_level: bfloat16 [3, 3, 128, 128], replicated, may hold values from -0.1875 to 0.1875
- w_down: bfloat16 [2, 2, 128, 256], replicated, may hold values from -0.25 to 0.25
- w_neck: bfloat16 [3, 3, 256, 256], replicated, may hold values from -0.125 to 0.125
- cotangent: bfloat16 [128, 512, 256], P('gy', None, 'gx'), may hold values from -6 to 6
Outputs:
- neck_out: bfloat16 [128, 512, 256], P('gy', None, 'gx')
- grad_input: bfloat16 [256, 1024, 128], P('gy', 'gx')
- grad_level: bfloat16 [3, 3, 128, 128], replicated
- grad_down: bfloat16 [2, 2, 128, 256], replicated
- grad_neck: bfloat16 [3, 3, 256, 256], replicated
All inputs are finite; a program needn't handle non-finite values.
Results may differ from a plain program's by a relative error of at most 0.012.
Values may be sent and summed in bfloat16 or wider, within the bound.
A program may use at most 64 MiB of HBM per device.

v0:
```python
import math

import jax
import jax.numpy as jnp
from jax import lax
from jax.sharding import PartitionSpec as P


def extended(cells, sides, width):
    for axis, dim in sides:
        count = lax.axis_size(axis)
        ends = count - 1
        head = lax.slice_in_dim(cells, 0, width, axis=dim)
        tail = lax.slice_in_dim(cells, cells.shape[dim] - width, cells.shape[dim], axis=dim)
        cells = jnp.concatenate(
            [
                lax.ppermute(tail, axis, [(i, (i + 1) % count) for i in range(ends)]),
                cells,
                lax.ppermute(head, axis, [((i + 1) % count, i) for i in range(ends)]),
            ],
            axis=dim,
        )
    return cells


def slope_of(value):
    gate = jax.nn.sigmoid(value)
    return gate + value * gate * (1.0 - gate)


def tile_rims(field_in):
    return extended(field_in, (("gy", 0), ("gx", 1)), 1)


def conv_padded(padded, weights):
    row_count = padded.shape[0] - 2
    col_count = padded.shape[1] - 2
    result = jnp.zeros((row_count * col_count, weights.shape[3]), jnp.float32)
    for offset_y in range(3):
        for offset_x in range(3):
            window = padded[offset_y : offset_y + row_count, offset_x : offset_x + col_count]
            window = window.reshape(row_count * col_count, padded.shape[2])
            result = result + jnp.dot(
                window, weights[offset_y, offset_x], preferred_element_type=jnp.float32
            )
    return result


def weight_terms(padded, grads):
    row_count = grads.shape[0]
    col_count = grads.shape[1]
    flat_grads = grads.reshape(row_count * col_count, grads.shape[2])
    kernel_rows = []
    for offset_y in range(3):
        kernel_row = []
        for offset_x in range(3):
            window = padded[offset_y : offset_y + row_count, offset_x : offset_x + col_count]
            window = window.reshape(row_count * col_count, padded.shape[2])
            kernel_row.append(
                lax.dot_general(
                    window, flat_grads, (((0,), (0,)), ((), ())), preferred_element_type=jnp.float32
                )
            )
        kernel_rows.append(jnp.stack(kernel_row))
    return jnp.stack(kernel_rows)


def local(level_in, w_level, w_down, w_neck, cotangent):
    tile_rows = level_in.shape[0]
    tile_cols = level_in.shape[1]
    level_width = level_in.shape[2]
    neck_width = w_neck.shape[3]
    half_rows = tile_rows // 2
    half_cols = tile_cols // 2
    level_pad = tile_rims(level_in)
    level_pre = conv_padded(level_pad, w_level)
    level_flat = level_in.reshape(tile_rows * tile_cols, level_width).astype(jnp.float32)
    level_act = (level_flat + jax.nn.silu(level_pre)).astype(jnp.bfloat16)
    level_grid = level_act.reshape(half_rows, 2, half_cols, 2, level_width)
    neck_in = jnp.einsum(
        "hpwqc,pqcd->hwd", level_grid, w_down, preferred_element_type=jnp.float32
    ).astype(jnp.bfloat16)
    neck_pad = tile_rims(neck_in)
    neck_pre = conv_padded(neck_pad, w_neck)
    neck_flat = neck_in.reshape(half_rows * half_cols, neck_width).astype(jnp.float32)
    neck_tile = (
        (neck_flat + jax.nn.silu(neck_pre))
        .astype(jnp.bfloat16)
        .reshape(half_rows, half_cols, neck_width)
    )
    neck_out = lax.all_to_all(neck_tile, "gx", split_axis=2, concat_axis=1, tiled=True)
    neck_cot = lax.all_to_all(cotangent, "gx", split_axis=1, concat_axis=2, tiled=True)
    cot_flat = neck_cot.reshape(half_rows * half_cols, neck_width).astype(jnp.float32)
    neck_gate = (
        (cot_flat * slope_of(neck_pre))
        .astype(jnp.bfloat16)
        .reshape(half_rows, half_cols, neck_width)
    )
    flip_neck = jnp.transpose(w_neck[::-1, ::-1], (0, 1, 3, 2))
    gate_pad = tile_rims(neck_gate)
    neck_back = conv_padded(gate_pad, flip_neck)
    cot_tile = neck_cot.reshape(half_rows * half_cols, neck_width).astype(jnp.float32)
    neck_grad = (
        (cot_tile + neck_back).astype(jnp.bfloat16).reshape(half_rows, half_cols, neck_width)
    )
    neck_wgrad = weight_terms(neck_pad, neck_gate)
    level_back = jnp.einsum(
        "hwd,pqcd->hpwqc", neck_grad, w_down, preferred_element_type=jnp.float32
    )
    level_back = level_back.reshape(tile_rows * tile_cols, level_width)
    down_wgrad = jnp.einsum(
        "hpwqc,hwd->pqcd", level_grid, neck_grad, preferred_element_type=jnp.float32
    )
    level_gate = (
        (level_back * slope_of(level_pre))
        .astype(jnp.bfloat16)
        .reshape(tile_rows, tile_cols, level_width)
    )
    flip_level = jnp.transpose(w_level[::-1, ::-1], (0, 1, 3, 2))
    level_gpad = tile_rims(level_gate)
    grad_input = (level_back + conv_padded(level_gpad, flip_level)).astype(jnp.bfloat16)
    grad_input = grad_input.reshape(tile_rows, tile_cols, level_width)
    level_wgrad = weight_terms(level_pad, level_gate)
    device_count = lax.axis_size("gy") * lax.axis_size("gx")
    level_count = tile_rows * tile_cols * device_count
    level_scale = 1.0 / math.sqrt(level_count)
    neck_scale = 1.0 / math.sqrt(level_count // 4)
    reduced = lax.psum((level_wgrad, down_wgrad, neck_wgrad), ("gy", "gx"))
    grad_level = (reduced[0] * level_scale).astype(jnp.bfloat16)
    grad_down = (reduced[1] * neck_scale).astype(jnp.bfloat16)
    grad_neck = (reduced[2] * neck_scale).astype(jnp.bfloat16)
    return (neck_out, grad_input, grad_level, grad_down, grad_neck)


def solution(mesh):
    return jax.shard_map(
        local,
        mesh=mesh,
        in_specs=(P("gy", "gx", None), P(), P(), P(), P("gy", None, "gx")),
        out_specs=(P("gy", None, "gx"), P("gy", "gx", None), P(), P(), P()),
        check_vma=False,
    )
```

profile of v0, /device:TPU:1, one launch (start us, length us, event | category | flops | bytes accessed | tf_op | source)
XLA Modules:
  0.0 617.6 jit_solution(6595421685957169687)
XLA Ops:
  7.2 1.3 copy.37
  8.5 1.2 reshape.213
  9.7 7.6 %all-to-all-start.1 = ((bf16[16,2,1024]{2,1,0:T(2,128)(2,1)}), bf16[16,2,1024]{2,1,0:T(2,128)(2,1)S(1)}, u32[]{:S(2)}, u32[]{:S(2)}) async-start(bf16[16,2,1024]{2,1,0:T(2,128)(2,1)} %reshape.213), calls=%async_computation.1 | async-start | bytes 131072 | tf_op jit(solution)/shard_map/all_to_all | solution.py:92
  17.3 4.4 collective-permute-start
  21.7 2.1 collective-permute-start.1
  23.9 3.3 collective-permute-done.1
  27.3 3.3 collective-permute-start.2
  30.6 1.3 collective-permute-start.3
  32.3 2.7 collective-permute-done.3
  36.3 0.9 add_convert_fusion
  38.1 1.9 collective-permute-start.5
  40.1 3.6 collective-permute-start.4
  44.6 3.1 collective-permute-start.6
  47.7 1.3 collective-permute-start.7
  50.2 1.8 collective-permute-done.7
  53.0 0.8 convolution_add_fusion.21
  53.9 0.8 fusion.19
  54.7 1.2 reshape.214
  55.9 1.4 copy.38
  57.3 0.9 reshape.205
  58.2 1.0 copy.40
  59.9 1.9 multiply_convert_fusion.4
  63.5 0.9 convolution_bitcast_fusion.6
  64.4 0.9 convolution_bitcast_fusion.7
  65.3 0.9 convolution_bitcast_fusion.8
  66.2 0.9 convolution_bitcast_fusion.9
  67.1 1.0 copy.34
  68.2 0.9 reshape.211
  69.1 9.1 %all-to-all-start = ((bf16[16,2,1024]{2,1,0:T(2,128)(2,1)}), bf16[16,2,1024]{2,1,0:T(2,128)(2,1)S(1)}, u32[]{:S(2)}, u32[]{:S(2)}) async-start(bf16[16,2,1024]{2,1,0:T(2,128)(2,1)} %reshape.211), calls=%async_computation | async-start | bytes 131072 | tf_op jit(solution)/shard_map/all_to_all | solution.py:91
  78.2 2.1 collective-permute-start.9
  80.3 5.5 collective-permute-start.8
  86.0 0.9 copy-done.18
  87.1 1.5 pad_maximum_fusion
  88.6 3.5 collective-permute-start.10
  92.2 1.3 collective-permute-start.11
  93.7 2.8 collective-permute-done.11
  101.2 1.9 collective-permute-start.13
  103.1 4.0 collective-permute-start.12
  107.1 0.9 pad_maximum_fusion.1
  108.0 1.1 convolution_bitcast_fusion
  109.1 3.2 collective-permute-start.14
  112.4 1.3 collective-permute-start.15
  113.9 2.8 collective-permute-done.15
  118.3 0.9 fusion.4
  119.5 0.9 all_to_all.23
  120.3 484.8 %all-reduce.3.cloned.1.call-done = (f32[3,3,128,128]{3,2,1,0:T(8,128)}, f32[2,2,128,256]{3,2,1,0:T(8,128)}, f32[3,3,256,256]{3,2,1,0:T(8,128)}) async-done(((f32[3,3,128,128]{3,2,1,0:T(8,128)}, f32[2,2,128,256]{3,2,1,0:T(8,128)}, f32[3,3,256,256]{3,2,1,0:T(8,128)}), (f32[3,3,128,128]{3,2,1,0:T(8,128)}, f32[2,2,128,256]{3,2,1,0:T(8,128)}, f32[3,3,256,256]{3,2,1,0:T(8,128)})) %all-reduce.3.cloned.1.call-update) | async-done | bytes 3473424 | tf_op jit(solution)/shard_map/psum | solution.py:128
  605.2 1.9 multiply_convert_fusion.1
  607.8 2.9 multiply_convert_fusion
  (184 shorter events, 15.8 us)
Async XLA Ops:
  7.2 30.8 %copy-start = (bf16[2,2,128,256]{3,2,1,0:T(8,128)(2,1)S(1)}, bf16[2,2,128,256]{3,2,1,0:T(8,128)(2,1)}, u32[]{:S(2)}) copy-start(bf16[2,2,128,256]{3,2,1,0:T(8,128)(2,1)} %param.7) | copy-start | bytes 786436
  7.2 10.1 %copy-start.2 = (bf16[8,64,128]{2,1,0:T(8,128)(2,1)S(1)}, bf16[8,64,128]{2,1,0:T(8,128)(2,1)}, u32[]{:S(2)}) copy-start(bf16[8,64,128]{2,1,0:T(8,128)(2,1)} %param.5) | copy-start | bytes 393220
  7.2 16.6 %copy-start.1 = (bf16[3,3,256,256]{3,2,1,0:T(8,128)(2,1)S(1)}, bf16[3,3,256,256]{3,2,1,0:T(8,128)(2,1)}, u32[]{:S(2)}) copy-start(bf16[3,3,256,256]{3,2,1,0:T(8,128)(2,1)} %param.8) | copy-start | bytes 3538948
  9.7 45.0 %all-to-all-start.1 = ((bf16[16,2,1024]{2,1,0:T(2,128)(2,1)}), bf16[16,2,1024]{2,1,0:T(2,128)(2,1)S(1)}, u32[]{:S(2)}, u32[]{:S(2)}) async-start(bf16[16,2,1024]{2,1,0:T(2,128)(2,1)} %reshape.213), calls=%async_computation.1 | async-start | bytes 131072 | tf_op jit(solution)/shard_map/all_to_all | solution.py:92
  17.3 6.6 %collective-permute-start = (bf16[1,64,128]{2,1,0:T(8,128)(2,1)S(1)}, bf16[1,64,128]{2,1,0:T(8,128)(2,1)S(1)}, u32[]{:S(2)}, u32[]{:S(2)}) collective-permute-start(bf16[1,64,128]{2,1,0:T(8,128)(2,1)S(1)} %get-tuple-element.39), channel_id=1, source_target_pairs={{0,16},{16,32},{32,48},{48,64},{64,80},{80,96},{96,112},{112,128},... | collective-permute-start | bytes 49160 | tf_op jit(solution)/shard_map/ppermute | solution.py:17
  21.7 10.2 %copy-start.16 = (bf16[3,3,128,128]{3,2,1,0:T(8,128)(2,1)S(1)}, bf16[3,3,128,128]{3,2,1,0:T(8,128)(2,1)}, u32[]{:S(2)}) copy-start(bf16[3,3,128,128]{3,2,1,0:T(8,128)(2,1)} %param.6) | copy-start | bytes 884740
  21.7 5.5 collective-permute-start.1
  27.3 8.3 %copy-start.3 = (bf16[8,64,128]{2,1,0:T(8,128)(2,1)}, bf16[8,64,128]{2,1,0:T(8,128)(2,1)S(1)}, u32[]{:S(2)}) copy-start(bf16[8,64,128]{2,1,0:T(8,128)(2,1)S(1)} %get-tuple-element.37) | copy-start | bytes 393220
  27.3 4.9 collective-permute-start.2
  30.6 4.4 collective-permute-start.3
  35.2 1.1 copy-start.38
  38.1 6.3 %collective-permute-start.5 = (bf16[1,32,256]{2,1,0:T(8,128)(2,1)S(1)}, bf16[1,32,256]{2,1,0:T(8,128)(2,1)S(1)}, u32[]{:S(2)}, u32[]{:S(2)}) collective-permute-start(bf16[1,32,256]{2,1,0:T(8,128)(2,1)S(1)} %get-tuple-element.67), channel_id=1, source_target_pairs={{16,0},{32,16},{48,32},{64,48},{80,64},{96,80},{112,96},{128,112},... | collective-permute-start | bytes 49160 | tf_op jit(solution)/shard_map/ppermute | solution.py:19
  40.1 4.5 collective-permute-start.4
  44.6 5.2 collective-permute-start.6
  47.7 4.4 collective-permute-start.7
  52.1 1.7 copy-start.23
  52.2 1.7 copy-start.25
  52.2 1.7 copy-start.27
  52.2 1.7 copy-start.29
  52.2 1.7 copy-start.31
  58.2 4.2 copy-start.32
  58.2 4.4 copy-start.41
  58.2 4.6 copy-start.30
  61.8 1.7 copy-start.28
  62.4 2.0 copy-start.26
  62.6 2.7 copy-start.22
  62.8 3.4 copy-start.24
  63.5 14.7 %copy-start.42 = (bf16[1,32,256]{2,1,0:T(8,128)(2,1)S(1)}, bf16[1,32,256]{2,1,0:T(8,128)(2,1)}, u32[]{:S(2)}) copy-start(bf16[1,32,256]{2,1,0:T(8,128)(2,1)} %get-tuple-element.63) | copy-start | bytes 49156
  69.1 16.8 %copy-start.17 = (f32[1,256,256]{2,1,0:T(8,128)S(1)}, f32[1,256,256]{2,1,0:T(8,128)}, u32[]{:S(2)}) copy-start(f32[1,256,256]{2,1,0:T(8,128)} %convolution_bitcast_fusion.6) | copy-start | bytes 786436
  69.1 50.1 %all-to-all-start = ((bf16[16,2,1024]{2,1,0:T(2,128)(2,1)}), bf16[16,2,1024]{2,1,0:T(2,128)(2,1)S(1)}, u32[]{:S(2)}, u32[]{:S(2)}) async-start(bf16[16,2,1024]{2,1,0:T(2,128)(2,1)} %reshape.211), calls=%async_computation | async-start | bytes 131072 | tf_op jit(solution)/shard_map/all_to_all | solution.py:91
  78.2 527.0 %all-reduce.3.cloned.1.call-start = ((), (), s32[]{:S(2)}) async-start(), calls=%async_computation.2 | async-start | bytes 6946816 | tf_op jit(solution)/shard_map/psum | solution.py:128
  78.2 10.4 %collective-permute-start.9 = (bf16[1,32,256]{2,1,0:T(8,128)(2,1)S(1)}, bf16[1,32,256]{2,1,0:T(8,128)(2,1)S(1)}, u32[]{:S(2)}, u32[]{:S(2)}) collective-permute-start(bf16[1,32,256]{2,1,0:T(8,128)(2,1)S(1)} %copy-done.42), channel_id=1, source_target_pairs={{16,0},{32,16},{48,32},{64,48},{80,64},{96,80},{112,96},{128,112},... | collective-permute-start | bytes 49160 | tf_op jit(solution)/shard_map/ppermute | solution.py:19
  80.3 8.3 %collective-permute-start.8 = (bf16[1,32,256]{2,1,0:T(8,128)(2,1)S(1)}, bf16[1,32,256]{2,1,0:T(8,128)(2,1)S(1)}, u32[]{:S(2)}, u32[]{:S(2)}) collective-permute-start(bf16[1,32,256]{2,1,0:T(8,128)(2,1)S(1)} %get-tuple-element.62), channel_id=1, source_target_pairs={{0,16},{16,32},{32,48},{48,64},{64,80},{80,96},{96,112},{112,128},... | collective-permute-start | bytes 49160 | tf_op jit(solution)/shard_map/ppermute | solution.py:17
  85.9 1.1 copy-start.20
  88.6 5.1 collective-permute-start.10
  92.2 4.4 collective-permute-start.11
  98.3 1.2 copy-start.39
  98.6 1.2 copy-start.14
  98.8 1.4 copy-start.12
  99.0 1.5 copy-start.10
  99.3 1.7 copy-start.8
  101.2 7.9 %collective-permute-start.13 = (bf16[1,64,128]{2,1,0:T(8,128)(2,1)S(1)}, bf16[1,64,128]{2,1,0:T(8,128)(2,1)S(1)}, u32[]{:S(2)}, u32[]{:S(2)}) collective-permute-start(bf16[1,64,128]{2,1,0:T(8,128)(2,1)S(1)} %get-tuple-element.32), channel_id=1, source_target_pairs={{16,0},{32,16},{48,32},{64,48},{80,64},{96,80},{112,96},{128,112},... | collective-permute-start | bytes 49160 | tf_op jit(solution)/shard_map/ppermute | solution.py:19
  103.1 4.9 copy-start.37
  103.1 6.0 collective-permute-start.12
  109.1 4.6 copy-start.15
  109.1 4.8 collective-permute-start.14
  112.4 4.4 collective-permute-start.15
  605.2 1.9 copy-start.35
  (14 other events, 11.8 us)
Sparse Core Ops, SparseCore 0:
  109.2 495.9 all-reduce.2
where the time goes:
time: 620 us; the launch traced here: 618 us
  waiting for transfers between devices  498 us (80%)
  starting transfers between devices  60.5 us (10%)
  matrix products  19 us (3%)
  between operations  15.3 us (2%)
  local copies, waits for them, and re-layouts  15 us (2%)
  other arithmetic  9.4 us (2%)
    psum x1, waiting for transfers between devices, local(): reduced = lax.psum((level_wgrad, down_wgrad, neck_wgrad), ('gy', 'gx'))  485 us
    ppermute x8, starting transfers between devices, extended(): lax.ppermute(tail, axis, [(i, (i + 1) % count) for i in range(ends)])  30.6 us
    ppermute x8, waiting for transfers between devices, extended(): lax.ppermute(head, axis, [((i + 1) % count, i) for i in range(ends)])  13.5 us
    ppermute x8, starting transfers between devices, extended(): lax.ppermute(head, axis, [((i + 1) % count, i) for i in range(ends)])  13.2 us
  transfers between devices with their start and end apart: 19, of which 7 were waited for; matrix products, arithmetic and copies ran while one was open for 3% of the time, Pallas kernels for 0%

commit v1 on v0

--- a/solution.py
+++ b/solution.py
@@ -1,9 +1,14 @@
+import functools
 import math
 
 import jax
 import jax.numpy as jnp
 from jax import lax
+from jax.experimental import pallas as pl
+from jax.experimental.pallas import tpu as pltpu
 from jax.sharding import PartitionSpec as P
+
+MESH = pl.DeviceIdType.MESH
 
 
 def extended(cells, sides, width):
@@ -63,6 +68,225 @@
             )
         kernel_rows.append(jnp.stack(kernel_row))
     return jnp.stack(kernel_rows)
+
+
+TILES = 14
+HALF = 7
+LEVEL_OWNERS = 12
+
+
+def sums_kernel(
+    scales,
+    neck_ref, down_ref, level_ref,
+    neck_out, down_out, level_out,
+    pair_send, pair_recv, work, near_a, near_b, far_a, far_b, piece, z_recv, whole, fin,
+    pair_sems, near_sems, far_sems, z_sems, zb_sems, out1_sems, out2_sems,
+):
+    gy, gx = lax.axis_index("gy"), lax.axis_index("gx")
+    z, core = gy // 2, gy % 2
+    x, y = gx // 4, gx % 4
+    other = 1 - core
+
+    def at(zz, cc, xx, yy):
+        return (zz * 2 + cc, xx * 4 + yy)
+
+    pair_dev = at(z, other, x, y)
+    x_dev = [None] + [at(z, core, (x + k) % 4, y) for k in range(1, 4)]
+    y_dev = [None] + [at(z, core, x, (y + k) % 4) for k in range(1, 4)]
+    z_dev = [None] + [at((z + k) % 16, core, x, y) for k in range(1, 16)]
+
+    barrier = pltpu.get_barrier_semaphore()
+    peers = [pair_dev] + x_dev[1:] + y_dev[1:] + z_dev[1:]
+    for peer in peers:
+        pl.semaphore_signal(barrier, inc=1, device_id=peer, device_id_type=MESH)
+
+    def lanes(half):
+        return pl.ds(pl.multiple_of(half * 128, 128), 128)
+
+    def terms(half, o):
+        neck = neck_ref[pl.ds(pl.multiple_of(o * 144, 16), 144), lanes(half)]
+        down = down_ref[pl.ds(pl.multiple_of(o * 32, 16), 32), lanes(half)]
+        return neck.reshape(9, 16, 128), down.reshape(2, 16, 128)
+
+    def level_terms(half, o):
+        start = pl.multiple_of((half * LEVEL_OWNERS + o) * 48, 16)
+        return level_ref[pl.ds(start, 48), :].reshape(3, 16, 128)
+
+    def fill(o, carry):
+        neck, down = terms(other, o)
+        pair_send[o, 0:9] = neck.astype(jnp.bfloat16)
+        pair_send[o, 9:11] = down.astype(jnp.bfloat16)
+        return carry
+
+    def fill_level(o, carry):
+        pair_send[o, 11:14] = level_terms(other, o).astype(jnp.bfloat16)
+        return carry
+
+    lax.fori_loop(0, 16, fill, 0)
+    lax.fori_loop(0, LEVEL_OWNERS, fill_level, 0)
+    pair_send[LEVEL_OWNERS:, 11:14] = jnp.zeros((16 - LEVEL_OWNERS, 3, 16, 128), jnp.bfloat16)
+
+    pl.semaphore_wait(barrier, len(peers))
+
+    def copy(src, dst, sems, k, dev):
+        return pltpu.make_async_remote_copy(
+            src_ref=src, dst_ref=dst, send_sem=sems.at[0, k], recv_sem=sems.at[1, k],
+            device_id=dev, device_id_type=MESH,
+        )
+
+    pair = copy(pair_send, pair_recv, pair_sems, 0, pair_dev)
+    pair.start()
+    pair.wait()
+
+    def join(o, carry):
+        neck, down = terms(core, o)
+        xo, yo = o // 4, o % 4
+        work[xo, yo, 0:9] = (neck + pair_recv[o, 0:9].astype(jnp.float32)).astype(jnp.bfloat16)
+        work[xo, yo, 9:11] = (down + pair_recv[o, 9:11].astype(jnp.float32)).astype(jnp.bfloat16)
+        return carry
+
+    def join_level(o, carry):
+        total = level_terms(core, o) + pair_recv[o, 11:14].astype(jnp.float32)
+        work[o // 4, o % 4, 11:14] = total.astype(jnp.bfloat16)
+        return carry
+
+    lax.fori_loop(0, 16, join, 0)
+    lax.fori_loop(0, LEVEL_OWNERS, join_level, 0)
+    work[LEVEL_OWNERS // 4:, :, 11:14] = jnp.zeros((1, 4, 3, 16, 128), jnp.bfloat16)
+
+    stage = []
+    for k in range(1, 4):
+        xp, yp = (x + k) % 4, (y + k) % 4
+        stage.append(copy(work.at[xp, :, 0:HALF], near_a.at[k], near_sems, k, x_dev[k]))
+        stage.append(copy(work.at[:, yp, HALF:], near_b.at[k], near_sems, 4 + k, y_dev[k]))
+    for c in stage:
+        c.start()
+    for c in stage:
+        c.wait_recv()
+    f32 = jnp.float32
+    for p in range(4):
+        a = work[x, p, 0:HALF].astype(f32)
+        b = work[p, y, HALF:].astype(f32)
+        for k in range(1, 4):
+            a = a + near_a[k, p].astype(f32)
+            b = b + near_b[k, p].astype(f32)
+        near_a[0, p] = a.astype(jnp.bfloat16)
+        near_b[0, p] = b.astype(jnp.bfloat16)
+    for c in stage:
+        c.wait_send()
+    stage = []
+    for k in range(1, 4):
+        xp, yp = (x + k) % 4, (y + k) % 4
+        stage.append(copy(near_a.at[0, yp], far_a.at[k], far_sems, k, y_dev[k]))
+        stage.append(copy(near_b.at[0, xp], far_b.at[k], far_sems, 4 + k, x_dev[k]))
+    for c in stage:
+        c.start()
+    for c in stage:
+        c.wait_recv()
+    a = near_a[0, y].astype(f32)
+    b = near_b[0, x].astype(f32)
+    for k in range(1, 4):
+        a = a + far_a[k].astype(f32)
+        b = b + far_b[k].astype(f32)
+    piece[0:HALF] = a.astype(jnp.bfloat16)
+    piece[HALF:TILES] = b.astype(jnp.bfloat16)
+    piece[TILES:] = jnp.zeros((2, 16, 128), jnp.bfloat16)
+    for c in stage:
+        c.wait_send()
+
+    stage = [copy(piece.at[(z + k) % 16], z_recv.at[k], z_sems, k, z_dev[k]) for k in range(1, 16)]
+    for c in stage:
+        c.start()
+    for c in stage:
+        c.wait_recv()
+    total = piece[z].astype(f32)
+    for k in range(1, 16):
+        total = total + z_recv[k].astype(f32)
+    scale = jnp.where(z < 11, scales[0], scales[1])
+    fin[z] = (total * scale).astype(jnp.bfloat16)
+    for c in stage:
+        c.wait_send()
+
+    stage = []
+    for k in range(1, 16):
+        stage.append(copy(fin.at[z], fin.at[z], zb_sems, k, z_dev[k]))
+    for c in stage:
+        c.start()
+    for c in stage:
+        c.wait_recv()
+    for c in stage:
+        c.wait_send()
+    whole[core, x, y] = fin[0:TILES]
+    stage = []
+    for k in range(1, 4):
+        mine_a, mine_b = whole.at[core, x, y, 0:HALF], whole.at[core, x, y, HALF:]
+        stage.append(copy(mine_a, mine_a, out1_sems, k, y_dev[k]))
+        stage.append(copy(mine_b, mine_b, out1_sems, 4 + k, x_dev[k]))
+    for c in stage:
+        c.start()
+    for c in stage:
+        c.wait_recv()
+    for c in stage:
+        c.wait_send()
+    stage = []
+    for k in range(1, 4):
+        mine_a, mine_b = whole.at[core, x, :, 0:HALF], whole.at[core, :, y, HALF:]
+        stage.append(copy(mine_a, mine_a, out2_sems, k, x_dev[k]))
+        stage.append(copy(mine_b, mine_b, out2_sems, 4 + k, y_dev[k]))
+    for c in stage:
+        c.start()
+    for c in stage:
+        c.wait_recv()
+    for c in stage:
+        c.wait_send()
+    pair = copy(whole.at[core], whole.at[core], pair_sems, 1, pair_dev)
+    pair.start()
+    pair.wait()
+
+    for half in range(2):
+        def spread(o, carry, half=half):
+            xo, yo = o // 4, o % 4
+            cols = slice(half * 128, half * 128 + 128)
+            neck_out[pl.ds(pl.multiple_of(o * 144, 16), 144), cols] = whole[half, xo, yo, 0:9].reshape(144, 128)
+            down_out[pl.ds(pl.multiple_of(o * 32, 16), 32), cols] = whole[half, xo, yo, 9:11].reshape(32, 128)
+            return carry
+
+        def spread_level(o, carry, half=half):
+            start = pl.multiple_of((half * LEVEL_OWNERS + o) * 48, 16)
+            level_out[pl.ds(start, 48), :] = whole[half, o // 4, o % 4, 11:14].reshape(48, 128)
+            return carry
+
+        lax.fori_loop(0, 16, spread, 0)
+        lax.fori_loop(0, LEVEL_OWNERS, spread_level, 0)
+
+
+def summed(neck, down, level, neck_scale, level_scale):
+    bf16 = jnp.bfloat16
+    vmem = pl.BlockSpec(memory_space=pltpu.VMEM)
+    dma = pltpu.SemaphoreType.DMA
+    return pl.pallas_call(
+        functools.partial(sums_kernel, (neck_scale, level_scale)),
+        out_shape=[jax.ShapeDtypeStruct(t.shape, bf16) for t in (neck, down, level)],
+        in_specs=[vmem] * 3,
+        out_specs=[vmem] * 3,
+        scratch_shapes=[
+            pltpu.VMEM((16, TILES, 16, 128), bf16),
+            pltpu.VMEM((16, TILES, 16, 128), bf16),
+            pltpu.VMEM((4, 4, TILES, 16, 128), bf16),
+            pltpu.VMEM((4, 4, HALF, 16, 128), bf16),
+            pltpu.VMEM((4, 4, HALF, 16, 128), bf16),
+            pltpu.VMEM((4, HALF, 16, 128), bf16),
+            pltpu.VMEM((4, HALF, 16, 128), bf16),
+            pltpu.VMEM((16, 16, 128), bf16),
+            pltpu.VMEM((16, 16, 128), bf16),
+            pltpu.VMEM((2, 4, 4, TILES, 16, 128), bf16),
+            pltpu.VMEM((16, 16, 128), bf16),
+            dma((2, 2)), dma((2, 8)), dma((2, 8)), dma((2, 16)), dma((2, 16)), dma((2, 8)), dma((2, 8)),
+        ],
+        compiler_params=pltpu.CompilerParams(
+            collective_id=0, has_side_effects=True, vmem_limit_bytes=48 * 1024 * 1024
+        ),
+    )(neck, down, level)
 
 
 def local(level_in, w_level, w_down, w_neck, cotangent):
@@ -125,10 +349,16 @@
     level_count = tile_rows * tile_cols * device_count
     level_scale = 1.0 / math.sqrt(level_count)
     neck_scale = 1.0 / math.sqrt(level_count // 4)
-    reduced = lax.psum((level_wgrad, down_wgrad, neck_wgrad), ("gy", "gx"))
-    grad_level = (reduced[0] * level_scale).astype(jnp.bfloat16)
-    grad_down = (reduced[1] * neck_scale).astype(jnp.bfloat16)
-    grad_neck = (reduced[2] * neck_scale).astype(jnp.bfloat16)
+    neck_sum, down_sum, level_sum = summed(
+        neck_wgrad.reshape(9 * neck_width, neck_width),
+        down_wgrad.reshape(4 * level_width, neck_width),
+        level_wgrad.reshape(9 * level_width, level_width),
+        neck_scale,
+        level_scale,
+    )
+    grad_level = level_sum.reshape(w_level.shape)
+    grad_down = down_sum.reshape(w_down.shape)
+    grad_neck = neck_sum.reshape(w_neck.shape)
     return (neck_out, grad_input, grad_level, grad_down, grad_neck)
 
 

time: 620 us -> 185 us (0.30)
  waiting for transfers between devices: 498 us -> 12.5 us
  Pallas kernels: 0 us -> 69.8 us
  between operations: 15.3 us -> 1.93 us
  other arithmetic: 9.4 us -> 1.67 us
    psum x1 -> x0, waiting for transfers between devices: 485 us -> none  [local(): reduced = lax.psum((level_wgrad, down_wgrad, neck_wgrad), ('gy', 'gx'))]
    pallas_call x0 -> x1, Pallas kernels: none -> 69.8 us  [summed(): pl.pallas_call(functools.partial(sums_kernel, (neck_scale, level_scale)),...]
  transfers between devices with their start and end apart: 19 -> 18, of which waited for: 7 -> 5; matrix products, arithmetic and copies ran while one was open for 3% -> 11% of each run, Pallas kernels for 0% -> 38%
where the time goes in v1:
time: 185 us; the launch traced here: 182 us
  Pallas kernels  69.8 us (38%)
  starting transfers between devices  59.6 us (32%)
  local copies, waits for them, and re-layouts  18.7 us (10%)
  matrix products  18.3 us (10%)
  waiting for transfers between devices  12.5 us (7%)
  between operations  1.93 us (1%)
    pallas_call x1, Pallas kernels, summed(): pl.pallas_call(functools.partial(sums_kernel, (neck_scale, level_scale)),...  69.8 us
    ppermute x8, starting transfers between devices, extended(): lax.ppermute(tail, axis, [(i, (i + 1) % count) for i in range(ends)])  30.5 us
    ppermute x8, starting transfers between devices, extended(): lax.ppermute(head, axis, [((i + 1) % count, i) for i in range(ends)])  16.1 us
    ppermute x8, waiting for transfers between devices, extended(): lax.ppermute(head, axis, [((i + 1) % count, i) for i in range(ends)])  12.4 us
    dot_general x36, matrix products, conv_padded(): jnp.dot(window, weights[offset_y, offset_x], preferred_element_type=jnp.f...  11 us
    unnamed x89, local copies, waits for them, and re-layouts  9.9 us
    all_to_all x1, starting transfers between devices, local(): lax.all_to_all(neck_tile, 'gx', split_axis=2, concat_axis=1, tiled=True)  8.8 us
    dot_general x18, matrix products, weight_terms(): lax.dot_general(window, flat_grads, (((0,), (0,)), ((), ())), preferred_e...  6.68 us
  transfers between devices with their start and end apart: 18, of which 5 were waited for; matrix products, arithmetic and copies ran while one was open for 11% of the time, Pallas kernels for 38%

profile of v1, /device:TPU:1, one launch (start us, length us, event | category | flops | bytes accessed | tf_op | source)
XLA Modules:
  0.0 182.4 jit_solution(13566726515808880430)
XLA Ops:
  0.7 0.8 fusion.67
  1.5 4.9 %collective-permute-start = (bf16[1,64,128]{2,1,0:T(8,128)(2,1)S(1)}, bf16[1,64,128]{2,1,0:T(8,128)(2,1)S(1)}, u32[]{:S(2)}, u32[]{:S(2)}) collective-permute-start(bf16[1,64,128]{2,1,0:T(8,128)(2,1)S(1)} %get-tuple-element.42), channel_id=1, source_target_pairs={{0,16},{16,32},{32,48},{48,64},{64,80},{80,96},{96,112},{112,128},... | collective-permute-start | bytes 49160 | tf_op jit(solution)/shard_map/ppermute | solution.py:22
  6.4 5.1 %collective-permute-start.1 = (bf16[1,64,128]{2,1,0:T(8,128)(2,1)S(1)}, bf16[1,64,128]{2,1,0:T(8,128)(2,1)S(1)}, u32[]{:S(2)}, u32[]{:S(2)}) collective-permute-start(bf16[1,64,128]{2,1,0:T(8,128)(2,1)S(1)} %get-tuple-element.41), channel_id=1, source_target_pairs={{16,0},{32,16},{48,32},{64,48},{80,64},{96,80},{112,96},{128,112},... | collective-permute-start | bytes 49160 | tf_op jit(solution)/shard_map/ppermute | solution.py:24
  11.6 1.2 copy.34
  12.7 1.2 reshape.235
  13.9 4.2 %all-to-all-start.1 = ((bf16[16,2,1024]{2,1,0:T(2,128)(2,1)}), bf16[16,2,1024]{2,1,0:T(2,128)(2,1)}, u32[]{:S(2)}, u32[]{:S(2)}) async-start(bf16[16,2,1024]{2,1,0:T(2,128)(2,1)} %reshape.235), calls=%async_computation.1 | async-start | bytes 131072 | tf_op jit(solution)/shard_map/all_to_all | solution.py:316
  18.3 0.8 copy-done.2
  19.2 3.1 %collective-permute-start.2 = (bf16[10,1,128]{2,1,0:T(2,128)(2,1)S(1)}, bf16[10,1,128]{2,1,0:T(2,128)(2,1)S(1)}, u32[]{:S(2)}, u32[]{:S(2)}) collective-permute-start(bf16[10,1,128]{2,1,0:T(2,128)(2,1)S(1)} %get-tuple-element.30), channel_id=1, source_target_pairs={{0,1},{1,2},{2,3},{3,4},{4,5},{5,6},{6,7},{7,8},{8,9},{9,10},{10,1... | collective-permute-start | bytes 7688 | tf_op jit(solution)/shard_map/ppermute | solution.py:22
  22.3 1.3 collective-permute-start.3
  23.9 2.7 %collective-permute-done.3 = bf16[10,1,128]{2,1,0:T(2,128)(2,1)S(1)} collective-permute-done((bf16[10,1,128]{2,1,0:T(2,128)(2,1)S(1)}, bf16[10,1,128]{2,1,0:T(2,128)(2,1)S(1)}, u32[]{:S(2)}, u32[]{:S(2)}) %collective-permute-start.3) | collective-permute-done | bytes 2592 | tf_op jit(solution)/shard_map/ppermute | solution.py:24
  28.0 0.9 add_convert_fusion
  29.2 5.2 %collective-permute-start.4 = (bf16[1,32,256]{2,1,0:T(8,128)(2,1)S(1)}, bf16[1,32,256]{2,1,0:T(8,128)(2,1)S(1)}, u32[]{:S(2)}, u32[]{:S(2)}) collective-permute-start(bf16[1,32,256]{2,1,0:T(8,128)(2,1)S(1)} %get-tuple-element.69), channel_id=1, source_target_pairs={{0,16},{16,32},{32,48},{48,64},{64,80},{80,96},{96,112},{112,128},... | collective-permute-start | bytes 49160 | tf_op jit(solution)/shard_map/ppermute | solution.py:22
  34.4 1.9 %collective-permute-start.5 = (bf16[1,32,256]{2,1,0:T(8,128)(2,1)S(1)}, bf16[1,32,256]{2,1,0:T(8,128)(2,1)S(1)}, u32[]{:S(2)}, u32[]{:S(2)}) collective-permute-start(bf16[1,32,256]{2,1,0:T(8,128)(2,1)S(1)} %get-tuple-element.70), channel_id=1, source_target_pairs={{16,0},{32,16},{48,32},{64,48},{80,64},{96,80},{112,96},{128,112},... | collective-permute-start | bytes 49160 | tf_op jit(solution)/shard_map/ppermute | solution.py:24
  36.3 0.7 reverse_bitcast_fusion.1
  37.8 1.6 collective-permute-done.5
  39.5 3.1 %collective-permute-start.6 = (bf16[6,1,256]{2,1,0:T(2,128)(2,1)S(1)}, bf16[6,1,256]{2,1,0:T(2,128)(2,1)S(1)}, u32[]{:S(2)}, u32[]{:S(2)}) collective-permute-start(bf16[6,1,256]{2,1,0:T(2,128)(2,1)S(1)} %get-tuple-element.61), channel_id=1, source_target_pairs={{0,1},{1,2},{2,3},{3,4},{4,5},{5,6},{6,7},{7,8},{8,9},{9,10},{10,1... | collective-permute-start | bytes 9224 | tf_op jit(solution)/shard_map/ppermute | solution.py:22
  42.6 1.3 collective-permute-start.7
  44.7 2.3 %collective-permute-done.7 = bf16[6,1,256]{2,1,0:T(2,128)(2,1)S(1)} collective-permute-done((bf16[6,1,256]{2,1,0:T(2,128)(2,1)S(1)}, bf16[6,1,256]{2,1,0:T(2,128)(2,1)S(1)}, u32[]{:S(2)}, u32[]{:S(2)}) %collective-permute-start.7) | collective-permute-done | bytes 3104 | tf_op jit(solution)/shard_map/ppermute | solution.py:24
  47.9 0.8 convolution_add_fusion.21
  48.8 0.8 fusion.19
  49.6 2.0 %reshape.236 = bf16[512,4,16]{2,1,0:T(4,128)(2,1)} reshape(bf16[16,2,1024]{2,1,0:T(2,128)(2,1)} %all-to-all-done.1) | data formatting | bytes 131072
  51.6 1.4 copy.35
  53.0 0.9 reshape.227
  53.9 1.0 copy.37
  55.0 1.9 %multiply_convert_fusion.1 = (bf16[128,256]{1,0:T(8,128)(2,1)S(1)}, bf16[128,256]{1,0:T(8,128)(2,1)}) fusion(f32[128,256]{1,0:T(8,128)S(1)} %copy.37, bf16[4,32,256]{2,1,0:T(8,128)(2,1)S(1)} %fusion.9, f32[128,256]{1,0:T(8,128)} %fusion.19, f32[128,256]{1,0:T(8,128)} %convolution_add_fusion.21, bf16[128,256]{1,0:T(8,128)(2,1)} %bitcast.403, ...), kind=kOutput, calls=%fused_computation.117 | convolution fusion | flops 17235968 | bytes 786432 | tf_op jit(solution)/shard_map/dot_general | solution.py:48
  58.7 0.9 convolution_bitcast_fusion.5
  59.6 0.9 convolution_bitcast_fusion.2
  60.5 0.9 convolution_bitcast_fusion.1
  61.4 0.9 convolution_bitcast_fusion.3
  62.3 3.5 %collective-permute-start.8 = (bf16[1,32,256]{2,1,0:T(8,128)(2,1)}, bf16[1,32,256]{2,1,0:T(8,128)(2,1)S(1)}, u32[]{:S(2)}, u32[]{:S(2)}) collective-permute-start(bf16[1,32,256]{2,1,0:T(8,128)(2,1)} %get-tuple-element.65), channel_id=1, source_target_pairs={{0,16},{16,32},{32,48},{48,64},{64,80},{80,96},{96,112},{112,128},... | collective-permute-start | bytes 49160 | tf_op jit(solution)/shard_map/ppermute | solution.py:22
  65.8 1.9 %collective-permute-start.9 = (bf16[1,32,256]{2,1,0:T(8,128)(2,1)S(1)}, bf16[1,32,256]{2,1,0:T(8,128)(2,1)S(1)}, u32[]{:S(2)}, u32[]{:S(2)}) collective-permute-start(bf16[1,32,256]{2,1,0:T(8,128)(2,1)S(1)} %get-tuple-element.66), channel_id=1, source_target_pairs={{16,0},{32,16},{48,32},{64,48},{80,64},{96,80},{112,96},{128,112},... | collective-permute-start | bytes 49160 | tf_op jit(solution)/shard_map/ppermute | solution.py:24
  67.7 1.0 copy.31
  68.8 0.9 reshape.233
  69.7 8.8 %all-to-all-start = ((bf16[16,2,1024]{2,1,0:T(2,128)(2,1)}), bf16[16,2,1024]{2,1,0:T(2,128)(2,1)S(1)}, u32[]{:S(2)}, u32[]{:S(2)}) async-start(bf16[16,2,1024]{2,1,0:T(2,128)(2,1)} %reshape.233), calls=%async_computation | async-start | bytes 131072 | tf_op jit(solution)/shard_map/all_to_all | solution.py:315
  78.7 0.8 copy-done.18
  79.9 3.3 %collective-permute-start.10 = (bf16[6,1,256]{2,1,0:T(2,128)(2,1)S(1)}, bf16[6,1,256]{2,1,0:T(2,128)(2,1)S(1)}, u32[]{:S(2)}, u32[]{:S(2)}) collective-permute-start(bf16[6,1,256]{2,1,0:T(2,128)(2,1)S(1)} %get-tuple-element.57), channel_id=1, source_target_pairs={{0,1},{1,2},{2,3},{3,4},{4,5},{5,6},{6,7},{7,8},{8,9},{9,10},{10,1... | collective-permute-start | bytes 9224 | tf_op jit(solution)/shard_map/ppermute | solution.py:22
  83.1 1.3 collective-permute-start.11
  84.7 3.0 %collective-permute-done.11 = bf16[6,1,256]{2,1,0:T(2,128)(2,1)S(1)} collective-permute-done((bf16[6,1,256]{2,1,0:T(2,128)(2,1)S(1)}, bf16[6,1,256]{2,1,0:T(2,128)(2,1)S(1)}, u32[]{:S(2)}, u32[]{:S(2)}) %collective-permute-start.11) | collective-permute-done | bytes 3104 | tf_op jit(solution)/shard_map/ppermute | solution.py:24
  92.3 5.4 %collective-permute-start.12 = (bf16[1,64,128]{2,1,0:T(8,128)(2,1)S(1)}, bf16[1,64,128]{2,1,0:T(8,128)(2,1)S(1)}, u32[]{:S(2)}, u32[]{:S(2)}) collective-permute-start(bf16[1,64,128]{2,1,0:T(8,128)(2,1)S(1)} %get-tuple-element.34), channel_id=1, source_target_pairs={{0,16},{16,32},{32,48},{48,64},{64,80},{80,96},{96,112},{112,128},... | collective-permute-start | bytes 49160 | tf_op jit(solution)/shard_map/ppermute | solution.py:22
  97.8 1.9 %collective-permute-start.13 = (bf16[1,64,128]{2,1,0:T(8,128)(2,1)S(1)}, bf16[1,64,128]{2,1,0:T(8,128)(2,1)S(1)}, u32[]{:S(2)}, u32[]{:S(2)}) collective-permute-start(bf16[1,64,128]{2,1,0:T(8,128)(2,1)S(1)} %get-tuple-element.35), channel_id=1, source_target_pairs={{16,0},{32,16},{48,32},{64,48},{80,64},{96,80},{112,96},{128,112},... | collective-permute-start | bytes 49160 | tf_op jit(solution)/shard_map/ppermute | solution.py:24
  100.1 69.8 %shard_map.92 = (bf16[2304,256]{1,0:T(8,128)(2,1)S(1)}, bf16[512,256]{1,0:T(8,128)(2,1)S(1)}, bf16[1152,128]{1,0:T(8,128)(2,1)S(1)}) custom-call(f32[2304,256]{1,0:T(8,128)S(1)} %bitcast.336, f32[512,256]{1,0:T(8,128)S(1)} %convolution_bitcast_fusion.down_ref, f32[1152,128]{1,0:T(8,128)S(1)} %bitcast.337), custom_call_target="tpu_custom_call" | custom-call | tf_op jit(solution)/shard_map/pallas_call | solution.py:267
  169.9 2.1 %collective-permute-start.14 = (bf16[10,1,128]{2,1,0:T(2,128)(2,1)S(1)}, bf16[10,1,128]{2,1,0:T(2,128)(2,1)S(1)}, u32[]{:S(2)}, u32[]{:S(2)}) collective-permute-start(bf16[10,1,128]{2,1,0:T(2,128)(2,1)S(1)} %get-tuple-element.25), channel_id=1, source_target_pairs={{0,1},{1,2},{2,3},{3,4},{4,5},{5,6},{6,7},{7,8},{8,9},{9,10},{10,1... | collective-permute-start | bytes 7688 | tf_op jit(solution)/shard_map/ppermute | solution.py:22
  172.0 1.3 collective-permute-start.15
  173.6 2.8 %collective-permute-done.15 = bf16[10,1,128]{2,1,0:T(2,128)(2,1)S(1)} collective-permute-done((bf16[10,1,128]{2,1,0:T(2,128)(2,1)S(1)}, bf16[10,1,128]{2,1,0:T(2,128)(2,1)S(1)}, u32[]{:S(2)}, u32[]{:S(2)}) %collective-permute-start.15) | collective-permute-done | bytes 2592 | tf_op jit(solution)/shard_map/ppermute | solution.py:24
  178.0 0.9 fusion.4
  179.1 0.9 all_to_all.23
  180.0 0.7 copy.49
  181.4 1.0 copy.51
  (178 shorter events, 14.3 us)
Async XLA Ops:
  0.6 28.3 %copy-start = (bf16[2,2,128,256]{3,2,1,0:T(8,128)(2,1)S(1)}, bf16[2,2,128,256]{3,2,1,0:T(8,128)(2,1)}, u32[]{:S(2)}) copy-start(bf16[2,2,128,256]{3,2,1,0:T(8,128)(2,1)} %param.7) | copy-start | bytes 786436
  0.6 17.5 %copy-start.1 = (bf16[3,3,256,256]{3,2,1,0:T(8,128)(2,1)S(1)}, bf16[3,3,256,256]{3,2,1,0:T(8,128)(2,1)}, u32[]{:S(2)}) copy-start(bf16[3,3,256,256]{3,2,1,0:T(8,128)(2,1)} %param.8) | copy-start | bytes 3538948
  1.5 16.7 %collective-permute-start = (bf16[1,64,128]{2,1,0:T(8,128)(2,1)S(1)}, bf16[1,64,128]{2,1,0:T(8,128)(2,1)S(1)}, u32[]{:S(2)}, u32[]{:S(2)}) collective-permute-start(bf16[1,64,128]{2,1,0:T(8,128)(2,1)S(1)} %get-tuple-element.42), channel_id=1, source_target_pairs={{0,16},{16,32},{32,48},{48,64},{64,80},{80,96},{96,112},{112,128},... | collective-permute-start | bytes 49160 | tf_op jit(solution)/shard_map/ppermute | solution.py:22
  6.4 11.8 %collective-permute-start.1 = (bf16[1,64,128]{2,1,0:T(8,128)(2,1)S(1)}, bf16[1,64,128]{2,1,0:T(8,128)(2,1)S(1)}, u32[]{:S(2)}, u32[]{:S(2)}) collective-permute-start(bf16[1,64,128]{2,1,0:T(8,128)(2,1)S(1)} %get-tuple-element.41), channel_id=1, source_target_pairs={{16,0},{32,16},{48,32},{64,48},{80,64},{96,80},{112,96},{128,112},... | collective-permute-start | bytes 49160 | tf_op jit(solution)/shard_map/ppermute | solution.py:24
  13.9 35.6 %all-to-all-start.1 = ((bf16[16,2,1024]{2,1,0:T(2,128)(2,1)}), bf16[16,2,1024]{2,1,0:T(2,128)(2,1)}, u32[]{:S(2)}, u32[]{:S(2)}) async-start(bf16[16,2,1024]{2,1,0:T(2,128)(2,1)} %reshape.235), calls=%async_computation.1 | async-start | bytes 131072 | tf_op jit(solution)/shard_map/all_to_all | solution.py:316
  18.1 5.4 %copy-start.16 = (bf16[3,3,128,128]{3,2,1,0:T(8,128)(2,1)S(1)}, bf16[3,3,128,128]{3,2,1,0:T(8,128)(2,1)}, u32[]{:S(2)}) copy-start(bf16[3,3,128,128]{3,2,1,0:T(8,128)(2,1)} %param.6) | copy-start | bytes 884740
  19.1 8.1 %copy-start.3 = (bf16[8,64,128]{2,1,0:T(8,128)(2,1)}, bf16[8,64,128]{2,1,0:T(8,128)(2,1)S(1)}, u32[]{:S(2)}) copy-start(bf16[8,64,128]{2,1,0:T(8,128)(2,1)S(1)} %get-tuple-element.38) | copy-start | bytes 393220
  19.2 4.8 %collective-permute-start.2 = (bf16[10,1,128]{2,1,0:T(2,128)(2,1)S(1)}, bf16[10,1,128]{2,1,0:T(2,128)(2,1)S(1)}, u32[]{:S(2)}, u32[]{:S(2)}) collective-permute-start(bf16[10,1,128]{2,1,0:T(2,128)(2,1)S(1)} %get-tuple-element.30), channel_id=1, source_target_pairs={{0,1},{1,2},{2,3},{3,4},{4,5},{5,6},{6,7},{7,8},{8,9},{9,10},{10,1... | collective-permute-start | bytes 7688 | tf_op jit(solution)/shard_map/ppermute | solution.py:22
  22.3 4.4 %collective-permute-start.3 = (bf16[10,1,128]{2,1,0:T(2,128)(2,1)S(1)}, bf16[10,1,128]{2,1,0:T(2,128)(2,1)S(1)}, u32[]{:S(2)}, u32[]{:S(2)}) collective-permute-start(bf16[10,1,128]{2,1,0:T(2,128)(2,1)S(1)} %get-tuple-element.31), channel_id=1, source_target_pairs={{1,0},{2,1},{3,2},{4,3},{5,4},{6,5},{7,6},{8,7},{9,8},{10,9},{11,1... | collective-permute-start | bytes 7688 | tf_op jit(solution)/shard_map/ppermute | solution.py:24
  26.9 1.1 copy-start.35
  29.2 8.7 %collective-permute-start.4 = (bf16[1,32,256]{2,1,0:T(8,128)(2,1)S(1)}, bf16[1,32,256]{2,1,0:T(8,128)(2,1)S(1)}, u32[]{:S(2)}, u32[]{:S(2)}) collective-permute-start(bf16[1,32,256]{2,1,0:T(8,128)(2,1)S(1)} %get-tuple-element.69), channel_id=1, source_target_pairs={{0,16},{16,32},{32,48},{48,64},{64,80},{80,96},{96,112},{112,128},... | collective-permute-start | bytes 49160 | tf_op jit(solution)/shard_map/ppermute | solution.py:22
  34.4 5.1 %collective-permute-start.5 = (bf16[1,32,256]{2,1,0:T(8,128)(2,1)S(1)}, bf16[1,32,256]{2,1,0:T(8,128)(2,1)S(1)}, u32[]{:S(2)}, u32[]{:S(2)}) collective-permute-start(bf16[1,32,256]{2,1,0:T(8,128)(2,1)S(1)} %get-tuple-element.70), channel_id=1, source_target_pairs={{16,0},{32,16},{48,32},{64,48},{80,64},{96,80},{112,96},{128,112},... | collective-permute-start | bytes 49160 | tf_op jit(solution)/shard_map/ppermute | solution.py:24
  39.5 5.2 %collective-permute-start.6 = (bf16[6,1,256]{2,1,0:T(2,128)(2,1)S(1)}, bf16[6,1,256]{2,1,0:T(2,128)(2,1)S(1)}, u32[]{:S(2)}, u32[]{:S(2)}) collective-permute-start(bf16[6,1,256]{2,1,0:T(2,128)(2,1)S(1)} %get-tuple-element.61), channel_id=1, source_target_pairs={{0,1},{1,2},{2,3},{3,4},{4,5},{5,6},{6,7},{7,8},{8,9},{9,10},{10,1... | collective-permute-start | bytes 9224 | tf_op jit(solution)/shard_map/ppermute | solution.py:22
  42.6 4.4 %collective-permute-start.7 = (bf16[6,1,256]{2,1,0:T(2,128)(2,1)S(1)}, bf16[6,1,256]{2,1,0:T(2,128)(2,1)S(1)}, u32[]{:S(2)}, u32[]{:S(2)}) collective-permute-start(bf16[6,1,256]{2,1,0:T(2,128)(2,1)S(1)} %get-tuple-element.62), channel_id=1, source_target_pairs={{1,0},{2,1},{3,2},{4,3},{5,4},{6,5},{7,6},{8,7},{9,8},{10,9},{11,1... | collective-permute-start | bytes 9224 | tf_op jit(solution)/shard_map/ppermute | solution.py:24
  47.0 1.7 copy-start.21
  47.0 1.7 copy-start.25
  47.0 1.7 copy-start.27
  47.0 1.7 copy-start.29
  47.1 1.7 copy-start.31
  47.1 1.7 copy-start.23
  53.9 3.8 %copy-start.32 = (bf16[4,32,256]{2,1,0:T(8,128)(2,1)S(1)}, bf16[4,32,256]{2,1,0:T(8,128)(2,1)}, u32[]{:S(2)}) copy-start(bf16[4,32,256]{2,1,0:T(8,128)(2,1)} %copy-done.31) | copy-start | bytes 196612
  53.9 4.1 %copy-start.30 = (bf16[4,32,256]{2,1,0:T(8,128)(2,1)S(1)}, bf16[4,32,256]{2,1,0:T(8,128)(2,1)}, u32[]{:S(2)}) copy-start(bf16[4,32,256]{2,1,0:T(8,128)(2,1)} %copy-done.29) | copy-start | bytes 196612
  55.0 3.2 %copy-start.33 = (f32[128,256]{1,0:T(8,128)}, f32[128,256]{1,0:T(8,128)S(1)}, u32[]{:S(2)}) copy-start(f32[128,256]{1,0:T(8,128)S(1)} %copy.37) | copy-start | bytes 393220
  55.0 3.2 %copy-start.28 = (bf16[4,32,256]{2,1,0:T(8,128)(2,1)S(1)}, bf16[4,32,256]{2,1,0:T(8,128)(2,1)}, u32[]{:S(2)}) copy-start(bf16[4,32,256]{2,1,0:T(8,128)(2,1)} %copy-done.27) | copy-start | bytes 196612
  55.0 3.4 %copy-start.26 = (bf16[4,32,256]{2,1,0:T(8,128)(2,1)S(1)}, bf16[4,32,256]{2,1,0:T(8,128)(2,1)}, u32[]{:S(2)}) copy-start(bf16[4,32,256]{2,1,0:T(8,128)(2,1)} %copy-done.25) | copy-start | bytes 196612
  57.5 2.0 %copy-start.38 = (bf16[4,32,256]{2,1,0:T(8,128)(2,1)S(1)}, bf16[4,32,256]{2,1,0:T(8,128)(2,1)}, u32[]{:S(2)}) copy-start(bf16[4,32,256]{2,1,0:T(8,128)(2,1)} %get-tuple-element.67) | copy-start | bytes 196612
  57.8 2.7 %copy-start.24 = (bf16[4,32,256]{2,1,0:T(8,128)(2,1)S(1)}, bf16[4,32,256]{2,1,0:T(8,128)(2,1)}, u32[]{:S(2)}) copy-start(bf16[4,32,256]{2,1,0:T(8,128)(2,1)} %copy-done.23) | copy-start | bytes 196612
  58.0 3.4 %copy-start.22 = (bf16[4,32,256]{2,1,0:T(8,128)(2,1)S(1)}, bf16[4,32,256]{2,1,0:T(8,128)(2,1)}, u32[]{:S(2)}) copy-start(bf16[4,32,256]{2,1,0:T(8,128)(2,1)} %copy-done.21) | copy-start | bytes 196612
  62.3 17.5 %collective-permute-start.8 = (bf16[1,32,256]{2,1,0:T(8,128)(2,1)}, bf16[1,32,256]{2,1,0:T(8,128)(2,1)S(1)}, u32[]{:S(2)}, u32[]{:S(2)}) collective-permute-start(bf16[1,32,256]{2,1,0:T(8,128)(2,1)} %get-tuple-element.65), channel_id=1, source_target_pairs={{0,16},{16,32},{32,48},{48,64},{64,80},{80,96},{96,112},{112,128},... | collective-permute-start | bytes 49160 | tf_op jit(solution)/shard_map/ppermute | solution.py:22
  65.8 14.0 %collective-permute-start.9 = (bf16[1,32,256]{2,1,0:T(8,128)(2,1)S(1)}, bf16[1,32,256]{2,1,0:T(8,128)(2,1)S(1)}, u32[]{:S(2)}, u32[]{:S(2)}) collective-permute-start(bf16[1,32,256]{2,1,0:T(8,128)(2,1)S(1)} %get-tuple-element.66), channel_id=1, source_target_pairs={{16,0},{32,16},{48,32},{64,48},{80,64},{96,80},{112,96},{128,112},... | collective-permute-start | bytes 49160 | tf_op jit(solution)/shard_map/ppermute | solution.py:24
  69.7 8.9 %copy-start.17 = (f32[1,256,256]{2,1,0:T(8,128)S(1)}, f32[1,256,256]{2,1,0:T(8,128)}, u32[]{:S(2)}) copy-start(f32[1,256,256]{2,1,0:T(8,128)} %convolution_bitcast_fusion.5) | copy-start | bytes 786436
  69.7 109.2 %all-to-all-start = ((bf16[16,2,1024]{2,1,0:T(2,128)(2,1)}), bf16[16,2,1024]{2,1,0:T(2,128)(2,1)S(1)}, u32[]{:S(2)}, u32[]{:S(2)}) async-start(bf16[16,2,1024]{2,1,0:T(2,128)(2,1)} %reshape.233), calls=%async_computation | async-start | bytes 131072 | tf_op jit(solution)/shard_map/all_to_all | solution.py:315
  78.5 1.0 copy-start.19
  78.5 1.1 copy-start.20
  79.9 4.8 %collective-permute-start.10 = (bf16[6,1,256]{2,1,0:T(2,128)(2,1)S(1)}, bf16[6,1,256]{2,1,0:T(2,128)(2,1)S(1)}, u32[]{:S(2)}, u32[]{:S(2)}) collective-permute-start(bf16[6,1,256]{2,1,0:T(2,128)(2,1)S(1)} %get-tuple-element.57), channel_id=1, source_target_pairs={{0,1},{1,2},{2,3},{3,4},{4,5},{5,6},{6,7},{7,8},{8,9},{9,10},{10,1... | collective-permute-start | bytes 9224 | tf_op jit(solution)/shard_map/ppermute | solution.py:22
  83.1 4.6 %collective-permute-start.11 = (bf16[6,1,256]{2,1,0:T(2,128)(2,1)S(1)}, bf16[6,1,256]{2,1,0:T(2,128)(2,1)S(1)}, u32[]{:S(2)}, u32[]{:S(2)}) collective-permute-start(bf16[6,1,256]{2,1,0:T(2,128)(2,1)S(1)} %get-tuple-element.58), channel_id=1, source_target_pairs={{1,0},{2,1},{3,2},{4,3},{5,4},{6,5},{7,6},{8,7},{9,8},{10,9},{11,1... | collective-permute-start | bytes 9224 | tf_op jit(solution)/shard_map/ppermute | solution.py:24
  88.2 1.0 copy-start.34
  89.5 1.2 copy-start.4
  89.7 1.2 copy-start.10
  89.7 1.4 copy-start.8
  90.0 1.6 copy-start.6
  90.2 1.7 copy-start.36
  90.7 9.1 %copy-start.39 = (bf16[512,4,32]{0,2,1:T(8,128)(2,1)S(1)}, bf16[512,4,32]{0,2,1:T(8,128)(2,1)}, u32[]{:S(2)}) copy-start(bf16[512,4,32]{0,2,1:T(8,128)(2,1)} %dot_general.225) | copy-start | bytes 393220
  92.3 77.5 %collective-permute-start.12 = (bf16[1,64,128]{2,1,0:T(8,128)(2,1)S(1)}, bf16[1,64,128]{2,1,0:T(8,128)(2,1)S(1)}, u32[]{:S(2)}, u32[]{:S(2)}) collective-permute-start(bf16[1,64,128]{2,1,0:T(8,128)(2,1)S(1)} %get-tuple-element.34), channel_id=1, source_target_pairs={{0,16},{16,32},{32,48},{48,64},{64,80},{80,96},{96,112},{112,128},... | collective-permute-start | bytes 49160 | tf_op jit(solution)/shard_map/ppermute | solution.py:22
  97.8 72.1 %collective-permute-start.13 = (bf16[1,64,128]{2,1,0:T(8,128)(2,1)S(1)}, bf16[1,64,128]{2,1,0:T(8,128)(2,1)S(1)}, u32[]{:S(2)}, u32[]{:S(2)}) collective-permute-start(bf16[1,64,128]{2,1,0:T(8,128)(2,1)S(1)} %get-tuple-element.35), channel_id=1, source_target_pairs={{16,0},{32,16},{48,32},{64,48},{80,64},{96,80},{112,96},{128,112},... | collective-permute-start | bytes 49160 | tf_op jit(solution)/shard_map/ppermute | solution.py:24
  100.1 73.3 %copy-start.15 = (bf16[3,3,128,128]{2,3,1,0:T(8,128)(2,1)S(1)}, bf16[3,3,128,128]{2,3,1,0:T(8,128)(2,1)}, u32[]{:S(2)}) copy-start(bf16[3,3,128,128]{2,3,1,0:T(8,128)(2,1)} %reverse_bitcast_fusion.1) | copy-start | bytes 884740
  169.9 3.6 %collective-permute-start.14 = (bf16[10,1,128]{2,1,0:T(2,128)(2,1)S(1)}, bf16[10,1,128]{2,1,0:T(2,128)(2,1)S(1)}, u32[]{:S(2)}, u32[]{:S(2)}) collective-permute-start(bf16[10,1,128]{2,1,0:T(2,128)(2,1)S(1)} %get-tuple-element.25), channel_id=1, source_target_pairs={{0,1},{1,2},{2,3},{3,4},{4,5},{5,6},{6,7},{7,8},{8,9},{9,10},{10,1... | collective-permute-start | bytes 7688 | tf_op jit(solution)/shard_map/ppermute | solution.py:22
  172.0 4.4 %collective-permute-start.15 = (bf16[10,1,128]{2,1,0:T(2,128)(2,1)S(1)}, bf16[10,1,128]{2,1,0:T(2,128)(2,1)S(1)}, u32[]{:S(2)}, u32[]{:S(2)}) collective-permute-start(bf16[10,1,128]{2,1,0:T(2,128)(2,1)S(1)} %get-tuple-element.26), channel_id=1, source_target_pairs={{1,0},{2,1},{3,2},{4,3},{5,4},{6,5},{7,6},{8,7},{9,8},{10,9},{11,1... | collective-permute-start | bytes 7688 | tf_op jit(solution)/shard_map/ppermute | solution.py:24
  (10 other events, 8.8 us)

commit v2 on v0

v2 whole, which is shorter than its diff:
```python
import functools
import math

import jax
import jax.numpy as jnp
from jax import lax
from jax.experimental import pallas as pl
from jax.experimental.pallas import tpu as pltpu
from jax.sharding import PartitionSpec as P

MESH = pl.DeviceIdType.MESH
BF16, F32 = jnp.bfloat16, jnp.float32

RIM = 5
WIDE = 96
NARROW = 48
SIDES = [(dy, dx) for dy in (-1, 0, 1) for dx in (-1, 0, 1) if (dy, dx) != (0, 0)]
NECK_TILES = 9
REST_TILES = 5
LEVEL_OWNERS = 12


def sigmoid(v):
    return 1.0 / (1.0 + jnp.exp(-v))


def slope_of(v):
    s = jax.nn.sigmoid(v)
    return s + v * s * (1.0 - s)


def dot(a, b):
    return jnp.dot(a, b, preferred_element_type=F32)


def dot_nt(a, b):
    return lax.dot_general(a, b, (((1,), (1,)), ((), ())), preferred_element_type=F32)


def dot_tn(a, b):
    return lax.dot_general(a, b, (((0,), (0,)), ((), ())), preferred_element_type=F32)


def kernel(
    scales,
    level_in, wl_hbm, wd_hbm, wn_hbm, cot_in,
    neck_out, grad_input, grad_level, grad_down, grad_neck,
    wl, wd, wn, wlt,
    lp, lf, im_l, pre_l, act, dn, nf, im_n, cf, gf, im_g, gate_own, ng, lbf, gp, g2f, im_b,
    cot_send, cot_recv, ct, hr, hc, hx, no_send, no_recv,
    neck_own, level_acc, down_acc,
    a_pair_s, a_pair_r, a_work, a_xy, a_piece, a_z, a_fin, a_all,
    b_pair_s, b_pair_r, b_work, b_xy, b_piece, b_z, b_fin, b_all,
    w_sem, e1_sem, cot_sem, ch_sem, no_sem, e4_sem,
    pair_sem, xy_sem, z_sem, zb_sem, xyb_sem,
):
    gy, gx = lax.axis_index("gy"), lax.axis_index("gx")
    z, core = gy // 2, gy % 2
    other = 1 - core

    def side(dy, dx):
        return ((gy + dy + 32) % 32, (gx + dx + 16) % 16)

    pair_dev = (z * 2 + other, gx)
    plane = [None] + [(gy, (gx + k) % 16) for k in range(1, 16)]

    def column(zz):
        return (zz * 2 + core, gx)

    barrier = pltpu.get_barrier_semaphore()
    peers = plane[1:] + [column((z + k) % 16) for k in range(1, 16)] + [side(dy, dx) for dy, dx in SIDES if dy != 0]
    for peer in peers:
        pl.semaphore_signal(barrier, inc=1, device_id=peer, device_id_type=MESH)

    loads = [
        pltpu.make_async_copy(wl_hbm, wl, w_sem.at[0]),
        pltpu.make_async_copy(wd_hbm, wd, w_sem.at[1]),
        pltpu.make_async_copy(wn_hbm, wn, w_sem.at[2]),
    ]
    for load in loads:
        load.start()

    def copy(src, dst, sems, k, dev):
        return pltpu.make_async_remote_copy(
            src_ref=src, dst_ref=dst, send_sem=sems.at[0, k], recv_sem=sems.at[1, k],
            device_id=dev, device_id_type=MESH,
        )

    sent = []

    def go(copies):
        for c in copies:
            c.start()
        sent.extend(copies)
        return copies

    lane = lax.broadcasted_iota(jnp.int32, (16, 128), 1)
    for q in range(4):
        rows = [cot_in[r, :, 128 * q:128 * q + 128].astype(F32) for r in range(4)]
        for j in range(4):
            out = pltpu.roll(rows[3], (32 * (3 - j)) % 128, 1) if j != 3 else rows[3]
            for r in (2, 1, 0):
                part = pltpu.roll(rows[r], (32 * (r - j)) % 128, 1) if r != j else rows[r]
                out = jnp.where(lane < 32 * (r + 1), part, out)
            cot_send[4 * q + j] = out.astype(BF16)
    cot_recv[gx] = cot_send[gx]

    top_ok = jnp.where(gy > 0, 1.0, 0.0).astype(F32)
    bottom_ok = jnp.where(gy < 31, 1.0, 0.0).astype(F32)
    left_ok = jnp.where(gx > 0, 1.0, 0.0).astype(F32)
    right_ok = jnp.where(gx < 15, 1.0, 0.0).astype(F32)

    lf[0:8] = jnp.zeros((8, 128), F32)
    lf[8 + 18 * WIDE:] = jnp.zeros((8, 128), F32)
    for r in range(8):
        start = 8 + (r + RIM) * WIDE + 16
        lf[start:start + 64] = level_in[r].astype(F32)

    pl.semaphore_wait(barrier, len(peers))

    cot_copies = go([
        copy(cot_send.at[(gx + k) % 16], cot_recv.at[gx], cot_sem, k, plane[k]) for k in range(1, 16)
    ])
    src_rows = {-1: slice(0, RIM), 0: slice(0, 8), 1: slice(8 - RIM, 8)}
    src_cols = {-1: slice(0, 16), 0: slice(0, 64), 1: slice(48, 64)}
    dst_rows = {-1: slice(RIM + 8, RIM + 8 + RIM), 0: slice(RIM, RIM + 8), 1: slice(0, RIM)}
    dst_cols = {-1: slice(80, 96), 0: slice(16, 80), 1: slice(0, 16)}
    e1 = go([
        copy(level_in.at[src_rows[dy], src_cols[dx]], lp.at[dst_rows[dy], dst_cols[dx]], e1_sem, n, side(dy, dx))
        for n, (dy, dx) in enumerate(SIDES)
    ])

    loads[0].wait()
    for ky in range(3):
        for kx in range(3):
            w = wl[2 - ky, (2 - kx) * 128:(3 - kx) * 128, :].astype(F32)
            wlt[ky, kx * 128:(kx + 1) * 128, :] = w.T.astype(BF16)

    for c in cot_copies:
        c.wait_recv()
    ct[...] = cot_recv[...].reshape(256, 128).astype(F32).T.astype(BF16).reshape(4, 32, 256)
    one_row = {-1: slice(0, 1), 0: slice(0, 4), 1: slice(3, 4)}
    half_cols = {-1: slice(0, 16), 0: slice(0, 32), 1: slice(16, 32)}

    def rim_buffer(dy, dx):
        if dx == 0:
            return hr.at[(dy + 1) // 2]
        if dy == 0:
            return hc.at[(dx + 1) // 2]
        return hx.at[(dy + 1) // 2, (dx + 1) // 2]

    ch = go([
        copy(ct.at[one_row[dy], half_cols[dx]], rim_buffer(dy, dx), ch_sem, n, side(dy, dx))
        for n, (dy, dx) in enumerate(SIDES)
    ])

    for c in e1:
        c.wait_recv()
    for r in range(18):
        row_ok = top_ok if r < RIM else bottom_ok if r >= RIM + 8 else None
        base = 8 + r * WIDE
        left = lp[r, 0:16].astype(F32) * left_ok
        right = lp[r, 80:96].astype(F32) * right_ok
        if row_ok is not None:
            left, right = left * row_ok, right * row_ok
            lf[base + 16:base + 80] = lp[r, 16:80].astype(F32) * row_ok
        lf[base:base + 16] = left
        lf[base + 80:base + 96] = right
    for r in range(18):
        for kx in range(3):
            start = 7 + kx + r * WIDE
            im_l[r * WIDE:(r + 1) * WIDE, kx * 128:(kx + 1) * 128] = lf[start:start + WIDE].astype(BF16)

    for q in range(4):
        pre = dot(im_l[4 * q * WIDE:(4 * q + 4) * WIDE], wl[0])
        for ky in (1, 2):
            pre = pre + dot(im_l[(4 * q + ky) * WIDE:(4 * q + ky + 4) * WIDE], wl[ky])
        own = lf[8 + (4 * q + 1) * WIDE:8 + (4 * q + 5) * WIDE]
        act[4 * q * WIDE:(4 * q + 4) * WIDE] = own + pre * jax.nn.sigmoid(pre)
        if q in (1, 2):
            pre_l[(q - 1) * 4 * WIDE:q * 4 * WIDE] = pre

    for rr in range(16):
        for q in range(2):
            lanes = slice(128 * (2 * (rr % 2) + q), 128 * (2 * (rr % 2) + q) + 128)
            dn[(rr // 2) * NARROW:(rr // 2 + 1) * NARROW, lanes] = act[pl.ds(rr * WIDE + q, NARROW, stride=2), :].astype(BF16)
    loads[1].wait()
    col = lax.broadcasted_iota(jnp.int32, (NARROW, 256), 0)
    col_ok = jnp.where(col < 8, left_ok, jnp.where(col >= 40, right_ok, 1.0))
    col_own = jnp.where((col >= 8) & (col < 40), 1.0, 0.0)
    nf[0:8] = jnp.zeros((8, 256), F32)
    nf[8 + 8 * NARROW:] = jnp.zeros((8, 256), F32)
    neck_in = dot(dn[...], wd[...]).astype(BF16).astype(F32)
    for r in range(8):
        row = neck_in[r * NARROW:(r + 1) * NARROW] * col_ok
        if r < 2:
            row = row * top_ok
        if r >= 6:
            row = row * bottom_ok
        nf[8 + r * NARROW:8 + (r + 1) * NARROW] = row
    for kx in range(3):
        im_n[:, kx * 256:(kx + 1) * 256] = nf[7 + kx:7 + kx + 8 * NARROW].astype(BF16)
    loads[2].wait()
    neck_pre = dot(im_n[0:6 * NARROW], wn[0])
    for ky in (1, 2):
        neck_pre = neck_pre + dot(im_n[ky * NARROW:(ky + 6) * NARROW], wn[ky])

    for c in ch:
        c.wait_recv()
    for r in range(6):
        if 1 <= r <= 4:
            mid = ct[r - 1].astype(F32)
            left = hc[1, r - 1, 8:16].astype(F32) * left_ok
            right = hc[0, r - 1, 0:8].astype(F32) * right_ok
        else:
            n, ok = (1, top_ok) if r == 0 else (0, bottom_ok)
            mid = hr[n, 0].astype(F32) * ok
            left = hx[n, 1, 0, 8:16].astype(F32) * (left_ok * ok)
            right = hx[n, 0, 0, 0:8].astype(F32) * (right_ok * ok)
        base = r * NARROW
        cf[base:base + 8] = left
        cf[base + 8:base + 40] = mid
        cf[base + 40:base + 48] = right

    gate = (cf[...] * slope_of(neck_pre)).astype(BF16).astype(F32)
    gf[0:8] = jnp.zeros((8, 256), F32)
    gf[8 + 6 * NARROW:] = jnp.zeros((8, 256), F32)
    gf[8:8 + 6 * NARROW] = gate
    for r in range(4):
        gate_own[r * NARROW:(r + 1) * NARROW] = (gate[(r + 1) * NARROW:(r + 2) * NARROW] * col_own).astype(BF16)

    def half_lanes(half):
        return pl.ds(pl.multiple_of(half * 128, 128), 128)

    theirs = gate_own[:, half_lanes(other)]
    for ky in range(3):
        part = dot_tn(im_n[(1 + ky) * NARROW:(5 + ky) * NARROW], theirs)
        a_pair_s[48 * ky:48 * ky + 48] = part.astype(BF16).reshape(48, 16, 128)
    a_pair = go([copy(a_pair_s, a_pair_r, pair_sem, 0, pair_dev)])
    mine = gate_own[:, half_lanes(core)]
    for ky in range(3):
        neck_own[48 * ky:48 * ky + 48] = dot_tn(im_n[(1 + ky) * NARROW:(5 + ky) * NARROW], mine).reshape(48, 16, 128)

    rows = []
    for r in range(4):
        v = neck_pre[(r + 1) * NARROW + 8:(r + 1) * NARROW + 40]
        rows.append(nf[8 + (r + 2) * NARROW + 8:8 + (r + 2) * NARROW + 40] + v * jax.nn.sigmoid(v))
    no_send[...] = jnp.concatenate(rows, axis=0).T.astype(BF16).reshape(16, 16, 128)
    no_recv[gx] = no_send[gx]
    no_copies = go([copy(no_send.at[(gx + k) % 16], no_recv.at[gx], no_sem, k, plane[k]) for k in range(1, 16)])

    for kx in range(3):
        im_g[:, kx * 256:(kx + 1) * 256] = gf[7 + kx:7 + kx + 6 * NARROW].astype(BF16)
    back = None
    for ky in range(3):
        for kx in range(3):
            term = dot_nt(
                im_g[ky * NARROW:(ky + 4) * NARROW, kx * 256:(kx + 1) * 256],
                wn[2 - ky, (2 - kx) * 256:(3 - kx) * 256, :],
            )
            back = term if back is None else back + term
    for r in range(4):
        v = cf[(r + 1) * NARROW:(r + 2) * NARROW] + back[r * NARROW:(r + 1) * NARROW]
        ng[r * NARROW:(r + 1) * NARROW] = (v * col_own).astype(BF16)
    spread = dot_nt(ng[...], wd[...])
    for r in range(4):
        for p in range(2):
            for q in range(2):
                lanes = slice(128 * (2 * p + q), 128 * (2 * p + q) + 128)
                lbf[pl.ds((2 * r + p) * WIDE + q, NARROW, stride=2), :] = spread[r * NARROW:(r + 1) * NARROW, lanes]
    for r in range(8):
        rows_r = slice(r * WIDE + 16, r * WIDE + 80)
        gp[r + 1, 16:80] = (lbf[rows_r] * slope_of(pre_l[rows_r])).astype(BF16)
    e4_src = {-1: slice(1, 2), 0: slice(1, 9), 1: slice(8, 9)}
    e4_dst = {-1: slice(9, 10), 0: slice(1, 9), 1: slice(0, 1)}
    e4_scol = {-1: slice(16, 32), 0: slice(16, 80), 1: slice(64, 80)}
    e4 = go([
        copy(gp.at[e4_src[dy], e4_scol[dx]], gp.at[e4_dst[dy], dst_cols[dx]], e4_sem, n, side(dy, dx))
        for n, (dy, dx) in enumerate(SIDES)
    ])

    own_gate = gp[1:9, 16:80].reshape(512, 128)
    for ky in range(3):
        window = jnp.concatenate(
            [im_l[(4 + ky + r) * WIDE + 16:(4 + ky + r) * WIDE + 80] for r in range(8)], axis=0
        )
        level_acc[ky * 384:(ky + 1) * 384] = dot_tn(window, own_gate)
    down_acc[...] = dot_tn(dn[2 * NARROW:6 * NARROW], ng[...])

    def rest_terms(half):
        down = down_acc[:, half_lanes(half)].reshape(16, 2, 16, 128)
        level = level_acc[pl.ds(pl.multiple_of(half * 576, 576), 576), :].reshape(LEVEL_OWNERS, 3, 16, 128)
        return down, level

    down, level = rest_terms(other)
    nothing = jnp.zeros((16 - LEVEL_OWNERS, 3, 16, 128), BF16)
    b_pair_s[:, 0:2] = down.astype(BF16)
    b_pair_s[0:LEVEL_OWNERS, 2:5] = level.astype(BF16)
    b_pair_s[LEVEL_OWNERS:, 2:5] = nothing
    b_pair = go([copy(b_pair_s, b_pair_r, pair_sem, 1, pair_dev)])

    def plane_stage(work, buf, sems, first):
        return go([copy(work(( gx + k) % 16), buf.at[k], sems, first + k, plane[k]) for k in range(1, 16)])

    def a_piece_of(o):
        return a_work.at[pl.ds(o * NECK_TILES, NECK_TILES)]

    def b_piece_of(o):
        return b_work.at[o]

    a_pair[0].wait_recv()
    for n in range(16):
        part = slice(n * NECK_TILES, (n + 1) * NECK_TILES)
        a_work[part] = (neck_own[part] + a_pair_r[part].astype(F32)).astype(BF16)
    a_plane = plane_stage(a_piece_of, a_xy, xy_sem, 0)

    b_pair[0].wait_recv()
    down, level = rest_terms(core)
    b_work[:, 0:2] = (down + b_pair_r[:, 0:2].astype(F32)).astype(BF16)
    b_work[0:LEVEL_OWNERS, 2:5] = (level + b_pair_r[0:LEVEL_OWNERS, 2:5].astype(F32)).astype(BF16)
    b_work[LEVEL_OWNERS:, 2:5] = nothing
    b_plane = plane_stage(b_piece_of, b_xy, xy_sem, 16)

    for c in e4:
        c.wait_recv()
    g2f[0:8] = jnp.zeros((8, 128), F32)
    g2f[8 + 10 * WIDE:] = jnp.zeros((8, 128), F32)
    for r in range(10):
        row_ok = top_ok if r == 0 else bottom_ok if r == 9 else None
        base = 8 + r * WIDE
        left, mid, right = gp[r, 0:16].astype(F32) * left_ok, gp[r, 16:80].astype(F32), gp[r, 80:96].astype(F32) * right_ok
        if row_ok is not None:
            left, mid, right = left * row_ok, mid * row_ok, right * row_ok
        g2f[base:base + 16] = left
        g2f[base + 16:base + 80] = mid
        g2f[base + 80:base + 96] = right
    for r in range(10):
        for kx in range(3):
            start = 7 + kx + r * WIDE
            im_b[r * WIDE:(r + 1) * WIDE, kx * 128:(kx + 1) * 128] = g2f[start:start + WIDE].astype(BF16)
    for q in range(2):
        total = lbf[4 * q * WIDE:(4 * q + 4) * WIDE]
        for ky in range(3):
            total = total + dot(im_b[(4 * q + ky) * WIDE:(4 * q + ky + 4) * WIDE], wlt[ky])
        grad_input[4 * q:4 * q + 4] = total.reshape(4, WIDE, 128)[:, 16:80].astype(BF16)

    for c in no_copies:
        c.wait_recv()
    for q in range(4):
        pieces = [no_recv[4 * q + j].astype(F32) for j in range(4)]
        for r in range(4):
            out = pltpu.roll(pieces[3], (32 * (3 - r)) % 128, 1) if r != 3 else pieces[3]
            for j in (2, 1, 0):
                part = pltpu.roll(pieces[j], (32 * (j - r)) % 128, 1) if r != j else pieces[j]
                out = jnp.where(lane < 32 * (j + 1), part, out)
            neck_out[r, :, 128 * q:128 * q + 128] = out.astype(BF16)

    def z_send(piece, buf, tiles, first, sems, offset):
        copies = []
        for t in range(tiles):
            c = copy_z(piece.at[t], buf.at[z], sems, offset + t, offset + z, column(first + t))
            copies.append((z != first + t, c))
        return copies

    def copy_z(src, dst, sems, ks, kr, dev):
        return pltpu.make_async_remote_copy(
            src_ref=src, dst_ref=dst, send_sem=sems.at[0, ks], recv_sem=sems.at[1, kr],
            device_id=dev, device_id_type=MESH,
        )

    def start_all(copies):
        for cond, c in copies:
            pl.when(cond)(c.start)

    def plane_sum(piece_of, buf, own_ref, copies, out):
        for c in copies:
            c.wait_recv()
        total = own_ref[...].astype(F32)
        for k in range(1, 16):
            total = total + buf[k].astype(F32)
        out[...] = total.astype(BF16)

    def owns(first, tiles):
        return (z >= first) & (z < first + tiles)

    def z_sum(piece, buf, fin, tiles, first, sems, offset, scale):
        @pl.when(owns(first, tiles))
        def _():
            mine = z - first
            for s in range(16):
                @pl.when(z != s)
                def _(s=s):
                    copy_z(piece.at[0], buf.at[s], sems, offset, offset + s, column(s)).wait_recv()
            buf[z] = piece[mine]
            total = buf[0].astype(F32)
            for s in range(1, 16):
                total = total + buf[s].astype(F32)
            fin[mine] = (total * scale).astype(BF16)
            for s in range(16):
                @pl.when(z != s)
                def _(s=s):
                    copy_z(fin.at[mine], fin.at[mine], zb_sem, offset + s, offset + mine, column(s)).start()

    def z_back(fin, tiles, first, offset):
        for t in range(tiles):
            @pl.when(z != first + t)
            def _(t=t):
                copy_z(fin.at[t], fin.at[t], zb_sem, offset, offset + t, column(first + t)).wait_recv()

    def z_back_sent(fin, tiles, first, offset):
        @pl.when(owns(first, tiles))
        def _():
            for s in range(16):
                @pl.when(z != s)
                def _(s=s):
                    copy_z(fin.at[0], fin.at[0], zb_sem, offset + s, offset, column(s)).wait_send()

    plane_sum(a_piece_of, a_xy, a_piece_of(gx), a_plane, a_piece)
    a_zs = z_send(a_piece, a_z, NECK_TILES, 0, z_sem, 0)
    start_all(a_zs)
    plane_sum(b_piece_of, b_xy, b_piece_of(gx), b_plane, b_piece)
    b_zs = z_send(b_piece, b_z, REST_TILES, NECK_TILES, z_sem, 16)
    start_all(b_zs)
    z_sum(a_piece, a_z, a_fin, NECK_TILES, 0, z_sem, 0, scales[0])
    z_sum(b_piece, b_z, b_fin, REST_TILES, NECK_TILES, z_sem, 16, jnp.where(z < NECK_TILES + 2, scales[0], scales[1]))

    z_back(a_fin, NECK_TILES, 0, 0)
    a_all[core, gx] = a_fin[...]
    a_mine = a_all.at[core, gx]
    a_back = go([copy(a_mine, a_mine, xyb_sem, k, plane[k]) for k in range(1, 16)])
    z_back(b_fin, REST_TILES, NECK_TILES, 16)
    b_all[core, gx] = b_fin[...]
    b_mine = b_all.at[core, gx]
    b_back = go([copy(b_mine, b_mine, xyb_sem, 16 + k, plane[k]) for k in range(1, 16)])

    def landed(ref, tiles, sems, first):
        for k in range(1, 16):
            slot = ref.at[core, (gx + 16 - k) % 16]
            copy(slot, slot, sems, first + k, plane[k]).wait_recv()

    landed(a_all, NECK_TILES, xyb_sem, 0)
    a_swap = go([copy(a_all.at[core], a_all.at[core], pair_sem, 2, pair_dev)])
    landed(b_all, REST_TILES, xyb_sem, 16)
    b_swap = go([copy(b_all.at[core], b_all.at[core], pair_sem, 3, pair_dev)])
    copy(a_all.at[other], a_all.at[other], pair_sem, 2, pair_dev).wait_recv()
    for half in range(2):
        lanes = slice(half * 128, half * 128 + 128)
        grad_neck[:, lanes] = a_all[half].reshape(2304, 128)
    copy(b_all.at[other], b_all.at[other], pair_sem, 3, pair_dev).wait_recv()
    for half in range(2):
        lanes = slice(half * 128, half * 128 + 128)
        grad_down[:, lanes] = b_all[half, :, 0:2].reshape(512, 128)
        grad_level[half * 576:(half + 1) * 576] = b_all[half, 0:LEVEL_OWNERS, 2:5].reshape(576, 128)

    for c in sent:
        c.wait_send()
    for cond, c in a_zs + b_zs:
        pl.when(cond)(c.wait_send)
    z_back_sent(a_fin, NECK_TILES, 0, 0)
    z_back_sent(b_fin, REST_TILES, NECK_TILES, 16)


def local(level_in, w_level, w_down, w_neck, cotangent):
    device_count = lax.axis_size("gy") * lax.axis_size("gx")
    level_count = level_in.shape[0] * level_in.shape[1] * device_count
    level_scale = 1.0 / math.sqrt(level_count)
    neck_scale = 1.0 / math.sqrt(level_count // 4)
    vmem = pl.BlockSpec(memory_space=pltpu.VMEM)
    hbm = pl.BlockSpec(memory_space=pl.ANY)
    dma = pltpu.SemaphoreType.DMA

    def v(*shape, dtype=BF16):
        return pltpu.VMEM(shape, dtype)

    def group(tiles, flat):
        whole = (16 * tiles, 16, 128) if flat else (16, tiles, 16, 128)
        return [
            v(*whole), v(*whole), v(*whole), v(16, tiles, 16, 128), v(tiles, 16, 128), v(16, 16, 128), v(tiles, 16, 128),
            v(2, 16, tiles, 16, 128),
        ]

    outs = pl.pallas_call(
        functools.partial(kernel, (neck_scale, level_scale)),
        out_shape=[
            jax.ShapeDtypeStruct((4, 16, 512), BF16),
            jax.ShapeDtypeStruct((8, 64, 128), BF16),
            jax.ShapeDtypeStruct((1152, 128), BF16),
            jax.ShapeDtypeStruct((512, 256), BF16),
            jax.ShapeDtypeStruct((2304, 256), BF16),
        ],
        in_specs=[vmem, hbm, hbm, hbm, vmem],
        out_specs=[vmem] * 5,
        scratch_shapes=[
            v(3, 384, 128), v(512, 256), v(3, 768, 256), v(3, 384, 128),
            v(18, WIDE, 128), v(16 + 18 * WIDE, 128, dtype=F32), v(18 * WIDE, 384),
            v(8 * WIDE, 128, dtype=F32), v(16 * WIDE, 128, dtype=F32), v(8 * NARROW, 512),
            v(16 + 8 * NARROW, 256, dtype=F32), v(8 * NARROW, 768),
            v(6 * NARROW, 256, dtype=F32), v(16 + 6 * NARROW, 256, dtype=F32), v(6 * NARROW, 768),
            v(4 * NARROW, 256), v(4 * NARROW, 256), v(8 * WIDE, 128, dtype=F32),
            v(10, WIDE, 128), v(16 + 10 * WIDE, 128, dtype=F32), v(10 * WIDE, 384),
            v(16, 16, 128), v(16, 16, 128), v(4, 32, 256), v(2, 1, 32, 256), v(2, 4, 16, 256), v(2, 2, 1, 16, 256),
            v(16, 16, 128), v(16, 16, 128),
            v(144, 16, 128, dtype=F32), v(1152, 128, dtype=F32), v(512, 256, dtype=F32),
            *group(NECK_TILES, True), *group(REST_TILES, False),
            dma((3,)), dma((2, 8)), dma((2, 16)), dma((2, 8)), dma((2, 16)), dma((2, 8)),
            dma((2, 4)), dma((2, 32)), dma((2, 32)), dma((2, 32)), dma((2, 32)),
        ],
        compiler_params=pltpu.CompilerParams(
            collective_id=0, has_side_effects=True, vmem_limit_bytes=56 * 1024 * 1024
        ),
    )(
        level_in,
        w_level.reshape(3, 384, 128),
        w_down.reshape(512, 256),
        w_neck.reshape(3, 768, 256),
        jnp.transpose(cotangent, (0, 2, 1)),
    )
    return (
        jnp.transpose(outs[0], (0, 2, 1)),
        outs[1],
        outs[2].reshape(w_level.shape),
        outs[3].reshape(w_down.shape),
        outs[4].reshape(w_neck.shape),
    )


def solution(mesh):
    return jax.shard_map(
        local,
        mesh=mesh,
        in_specs=(P("gy", "gx", None), P(), P(), P(), P("gy", None, "gx")),
        out_specs=(P("gy", None, "gx"), P("gy", "gx", None), P(), P(), P()),
        check_vma=False,
    )
```

time: 620 us -> 83.4 us (0.13)
  waiting for transfers between devices: 498 us -> 0 us
  Pallas kernels: 0 us -> 75 us
  starting transfers between devices: 60.5 us -> 0 us
  matrix products: 19 us -> 0 us
  between operations: 15.3 us -> 0.65 us
  other arithmetic: 9.4 us -> 0 us
  local copies, waits for them, and re-layouts: 15 us -> 7.51 us
    psum x1 -> x0, waiting for transfers between devices: 485 us -> none  [local(): reduced = lax.psum((level_wgrad, down_wgrad, neck_wgrad), ('gy', 'gx'))]
    pallas_call x0 -> x1, Pallas kernels: none -> 75 us  [local(): pl.pallas_call(functools.partial(kernel, (neck_scale, level_scale)), out_...]
    ppermute x16 -> x0, starting transfers between devices: 43.7 us -> none  [the longest x8 30.6 us: extended(): lax.ppermute(tail, axis, [(i, (i + 1) % count) for i in range(ends)])]
    dot_general x57 -> x0, matrix products: 19 us -> none  [the longest x36 10.9 us: conv_padded(): jnp.dot(window, weights[offset_y, offset_x], preferred_element_type=jnp.f...]
    all_to_all x2 -> x0, starting transfers between devices: 16.7 us -> none  [the longest x1 9.08 us: local(): lax.all_to_all(neck_tile, 'gx', split_axis=2, concat_axis=1, tiled=True)]
    ppermute x16 -> x0, waiting for transfers between devices: 13.6 us -> none  [the longest x8 13.5 us: extended(): lax.ppermute(head, axis, [((i + 1) % count, i) for i in range(ends)])]
  transfers between devices with their start and end apart: 19 -> 0, of which waited for: 7 -> 0; matrix products, arithmetic and copies ran while one was open for 3% -> 0% of each run, Pallas kernels for 0% -> 0%
where the time goes in v2:
time: 83.4 us; the launch traced here: 83.1 us
  Pallas kernels  75 us (90%)
  local copies, waits for them, and re-layouts  7.51 us (9%)
    pallas_call x1, Pallas kernels, local(): pl.pallas_call(functools.partial(kernel, (neck_scale, level_scale)), out_...  75 us
    unnamed x7, local copies, waits for them, and re-layouts  7.51 us

profile of v2, /device:TPU:1, one launch (start us, length us, event | category | flops | bytes accessed | tf_op | source)
XLA Modules:
  0.0 83.1 jit_solution(11158423480462012409)
XLA Ops:
  0.6 75.0 %shard_map.92 = (bf16[4,16,512]{2,1,0:T(8,128)(2,1)}, bf16[8,64,128]{2,1,0:T(8,128)(2,1)}, bf16[1152,128]{1,0:T(8,128)(2,1)}, bf16[512,256]{1,0:T(8,128)(2,1)}, bf16[2304,256]{1,0:T(8,128)(2,1)}) custom-call(bf16[8,64,128]{2,1,0:T(8,128)(2,1)} %level_in.1, bf16[3,384,128]{2,1,0:T(8,128)(2,1)} %bitcast.11, bf16[512,256]{1,0:T(8,128)(2,1)} %bitcast.13, ...), custom_call_target="tpu_custom_call" | custom-call | tf_op jit(solution)/shard_map/pallas_call | solution.py:482
  75.6 0.0 copy-start
  75.6 1.6 %copy.15 = bf16[4,512,16]{1,2,0:T(8,128)(2,1)} copy(bf16[4,512,16]{1,2,0:T(8,128)(2,1)} %bitcast.14) | data formatting | bytes 131072
  77.2 1.6 %copy.16 = bf16[8,64,128]{2,1,0:T(8,128)(2,1)} copy(bf16[8,64,128]{2,1,0:T(8,128)(2,1)} %get-tuple-element.21) | data formatting | bytes 262144
  78.8 1.7 %copy.17 = bf16[3,3,128,128]{3,2,1,0:T(8,128)(2,1)} copy(bf16[3,3,128,128]{3,2,1,0:T(8,128)(2,1)} %bitcast.10) | data formatting | bytes 589824
  80.5 1.7 %copy.18 = bf16[2,2,128,256]{3,2,1,0:T(8,128)(2,1)} copy(bf16[2,2,128,256]{3,2,1,0:T(8,128)(2,1)} %bitcast.12) | data formatting | bytes 524288
  82.1 0.0 copy-done
  82.1 1.0 %copy.19 = bf16[3,3,256,256]{3,2,1,0:T(8,128)(2,1)} copy(bf16[3,3,256,256]{3,2,1,0:T(8,128)(2,1)S(1)} %bitcast.8) | data formatting | bytes 2359296
Async XLA Ops:
  75.6 6.5 %copy-start = (bf16[2304,256]{1,0:T(8,128)(2,1)S(1)}, bf16[2304,256]{1,0:T(8,128)(2,1)}, u32[]{:S(2)}) copy-start(bf16[2304,256]{1,0:T(8,128)(2,1)} %get-tuple-element.14) | copy-start | bytes 3538948

commit v3 on v2

--- a/solution.py
+++ b/solution.py
@@ -43,14 +43,14 @@
 
 def kernel(
     scales,
-    level_in, wl_hbm, wd_hbm, wn_hbm, cot_in,
-    neck_out, grad_input, grad_level, grad_down, grad_neck,
-    wl, wd, wn, wlt,
+    level_in, wl_hbm, wd_hbm, wn_hbm, cot_hbm,
+    neck_out, grad_input, a_all, b_all,
+    level_own, cot_in, wl, wd, wn, wlt,
     lp, lf, im_l, pre_l, act, dn, nf, im_n, cf, gf, im_g, gate_own, ng, lbf, gp, g2f, im_b,
     cot_send, cot_recv, ct, hr, hc, hx, no_send, no_recv,
     neck_own, level_acc, down_acc,
-    a_pair_s, a_pair_r, a_work, a_xy, a_piece, a_z, a_fin, a_all,
-    b_pair_s, b_pair_r, b_work, b_xy, b_piece, b_z, b_fin, b_all,
+    a_pair_s, a_pair_r, a_work, a_xy, a_piece, a_z, a_fin,
+    b_pair_s, b_pair_r, b_work, b_xy, b_piece, b_z, b_fin,
     w_sem, e1_sem, cot_sem, ch_sem, no_sem, e4_sem,
     pair_sem, xy_sem, z_sem, zb_sem, xyb_sem,
 ):
@@ -73,6 +73,8 @@
         pl.semaphore_signal(barrier, inc=1, device_id=peer, device_id_type=MESH)
 
     loads = [
+        pltpu.make_async_copy(cot_hbm, cot_in, w_sem.at[3]),
+        pltpu.make_async_copy(level_in, level_own, w_sem.at[4]),
         pltpu.make_async_copy(wl_hbm, wl, w_sem.at[0]),
         pltpu.make_async_copy(wd_hbm, wd, w_sem.at[1]),
         pltpu.make_async_copy(wn_hbm, wn, w_sem.at[2]),
@@ -94,6 +96,7 @@
         sent.extend(copies)
         return copies
 
+    loads[0].wait()
     lane = lax.broadcasted_iota(jnp.int32, (16, 128), 1)
     for q in range(4):
         rows = [cot_in[r, :, 128 * q:128 * q + 128].astype(F32) for r in range(4)]
@@ -110,11 +113,12 @@
     left_ok = jnp.where(gx > 0, 1.0, 0.0).astype(F32)
     right_ok = jnp.where(gx < 15, 1.0, 0.0).astype(F32)
 
+    loads[1].wait()
     lf[0:8] = jnp.zeros((8, 128), F32)
     lf[8 + 18 * WIDE:] = jnp.zeros((8, 128), F32)
     for r in range(8):
         start = 8 + (r + RIM) * WIDE + 16
-        lf[start:start + 64] = level_in[r].astype(F32)
+        lf[start:start + 64] = level_own[r].astype(F32)
 
     pl.semaphore_wait(barrier, len(peers))
 
@@ -130,7 +134,7 @@
         for n, (dy, dx) in enumerate(SIDES)
     ])
 
-    loads[0].wait()
+    loads[2].wait()
     for ky in range(3):
         for kx in range(3):
             w = wl[2 - ky, (2 - kx) * 128:(3 - kx) * 128, :].astype(F32)
@@ -184,7 +188,7 @@
         for q in range(2):
             lanes = slice(128 * (2 * (rr % 2) + q), 128 * (2 * (rr % 2) + q) + 128)
             dn[(rr // 2) * NARROW:(rr // 2 + 1) * NARROW, lanes] = act[pl.ds(rr * WIDE + q, NARROW, stride=2), :].astype(BF16)
-    loads[1].wait()
+    loads[3].wait()
     col = lax.broadcasted_iota(jnp.int32, (NARROW, 256), 0)
     col_ok = jnp.where(col < 8, left_ok, jnp.where(col >= 40, right_ok, 1.0))
     col_own = jnp.where((col >= 8) & (col < 40), 1.0, 0.0)
@@ -200,7 +204,7 @@
         nf[8 + r * NARROW:8 + (r + 1) * NARROW] = row
     for kx in range(3):
         im_n[:, kx * 256:(kx + 1) * 256] = nf[7 + kx:7 + kx + 8 * NARROW].astype(BF16)
-    loads[2].wait()
+    loads[4].wait()
     neck_pre = dot(im_n[0:6 * NARROW], wn[0])
     for ky in (1, 2):
         neck_pre = neck_pre + dot(im_n[ky * NARROW:(ky + 6) * NARROW], wn[ky])
@@ -425,32 +429,31 @@
     z_sum(b_piece, b_z, b_fin, REST_TILES, NECK_TILES, z_sem, 16, jnp.where(z < NECK_TILES + 2, scales[0], scales[1]))
 
     z_back(a_fin, NECK_TILES, 0, 0)
-    a_all[core, gx] = a_fin[...]
-    a_mine = a_all.at[core, gx]
+    def a_slot(o):
+        return a_all.at[core, pl.ds(o * NECK_TILES, NECK_TILES)]
+
+    def b_slot(o):
+        return b_all.at[core, o]
+
+    a_all[core, pl.ds(gx * NECK_TILES, NECK_TILES)] = a_fin[...]
+    a_mine = a_slot(gx)
     a_back = go([copy(a_mine, a_mine, xyb_sem, k, plane[k]) for k in range(1, 16)])
     z_back(b_fin, REST_TILES, NECK_TILES, 16)
     b_all[core, gx] = b_fin[...]
     b_mine = b_all.at[core, gx]
     b_back = go([copy(b_mine, b_mine, xyb_sem, 16 + k, plane[k]) for k in range(1, 16)])
 
-    def landed(ref, tiles, sems, first):
+    def landed(slot_of, sems, first):
         for k in range(1, 16):
-            slot = ref.at[core, (gx + 16 - k) % 16]
+            slot = slot_of((gx + 16 - k) % 16)
             copy(slot, slot, sems, first + k, plane[k]).wait_recv()
 
-    landed(a_all, NECK_TILES, xyb_sem, 0)
-    a_swap = go([copy(a_all.at[core], a_all.at[core], pair_sem, 2, pair_dev)])
-    landed(b_all, REST_TILES, xyb_sem, 16)
-    b_swap = go([copy(b_all.at[core], b_all.at[core], pair_sem, 3, pair_dev)])
+    landed(a_slot, xyb_sem, 0)
+    go([copy(a_all.at[core], a_all.at[core], pair_sem, 2, pair_dev)])
+    landed(b_slot, xyb_sem, 16)
+    go([copy(b_all.at[core], b_all.at[core], pair_sem, 3, pair_dev)])
     copy(a_all.at[other], a_all.at[other], pair_sem, 2, pair_dev).wait_recv()
-    for half in range(2):
-        lanes = slice(half * 128, half * 128 + 128)
-        grad_neck[:, lanes] = a_all[half].reshape(2304, 128)
     copy(b_all.at[other], b_all.at[other], pair_sem, 3, pair_dev).wait_recv()
-    for half in range(2):
-        lanes = slice(half * 128, half * 128 + 128)
-        grad_down[:, lanes] = b_all[half, :, 0:2].reshape(512, 128)
-        grad_level[half * 576:(half + 1) * 576] = b_all[half, 0:LEVEL_OWNERS, 2:5].reshape(576, 128)
 
     for c in sent:
         c.wait_send()
@@ -460,13 +463,27 @@
     z_back_sent(b_fin, REST_TILES, NECK_TILES, 16)
 
 
+def results_kernel(strip, level, a_all, b_all, neck_out, grad_input, grad_level, grad_down, grad_neck, sems):
+    copies = [(strip, neck_out), (level, grad_input)]
+    for half in range(2):
+        lanes = slice(128 * half, 128 * half + 128)
+        copies.append((a_all.at[half], grad_neck.at[:, :, lanes]))
+        copies.append((b_all.at[half, :, 0:2], grad_down.at[:, :, :, lanes]))
+        copies.append((b_all.at[half, 0:LEVEL_OWNERS, 2:5], grad_level.at[half]))
+    copies = [pltpu.make_async_copy(src, dst, sems.at[n]) for n, (src, dst) in enumerate(copies)]
+    for c in copies:
+        c.start()
+    for c in copies:
+        c.wait()
+
+
 def local(level_in, w_level, w_down, w_neck, cotangent):
     device_count = lax.axis_size("gy") * lax.axis_size("gx")
     level_count = level_in.shape[0] * level_in.shape[1] * device_count
     level_scale = 1.0 / math.sqrt(level_count)
     neck_scale = 1.0 / math.sqrt(level_count // 4)
     vmem = pl.BlockSpec(memory_space=pltpu.VMEM)
-    hbm = pl.BlockSpec(memory_space=pl.ANY)
+    hbm = pl.BlockSpec(memory_space=pltpu.HBM)
     dma = pltpu.SemaphoreType.DMA
 
     def v(*shape, dtype=BF16):
@@ -476,7 +493,6 @@
         whole = (16 * tiles, 16, 128) if flat else (16, tiles, 16, 128)
         return [
             v(*whole), v(*whole), v(*whole), v(16, tiles, 16, 128), v(tiles, 16, 128), v(16, 16, 128), v(tiles, 16, 128),
-            v(2, 16, tiles, 16, 128),
         ]
 
     outs = pl.pallas_call(
@@ -484,13 +500,13 @@
         out_shape=[
             jax.ShapeDtypeStruct((4, 16, 512), BF16),
             jax.ShapeDtypeStruct((8, 64, 128), BF16),
-            jax.ShapeDtypeStruct((1152, 128), BF16),
-            jax.ShapeDtypeStruct((512, 256), BF16),
-            jax.ShapeDtypeStruct((2304, 256), BF16),
+            jax.ShapeDtypeStruct((2, 16 * NECK_TILES, 16, 128), BF16),
+            jax.ShapeDtypeStruct((2, 16, REST_TILES, 16, 128), BF16),
         ],
-        in_specs=[vmem, hbm, hbm, hbm, vmem],
-        out_specs=[vmem] * 5,
+        in_specs=[hbm] * 5,
+        out_specs=[vmem] * 4,
         scratch_shapes=[
+            v(8, 64, 128), v(4, 16, 512),
             v(3, 384, 128), v(512, 256), v(3, 768, 256), v(3, 384, 128),
             v(18, WIDE, 128), v(16 + 18 * WIDE, 128, dtype=F32), v(18 * WIDE, 384),
             v(8 * WIDE, 128, dtype=F32), v(16 * WIDE, 128, dtype=F32), v(8 * NARROW, 512),
@@ -502,19 +518,35 @@
             v(16, 16, 128), v(16, 16, 128),
             v(144, 16, 128, dtype=F32), v(1152, 128, dtype=F32), v(512, 256, dtype=F32),
             *group(NECK_TILES, True), *group(REST_TILES, False),
-            dma((3,)), dma((2, 8)), dma((2, 16)), dma((2, 8)), dma((2, 16)), dma((2, 8)),
+            dma((5,)), dma((2, 8)), dma((2, 16)), dma((2, 8)), dma((2, 16)), dma((2, 8)),
             dma((2, 4)), dma((2, 32)), dma((2, 32)), dma((2, 32)), dma((2, 32)),
         ],
         compiler_params=pltpu.CompilerParams(
-            collective_id=0, has_side_effects=True, vmem_limit_bytes=56 * 1024 * 1024
+            collective_id=0, has_side_effects=True, vmem_limit_bytes=24 * 1024 * 1024
         ),
     )(
-        level_in,
-        w_level.reshape(3, 384, 128),
-        w_down.reshape(512, 256),
-        w_neck.reshape(3, 768, 256),
-        jnp.transpose(cotangent, (0, 2, 1)),
+        *(pltpu.with_memory_space_constraint(t, pltpu.HBM) for t in (
+            level_in,
+            w_level.reshape(3, 384, 128),
+            w_down.reshape(512, 256),
+            w_neck.reshape(3, 768, 256),
+            jnp.transpose(cotangent, (0, 2, 1)),
+        ))
     )
+    outs = pl.pallas_call(
+        results_kernel,
+        out_shape=[
+            jax.ShapeDtypeStruct((4, 16, 512), BF16),
+            jax.ShapeDtypeStruct((8, 64, 128), BF16),
+            jax.ShapeDtypeStruct((2, LEVEL_OWNERS, 3, 16, 128), BF16),
+            jax.ShapeDtypeStruct((16, 2, 16, 256), BF16),
+            jax.ShapeDtypeStruct((144, 16, 256), BF16),
+        ],
+        in_specs=[vmem] * 4,
+        out_specs=[hbm] * 5,
+        scratch_shapes=[dma((8,))],
+        compiler_params=pltpu.CompilerParams(vmem_limit_bytes=1024 * 1024),
+    )(*outs)
     return (
         jnp.transpose(outs[0], (0, 2, 1)),
         outs[1],

time: 83.4 us -> 74.4 us (0.89)
  local copies, waits for them, and re-layouts: 7.51 us -> 0 us
  Pallas kernels: 75 us -> 73.6 us
    unnamed x7 -> x0, local copies, waits for them, and re-layouts: 7.51 us -> none
    pallas_call x1, Pallas kernels: 75 us -> 72.3 us  [local(): pl.pallas_call(functools.partial(kernel, (neck_scale, level_scale)), out_...]
    pallas_call x0 -> x1, Pallas kernels: none -> 1.32 us  [local(): pl.pallas_call(results_kernel, out_shape=[jax.ShapeDtypeStruct((4, 16, 51...]
where the time goes in v3:
time: 74.4 us; the launch traced here: 74.3 us
  Pallas kernels  73.6 us (99%)
    pallas_call x1, Pallas kernels, local(): pl.pallas_call(functools.partial(kernel, (neck_scale, level_scale)), out_...  72.3 us

profile of v3, /device:TPU:1, one launch (start us, length us, event | category | flops | bytes accessed | tf_op | source)
XLA Modules:
  0.0 74.3 jit_solution(11743852044644488900)
XLA Ops:
  0.6 72.3 %shard_map.92 = (bf16[4,16,512]{2,1,0:T(8,128)(2,1)S(1)}, bf16[8,64,128]{2,1,0:T(8,128)(2,1)S(1)}, bf16[2,144,16,128]{3,2,1,0:T(8,128)(2,1)S(1)}, bf16[2,16,5,16,128]{4,3,2,1,0:T(8,128)(2,1)S(1)}) custom-call(bf16[8,64,128]{2,1,0:T(8,128)(2,1)} %level_in.1, bf16[3,384,128]{2,1,0:T(8,128)(2,1)} %bitcast.9, bf16[512,256]{1,0:T(8,128)(2,1)} %bitcast.10, ...), custom_call_target="tpu_custom_call" | custom-call | tf_op jit(solution)/shard_map/pallas_call | solution.py:498
  73.0 1.3 %shard_map.93 = (bf16[4,16,512]{2,1,0:T(8,128)(2,1)}, bf16[8,64,128]{2,1,0:T(8,128)(2,1)}, bf16[2,12,3,16,128]{4,3,2,1,0:T(8,128)(2,1)}, bf16[16,2,16,256]{3,2,1,0:T(8,128)(2,1)}, bf16[144,16,256]{2,1,0:T(8,128)(2,1)}) custom-call(bf16[4,16,512]{2,1,0:T(8,128)(2,1)S(1)} %get-tuple-element.14.strip, bf16[8,64,128]{2,1,0:T(8,128)(2,1)S(1)} %get-tuple-element.15.level, ...), custom_call_target="tpu_custom_call" | custom-call | tf_op jit(solution)/shard_map/pallas_call | solution.py:536

commit v4 on v3

--- a/solution.py
+++ b/solution.py
@@ -15,13 +15,11 @@
 WIDE = 96
 NARROW = 48
 SIDES = [(dy, dx) for dy in (-1, 0, 1) for dx in (-1, 0, 1) if (dy, dx) != (0, 0)]
+FAR_FIRST = sorted(range(1, 16), key=lambda k: -(min(k // 4, 4 - k // 4) + min(k % 4, 4 - k % 4)))
+Z_FAR_FIRST = sorted(range(1, 16), key=lambda k: -min(k, 16 - k))
 NECK_TILES = 9
 REST_TILES = 5
 LEVEL_OWNERS = 12
-
-
-def sigmoid(v):
-    return 1.0 / (1.0 + jnp.exp(-v))
 
 
 def slope_of(v):
@@ -47,7 +45,7 @@
     neck_out, grad_input, a_all, b_all,
     level_own, cot_in, wl, wd, wn, wlt,
     lp, lf, im_l, pre_l, act, dn, nf, im_n, cf, gf, im_g, gate_own, ng, lbf, gp, g2f, im_b,
-    cot_send, cot_recv, ct, hr, hc, hx, no_send, no_recv,
+    cot_send, cot_recv, ct, hr, no_send, no_recv,
     neck_own, level_acc, down_acc,
     a_pair_s, a_pair_r, a_work, a_xy, a_piece, a_z, a_fin,
     b_pair_s, b_pair_r, b_work, b_xy, b_piece, b_z, b_fin,
@@ -62,7 +60,12 @@
         return ((gy + dy + 32) % 32, (gx + dx + 16) % 16)
 
     pair_dev = (z * 2 + other, gx)
-    plane = [None] + [(gy, (gx + k) % 16) for k in range(1, 16)]
+    x, y = gx // 4, gx % 4
+
+    def in_plane(k, sign=1):
+        return ((x + sign * (k // 4) + 4) % 4) * 4 + (y + sign * (k % 4) + 4) % 4
+
+    plane = [None] + [(gy, in_plane(k)) for k in range(1, 16)]
 
     def column(zz):
         return (zz * 2 + core, gx)
@@ -79,7 +82,7 @@
         pltpu.make_async_copy(wd_hbm, wd, w_sem.at[1]),
         pltpu.make_async_copy(wn_hbm, wn, w_sem.at[2]),
     ]
-    for load in loads:
+    for load in loads[:2]:
         load.start()
 
     def copy(src, dst, sems, k, dev):
@@ -97,6 +100,8 @@
         return copies
 
     loads[0].wait()
+    for load in loads[2:]:
+        load.start()
     lane = lax.broadcasted_iota(jnp.int32, (16, 128), 1)
     for q in range(4):
         rows = [cot_in[r, :, 128 * q:128 * q + 128].astype(F32) for r in range(4)]
@@ -105,7 +110,9 @@
             for r in (2, 1, 0):
                 part = pltpu.roll(rows[r], (32 * (r - j)) % 128, 1) if r != j else rows[r]
                 out = jnp.where(lane < 32 * (r + 1), part, out)
-            cot_send[4 * q + j] = out.astype(BF16)
+            cot_send[4 * q + j, 0] = out.astype(BF16)
+    for t in range(16):
+        cot_send[t, 1] = jnp.where(lane % 32 < 16, cot_send[(t + 1) % 16, 0].astype(F32), cot_send[(t + 15) % 16, 0].astype(F32)).astype(BF16)
     cot_recv[gx] = cot_send[gx]
 
     top_ok = jnp.where(gy > 0, 1.0, 0.0).astype(F32)
@@ -123,14 +130,14 @@
     pl.semaphore_wait(barrier, len(peers))
 
     cot_copies = go([
-        copy(cot_send.at[(gx + k) % 16], cot_recv.at[gx], cot_sem, k, plane[k]) for k in range(1, 16)
+        copy(cot_send.at[in_plane(k)], cot_recv.at[gx], cot_sem, k, plane[k]) for k in FAR_FIRST
     ])
     src_rows = {-1: slice(0, RIM), 0: slice(0, 8), 1: slice(8 - RIM, 8)}
     src_cols = {-1: slice(0, 16), 0: slice(0, 64), 1: slice(48, 64)}
     dst_rows = {-1: slice(RIM + 8, RIM + 8 + RIM), 0: slice(RIM, RIM + 8), 1: slice(0, RIM)}
     dst_cols = {-1: slice(80, 96), 0: slice(16, 80), 1: slice(0, 16)}
     e1 = go([
-        copy(level_in.at[src_rows[dy], src_cols[dx]], lp.at[dst_rows[dy], dst_cols[dx]], e1_sem, n, side(dy, dx))
+        copy(level_own.at[src_rows[dy], src_cols[dx]], lp.at[dst_rows[dy], dst_cols[dx]], e1_sem, n, side(dy, dx))
         for n, (dy, dx) in enumerate(SIDES)
     ])
 
@@ -142,21 +149,16 @@
 
     for c in cot_copies:
         c.wait_recv()
-    ct[...] = cot_recv[...].reshape(256, 128).astype(F32).T.astype(BF16).reshape(4, 32, 256)
-    one_row = {-1: slice(0, 1), 0: slice(0, 4), 1: slice(3, 4)}
-    half_cols = {-1: slice(0, 16), 0: slice(0, 32), 1: slice(16, 32)}
-
-    def rim_buffer(dy, dx):
-        if dx == 0:
-            return hr.at[(dy + 1) // 2]
-        if dy == 0:
-            return hc.at[(dx + 1) // 2]
-        return hx.at[(dy + 1) // 2, (dx + 1) // 2]
-
-    ch = go([
-        copy(ct.at[one_row[dy], half_cols[dx]], rim_buffer(dy, dx), ch_sem, n, side(dy, dx))
-        for n, (dy, dx) in enumerate(SIDES)
-    ])
+    cot_tile = cot_recv[:, 0].reshape(256, 128).astype(F32).T
+    cot_beside = cot_recv[:, 1].reshape(256, 128).astype(F32).T
+    for r in range(4):
+        base = (r + 1) * NARROW
+        cf[base:base + 8] = cot_beside[32 * r + 24:32 * r + 32] * left_ok
+        cf[base + 8:base + 40] = cot_tile[32 * r:32 * r + 32]
+        cf[base + 40:base + 48] = cot_beside[32 * r:32 * r + 8] * right_ok
+    ct[0] = cf[NARROW:2 * NARROW].astype(BF16)
+    ct[1] = cf[4 * NARROW:5 * NARROW].astype(BF16)
+    ch = go([copy(ct.at[n], hr.at[n], ch_sem, n, side(2 * n - 1, 0)) for n in range(2)])
 
     for c in e1:
         c.wait_recv()
@@ -209,29 +211,13 @@
     for ky in (1, 2):
         neck_pre = neck_pre + dot(im_n[ky * NARROW:(ky + 6) * NARROW], wn[ky])
 
-    for c in ch:
-        c.wait_recv()
-    for r in range(6):
-        if 1 <= r <= 4:
-            mid = ct[r - 1].astype(F32)
-            left = hc[1, r - 1, 8:16].astype(F32) * left_ok
-            right = hc[0, r - 1, 0:8].astype(F32) * right_ok
-        else:
-            n, ok = (1, top_ok) if r == 0 else (0, bottom_ok)
-            mid = hr[n, 0].astype(F32) * ok
-            left = hx[n, 1, 0, 8:16].astype(F32) * (left_ok * ok)
-            right = hx[n, 0, 0, 0:8].astype(F32) * (right_ok * ok)
-        base = r * NARROW
-        cf[base:base + 8] = left
-        cf[base + 8:base + 40] = mid
-        cf[base + 40:base + 48] = right
-
-    gate = (cf[...] * slope_of(neck_pre)).astype(BF16).astype(F32)
+    own = slice(NARROW, 5 * NARROW)
     gf[0:8] = jnp.zeros((8, 256), F32)
     gf[8 + 6 * NARROW:] = jnp.zeros((8, 256), F32)
-    gf[8:8 + 6 * NARROW] = gate
+    gate = (cf[own] * slope_of(neck_pre[own])).astype(BF16).astype(F32)
+    gf[8 + NARROW:8 + 5 * NARROW] = gate
     for r in range(4):
-        gate_own[r * NARROW:(r + 1) * NARROW] = (gate[(r + 1) * NARROW:(r + 2) * NARROW] * col_own).astype(BF16)
+        gate_own[r * NARROW:(r + 1) * NARROW] = (gate[r * NARROW:(r + 1) * NARROW] * col_own).astype(BF16)
 
     def half_lanes(half):
         return pl.ds(pl.multiple_of(half * 128, 128), 128)
@@ -245,13 +231,34 @@
     for ky in range(3):
         neck_own[48 * ky:48 * ky + 48] = dot_tn(im_n[(1 + ky) * NARROW:(5 + ky) * NARROW], mine).reshape(48, 16, 128)
 
+    def plane_stage(work, buf, sems, first):
+        return go([copy(work(in_plane(k)), buf.at[k], sems, first + k, plane[k]) for k in FAR_FIRST])
+
+    def a_piece_of(o):
+        return a_work.at[pl.ds(o * NECK_TILES, NECK_TILES)]
+
+    def b_piece_of(o):
+        return b_work.at[o]
+
+    a_pair[0].wait_recv()
+    for n in range(16):
+        part = slice(n * NECK_TILES, (n + 1) * NECK_TILES)
+        a_work[part] = (neck_own[part] + a_pair_r[part].astype(F32)).astype(BF16)
+    a_plane = plane_stage(a_piece_of, a_xy, xy_sem, 0)
+
     rows = []
     for r in range(4):
         v = neck_pre[(r + 1) * NARROW + 8:(r + 1) * NARROW + 40]
         rows.append(nf[8 + (r + 2) * NARROW + 8:8 + (r + 2) * NARROW + 40] + v * jax.nn.sigmoid(v))
     no_send[...] = jnp.concatenate(rows, axis=0).T.astype(BF16).reshape(16, 16, 128)
     no_recv[gx] = no_send[gx]
-    no_copies = go([copy(no_send.at[(gx + k) % 16], no_recv.at[gx], no_sem, k, plane[k]) for k in range(1, 16)])
+    no_copies = go([copy(no_send.at[in_plane(k)], no_recv.at[gx], no_sem, k, plane[k]) for k in FAR_FIRST])
+
+    for c in ch:
+        c.wait_recv()
+    for n, ok, rows in ((1, top_ok, slice(0, NARROW)), (0, bottom_ok, slice(5 * NARROW, 6 * NARROW))):
+        v = hr[n].astype(F32) * ok * slope_of(neck_pre[rows])
+        gf[8 + rows.start:8 + rows.stop] = v.astype(BF16).astype(F32)
 
     for kx in range(3):
         im_g[:, kx * 256:(kx + 1) * 256] = gf[7 + kx:7 + kx + 6 * NARROW].astype(BF16)
@@ -303,21 +310,6 @@
     b_pair_s[LEVEL_OWNERS:, 2:5] = nothing
     b_pair = go([copy(b_pair_s, b_pair_r, pair_sem, 1, pair_dev)])
 
-    def plane_stage(work, buf, sems, first):
-        return go([copy(work(( gx + k) % 16), buf.at[k], sems, first + k, plane[k]) for k in range(1, 16)])
-
-    def a_piece_of(o):
-        return a_work.at[pl.ds(o * NECK_TILES, NECK_TILES)]
-
-    def b_piece_of(o):
-        return b_work.at[o]
-
-    a_pair[0].wait_recv()
-    for n in range(16):
-        part = slice(n * NECK_TILES, (n + 1) * NECK_TILES)
-        a_work[part] = (neck_own[part] + a_pair_r[part].astype(F32)).astype(BF16)
-    a_plane = plane_stage(a_piece_of, a_xy, xy_sem, 0)
-
     b_pair[0].wait_recv()
     down, level = rest_terms(core)
     b_work[:, 0:2] = (down + b_pair_r[:, 0:2].astype(F32)).astype(BF16)
@@ -400,10 +392,8 @@
             for s in range(1, 16):
                 total = total + buf[s].astype(F32)
             fin[mine] = (total * scale).astype(BF16)
-            for s in range(16):
-                @pl.when(z != s)
-                def _(s=s):
-                    copy_z(fin.at[mine], fin.at[mine], zb_sem, offset + s, offset + mine, column(s)).start()
+            for k in Z_FAR_FIRST:
+                copy_z(fin.at[mine], fin.at[mine], zb_sem, offset + k, offset + mine, column((z + k) % 16)).start()
 
     def z_back(fin, tiles, first, offset):
         for t in range(tiles):
@@ -414,10 +404,8 @@
     def z_back_sent(fin, tiles, first, offset):
         @pl.when(owns(first, tiles))
         def _():
-            for s in range(16):
-                @pl.when(z != s)
-                def _(s=s):
-                    copy_z(fin.at[0], fin.at[0], zb_sem, offset + s, offset, column(s)).wait_send()
+            for k in Z_FAR_FIRST:
+                copy_z(fin.at[0], fin.at[0], zb_sem, offset + k, offset, column((z + k) % 16)).wait_send()
 
     plane_sum(a_piece_of, a_xy, a_piece_of(gx), a_plane, a_piece)
     a_zs = z_send(a_piece, a_z, NECK_TILES, 0, z_sem, 0)
@@ -437,15 +425,15 @@
 
     a_all[core, pl.ds(gx * NECK_TILES, NECK_TILES)] = a_fin[...]
     a_mine = a_slot(gx)
-    a_back = go([copy(a_mine, a_mine, xyb_sem, k, plane[k]) for k in range(1, 16)])
+    a_back = go([copy(a_mine, a_mine, xyb_sem, k, plane[k]) for k in FAR_FIRST])
     z_back(b_fin, REST_TILES, NECK_TILES, 16)
     b_all[core, gx] = b_fin[...]
     b_mine = b_all.at[core, gx]
-    b_back = go([copy(b_mine, b_mine, xyb_sem, 16 + k, plane[k]) for k in range(1, 16)])
+    b_back = go([copy(b_mine, b_mine, xyb_sem, 16 + k, plane[k]) for k in FAR_FIRST])
 
     def landed(slot_of, sems, first):
         for k in range(1, 16):
-            slot = slot_of((gx + 16 - k) % 16)
+            slot = slot_of(in_plane(k, -1))
             copy(slot, slot, sems, first + k, plane[k]).wait_recv()
 
     landed(a_slot, xyb_sem, 0)
@@ -514,7 +502,7 @@
             v(6 * NARROW, 256, dtype=F32), v(16 + 6 * NARROW, 256, dtype=F32), v(6 * NARROW, 768),
             v(4 * NARROW, 256), v(4 * NARROW, 256), v(8 * WIDE, 128, dtype=F32),
             v(10, WIDE, 128), v(16 + 10 * WIDE, 128, dtype=F32), v(10 * WIDE, 384),
-            v(16, 16, 128), v(16, 16, 128), v(4, 32, 256), v(2, 1, 32, 256), v(2, 4, 16, 256), v(2, 2, 1, 16, 256),
+            v(16, 2, 16, 128), v(16, 2, 16, 128), v(2, NARROW, 256), v(2, NARROW, 256),
             v(16, 16, 128), v(16, 16, 128),
             v(144, 16, 128, dtype=F32), v(1152, 128, dtype=F32), v(512, 256, dtype=F32),
             *group(NECK_TILES, True), *group(REST_TILES, False),

time: 74.4 us -> 76.4 us (1.027)
  Pallas kernels: 73.6 us -> 75.2 us
    pallas_call x1, Pallas kernels: 72.3 us -> 73.9 us  [local(): pl.pallas_call(functools.partial(kernel, (neck_scale, level_scale)), out_...]
where the time goes in v4:
time: 76.4 us; the launch traced here: 75.9 us
  Pallas kernels  75.2 us (98%)
    pallas_call x1, Pallas kernels, local(): pl.pallas_call(functools.partial(kernel, (neck_scale, level_scale)), out_...  73.9 us

profile of v4, /device:TPU:1, one launch (start us, length us, event | category | flops | bytes accessed | tf_op | source)
XLA Modules:
  0.0 75.9 jit_solution(9660949007016425242)
XLA Ops:
  0.6 73.9 %shard_map.92 = (bf16[4,16,512]{2,1,0:T(8,128)(2,1)S(1)}, bf16[8,64,128]{2,1,0:T(8,128)(2,1)S(1)}, bf16[2,144,16,128]{3,2,1,0:T(8,128)(2,1)S(1)}, bf16[2,16,5,16,128]{4,3,2,1,0:T(8,128)(2,1)S(1)}) custom-call(bf16[8,64,128]{2,1,0:T(8,128)(2,1)} %level_in.1, bf16[3,384,128]{2,1,0:T(8,128)(2,1)} %bitcast.9, bf16[512,256]{1,0:T(8,128)(2,1)} %bitcast.10, ...), custom_call_target="tpu_custom_call" | custom-call | tf_op jit(solution)/shard_map/pallas_call | solution.py:486
  74.5 1.3 %shard_map.93 = (bf16[4,16,512]{2,1,0:T(8,128)(2,1)}, bf16[8,64,128]{2,1,0:T(8,128)(2,1)}, bf16[2,12,3,16,128]{4,3,2,1,0:T(8,128)(2,1)}, bf16[16,2,16,256]{3,2,1,0:T(8,128)(2,1)}, bf16[144,16,256]{2,1,0:T(8,128)(2,1)}) custom-call(bf16[4,16,512]{2,1,0:T(8,128)(2,1)S(1)} %get-tuple-element.14.strip, bf16[8,64,128]{2,1,0:T(8,128)(2,1)S(1)} %get-tuple-element.15.level, ...), custom_call_target="tpu_custom_call" | custom-call | tf_op jit(solution)/shard_map/pallas_call | solution.py:524

commit v5 on v4

--- a/solution.py
+++ b/solution.py
@@ -18,6 +18,7 @@
 FAR_FIRST = sorted(range(1, 16), key=lambda k: -(min(k // 4, 4 - k // 4) + min(k % 4, 4 - k % 4)))
 Z_FAR_FIRST = sorted(range(1, 16), key=lambda k: -min(k, 16 - k))
 NECK_TILES = 9
+ROUTE = 5
 REST_TILES = 5
 LEVEL_OWNERS = 12
 
@@ -47,10 +48,10 @@
     lp, lf, im_l, pre_l, act, dn, nf, im_n, cf, gf, im_g, gate_own, ng, lbf, gp, g2f, im_b,
     cot_send, cot_recv, ct, hr, no_send, no_recv,
     neck_own, level_acc, down_acc,
-    a_pair_s, a_pair_r, a_work, a_xy, a_piece, a_z, a_fin,
+    a_pair_s, a_pair_r, a_work, near_a, near_b, far_a, far_b, a_piece, a_z, a_fin,
     b_pair_s, b_pair_r, b_work, b_xy, b_piece, b_z, b_fin,
     w_sem, e1_sem, cot_sem, ch_sem, no_sem, e4_sem,
-    pair_sem, xy_sem, z_sem, zb_sem, xyb_sem,
+    pair_sem, xy_sem, z_sem, zb_sem, xyb_sem, near_sem, far_sem, back1_sem, back2_sem,
 ):
     gy, gx = lax.axis_index("gy"), lax.axis_index("gx")
     z, core = gy // 2, gy % 2
@@ -69,11 +70,6 @@
 
     def column(zz):
         return (zz * 2 + core, gx)
-
-    barrier = pltpu.get_barrier_semaphore()
-    peers = plane[1:] + [column((z + k) % 16) for k in range(1, 16)] + [side(dy, dx) for dy, dx in SIDES if dy != 0]
-    for peer in peers:
-        pl.semaphore_signal(barrier, inc=1, device_id=peer, device_id_type=MESH)
 
     loads = [
         pltpu.make_async_copy(cot_hbm, cot_in, w_sem.at[3]),
@@ -84,6 +80,10 @@
     ]
     for load in loads[:2]:
         load.start()
+    barrier = pltpu.get_barrier_semaphore()
+    peers = plane[1:] + [column((z + k) % 16) for k in range(1, 16)] + [side(dy, dx) for dy, dx in SIDES if dy != 0]
+    for peer in peers:
+        pl.semaphore_signal(barrier, inc=1, device_id=peer, device_id_type=MESH)
 
     def copy(src, dst, sems, k, dev):
         return pltpu.make_async_remote_copy(
@@ -98,6 +98,16 @@
             c.start()
         sent.extend(copies)
         return copies
+
+    pl.semaphore_wait(barrier, len(peers))
+    src_rows = {-1: slice(0, RIM), 0: slice(0, 8), 1: slice(8 - RIM, 8)}
+    src_cols = {-1: slice(0, 16), 0: slice(0, 64), 1: slice(48, 64)}
+    dst_rows = {-1: slice(RIM + 8, RIM + 8 + RIM), 0: slice(RIM, RIM + 8), 1: slice(0, RIM)}
+    dst_cols = {-1: slice(80, 96), 0: slice(16, 80), 1: slice(0, 16)}
+    e1 = go([
+        copy(level_in.at[src_rows[dy], src_cols[dx]], lp.at[dst_rows[dy], dst_cols[dx]], e1_sem, n, side(dy, dx))
+        for n, (dy, dx) in enumerate(SIDES)
+    ])
 
     loads[0].wait()
     for load in loads[2:]:
@@ -120,26 +130,15 @@
     left_ok = jnp.where(gx > 0, 1.0, 0.0).astype(F32)
     right_ok = jnp.where(gx < 15, 1.0, 0.0).astype(F32)
 
+    cot_copies = go([
+        copy(cot_send.at[in_plane(k)], cot_recv.at[gx], cot_sem, k, plane[k]) for k in FAR_FIRST
+    ])
     loads[1].wait()
     lf[0:8] = jnp.zeros((8, 128), F32)
     lf[8 + 18 * WIDE:] = jnp.zeros((8, 128), F32)
     for r in range(8):
         start = 8 + (r + RIM) * WIDE + 16
         lf[start:start + 64] = level_own[r].astype(F32)
-
-    pl.semaphore_wait(barrier, len(peers))
-
-    cot_copies = go([
-        copy(cot_send.at[in_plane(k)], cot_recv.at[gx], cot_sem, k, plane[k]) for k in FAR_FIRST
-    ])
-    src_rows = {-1: slice(0, RIM), 0: slice(0, 8), 1: slice(8 - RIM, 8)}
-    src_cols = {-1: slice(0, 16), 0: slice(0, 64), 1: slice(48, 64)}
-    dst_rows = {-1: slice(RIM + 8, RIM + 8 + RIM), 0: slice(RIM, RIM + 8), 1: slice(0, RIM)}
-    dst_cols = {-1: slice(80, 96), 0: slice(16, 80), 1: slice(0, 16)}
-    e1 = go([
-        copy(level_own.at[src_rows[dy], src_cols[dx]], lp.at[dst_rows[dy], dst_cols[dx]], e1_sem, n, side(dy, dx))
-        for n, (dy, dx) in enumerate(SIDES)
-    ])
 
     loads[2].wait()
     for ky in range(3):
@@ -234,17 +233,20 @@
     def plane_stage(work, buf, sems, first):
         return go([copy(work(in_plane(k)), buf.at[k], sems, first + k, plane[k]) for k in FAR_FIRST])
 
-    def a_piece_of(o):
-        return a_work.at[pl.ds(o * NECK_TILES, NECK_TILES)]
-
     def b_piece_of(o):
         return b_work.at[o]
 
     a_pair[0].wait_recv()
     for n in range(16):
         part = slice(n * NECK_TILES, (n + 1) * NECK_TILES)
-        a_work[part] = (neck_own[part] + a_pair_r[part].astype(F32)).astype(BF16)
-    a_plane = plane_stage(a_piece_of, a_xy, xy_sem, 0)
+        a_work[n // 4, n % 4] = (neck_own[part] + a_pair_r[part].astype(F32)).astype(BF16)
+    x_peer = [None] + [(gy, (x + k) % 4 * 4 + y) for k in range(1, 4)]
+    y_peer = [None] + [(gy, x * 4 + (y + k) % 4) for k in range(1, 4)]
+    near = []
+    for k in (2, 1, 3):
+        near.append(copy(a_work.at[(x + k) % 4, :, 0:ROUTE], near_a.at[k], near_sem, k, x_peer[k]))
+        near.append(copy(a_work.at[:, (y + k) % 4, ROUTE:], near_b.at[k], near_sem, 4 + k, y_peer[k]))
+    go(near)
 
     rows = []
     for r in range(4):
@@ -340,6 +342,21 @@
             total = total + dot(im_b[(4 * q + ky) * WIDE:(4 * q + ky + 4) * WIDE], wlt[ky])
         grad_input[4 * q:4 * q + 4] = total.reshape(4, WIDE, 128)[:, 16:80].astype(BF16)
 
+    for c in near:
+        c.wait_recv()
+    for p in range(4):
+        via_x, via_y = a_work[x, p, 0:ROUTE].astype(F32), a_work[p, y, ROUTE:].astype(F32)
+        for k in range(1, 4):
+            via_x = via_x + near_a[k, p].astype(F32)
+            via_y = via_y + near_b[k, p].astype(F32)
+        near_a[0, p] = via_x.astype(BF16)
+        near_b[0, p] = via_y.astype(BF16)
+    far = []
+    for k in (2, 1, 3):
+        far.append(copy(near_a.at[0, (y + k) % 4], far_a.at[k], far_sem, k, y_peer[k]))
+        far.append(copy(near_b.at[0, (x + k) % 4], far_b.at[k], far_sem, 4 + k, x_peer[k]))
+    go(far)
+
     for c in no_copies:
         c.wait_recv()
     for q in range(4):
@@ -407,7 +424,14 @@
             for k in Z_FAR_FIRST:
                 copy_z(fin.at[0], fin.at[0], zb_sem, offset + k, offset, column((z + k) % 16)).wait_send()
 
-    plane_sum(a_piece_of, a_xy, a_piece_of(gx), a_plane, a_piece)
+    for c in far:
+        c.wait_recv()
+    via_x, via_y = near_a[0, y].astype(F32), near_b[0, x].astype(F32)
+    for k in range(1, 4):
+        via_x = via_x + far_a[k].astype(F32)
+        via_y = via_y + far_b[k].astype(F32)
+    a_piece[0:ROUTE] = via_x.astype(BF16)
+    a_piece[ROUTE:] = via_y.astype(BF16)
     a_zs = z_send(a_piece, a_z, NECK_TILES, 0, z_sem, 0)
     start_all(a_zs)
     plane_sum(b_piece_of, b_xy, b_piece_of(gx), b_plane, b_piece)
@@ -417,31 +441,54 @@
     z_sum(b_piece, b_z, b_fin, REST_TILES, NECK_TILES, z_sem, 16, jnp.where(z < NECK_TILES + 2, scales[0], scales[1]))
 
     z_back(a_fin, NECK_TILES, 0, 0)
-    def a_slot(o):
-        return a_all.at[core, pl.ds(o * NECK_TILES, NECK_TILES)]
-
     def b_slot(o):
         return b_all.at[core, o]
 
-    a_all[core, pl.ds(gx * NECK_TILES, NECK_TILES)] = a_fin[...]
-    a_mine = a_slot(gx)
-    a_back = go([copy(a_mine, a_mine, xyb_sem, k, plane[k]) for k in FAR_FIRST])
+    a_all[core, x, y] = a_fin[...]
+    leg1 = []
+    for k in (2, 1, 3):
+        mine_x, mine_y = a_all.at[core, x, y, 0:ROUTE], a_all.at[core, x, y, ROUTE:]
+        leg1.append(copy(mine_x, mine_x, back1_sem, k, y_peer[k]))
+        leg1.append(copy(mine_y, mine_y, back1_sem, 4 + k, x_peer[k]))
+    go(leg1)
     z_back(b_fin, REST_TILES, NECK_TILES, 16)
     b_all[core, gx] = b_fin[...]
-    b_mine = b_all.at[core, gx]
-    b_back = go([copy(b_mine, b_mine, xyb_sem, 16 + k, plane[k]) for k in FAR_FIRST])
-
-    def landed(slot_of, sems, first):
-        for k in range(1, 16):
-            slot = slot_of(in_plane(k, -1))
-            copy(slot, slot, sems, first + k, plane[k]).wait_recv()
-
-    landed(a_slot, xyb_sem, 0)
-    go([copy(a_all.at[core], a_all.at[core], pair_sem, 2, pair_dev)])
-    landed(b_slot, xyb_sem, 16)
+    b_mine = b_slot(gx)
+    go([copy(b_mine, b_mine, xyb_sem, 16 + k, plane[k]) for k in FAR_FIRST])
+    for c in leg1:
+        c.wait_recv()
+
+    def block_x(c, xx):
+        return a_all.at[c, xx, :, 0:ROUTE]
+
+    def block_y(c, yy):
+        return a_all.at[c, :, yy, ROUTE:]
+
+    leg2 = []
+    for k in (2, 1, 3):
+        leg2.append(copy(block_x(core, x), block_x(core, x), back2_sem, k, x_peer[k]))
+        leg2.append(copy(block_y(core, y), block_y(core, y), back2_sem, 4 + k, y_peer[k]))
+    go(leg2)
+
+    def swap(k):
+        bx, by = block_x(core, (x - k + 4) % 4), block_y(core, (y - k + 4) % 4)
+        go([copy(bx, bx, pair_sem, 4 + k, pair_dev), copy(by, by, pair_sem, 8 + k, pair_dev)])
+
+    swap(0)
+    for k in FAR_FIRST:
+        slot = b_slot(in_plane(k, -1))
+        copy(slot, slot, xyb_sem, 16 + k, plane[k]).wait_recv()
     go([copy(b_all.at[core], b_all.at[core], pair_sem, 3, pair_dev)])
-    copy(a_all.at[other], a_all.at[other], pair_sem, 2, pair_dev).wait_recv()
+    for k in (1, 3, 2):
+        bx, by = block_x(core, (x - k + 4) % 4), block_y(core, (y - k + 4) % 4)
+        copy(bx, bx, back2_sem, k, x_peer[k]).wait_recv()
+        copy(by, by, back2_sem, 4 + k, y_peer[k]).wait_recv()
+        swap(k)
     copy(b_all.at[other], b_all.at[other], pair_sem, 3, pair_dev).wait_recv()
+    for k in range(4):
+        bx, by = block_x(other, (x - k + 4) % 4), block_y(other, (y - k + 4) % 4)
+        copy(bx, bx, pair_sem, 4 + k, pair_dev).wait_recv()
+        copy(by, by, pair_sem, 8 + k, pair_dev).wait_recv()
 
     for c in sent:
         c.wait_send()
@@ -455,7 +502,7 @@
     copies = [(strip, neck_out), (level, grad_input)]
     for half in range(2):
         lanes = slice(128 * half, 128 * half + 128)
-        copies.append((a_all.at[half], grad_neck.at[:, :, lanes]))
+        copies.append((a_all.at[half], grad_neck.at[:, :, :, :, lanes]))
         copies.append((b_all.at[half, :, 0:2], grad_down.at[:, :, :, lanes]))
         copies.append((b_all.at[half, 0:LEVEL_OWNERS, 2:5], grad_level.at[half]))
     copies = [pltpu.make_async_copy(src, dst, sems.at[n]) for n, (src, dst) in enumerate(copies)]
@@ -477,18 +524,12 @@
     def v(*shape, dtype=BF16):
         return pltpu.VMEM(shape, dtype)
 
-    def group(tiles, flat):
-        whole = (16 * tiles, 16, 128) if flat else (16, tiles, 16, 128)
-        return [
-            v(*whole), v(*whole), v(*whole), v(16, tiles, 16, 128), v(tiles, 16, 128), v(16, 16, 128), v(tiles, 16, 128),
-        ]
-
     outs = pl.pallas_call(
         functools.partial(kernel, (neck_scale, level_scale)),
         out_shape=[
             jax.ShapeDtypeStruct((4, 16, 512), BF16),
             jax.ShapeDtypeStruct((8, 64, 128), BF16),
-            jax.ShapeDtypeStruct((2, 16 * NECK_TILES, 16, 128), BF16),
+            jax.ShapeDtypeStruct((2, 4, 4, NECK_TILES, 16, 128), BF16),
             jax.ShapeDtypeStruct((2, 16, REST_TILES, 16, 128), BF16),
         ],
         in_specs=[hbm] * 5,
@@ -505,9 +546,14 @@
             v(16, 2, 16, 128), v(16, 2, 16, 128), v(2, NARROW, 256), v(2, NARROW, 256),
             v(16, 16, 128), v(16, 16, 128),
             v(144, 16, 128, dtype=F32), v(1152, 128, dtype=F32), v(512, 256, dtype=F32),
-            *group(NECK_TILES, True), *group(REST_TILES, False),
+            v(16 * NECK_TILES, 16, 128), v(16 * NECK_TILES, 16, 128), v(4, 4, NECK_TILES, 16, 128),
+            v(4, 4, ROUTE, 16, 128), v(4, 4, NECK_TILES - ROUTE, 16, 128),
+            v(4, ROUTE, 16, 128), v(4, NECK_TILES - ROUTE, 16, 128),
+            v(NECK_TILES, 16, 128), v(16, 16, 128), v(NECK_TILES, 16, 128),
+            v(16, REST_TILES, 16, 128), v(16, REST_TILES, 16, 128), v(16, REST_TILES, 16, 128), v(16, REST_TILES, 16, 128),
+            v(REST_TILES, 16, 128), v(16, 16, 128), v(REST_TILES, 16, 128),
             dma((5,)), dma((2, 8)), dma((2, 16)), dma((2, 8)), dma((2, 16)), dma((2, 8)),
-            dma((2, 4)), dma((2, 32)), dma((2, 32)), dma((2, 32)), dma((2, 32)),
+            dma((2, 12)), dma((2, 32)), dma((2, 32)), dma((2, 32)), dma((2, 32)), dma((2, 8)), dma((2, 8)), dma((2, 8)), dma((2, 8)),
         ],
         compiler_params=pltpu.CompilerParams(
             collective_id=0, has_side_effects=True, vmem_limit_bytes=24 * 1024 * 1024
@@ -528,7 +574,7 @@
             jax.ShapeDtypeStruct((8, 64, 128), BF16),
             jax.ShapeDtypeStruct((2, LEVEL_OWNERS, 3, 16, 128), BF16),
             jax.ShapeDtypeStruct((16, 2, 16, 256), BF16),
-            jax.ShapeDtypeStruct((144, 16, 256), BF16),
+            jax.ShapeDtypeStruct((4, 4, NECK_TILES, 16, 256), BF16),
         ],
         in_specs=[vmem] * 4,
         out_specs=[hbm] * 5,

time: 76.4 us -> 75.7 us (level)
  no operation moved by 1% of the time
where the time goes in v5:
time: 75.7 us; the launch traced here: 75.2 us
  Pallas kernels  74.5 us (98%)
    pallas_call x1, Pallas kernels, local(): pl.pallas_call(functools.partial(kernel, (neck_scale, level_scale)), out_...  73.2 us

profile of v5, /device:TPU:1, one launch (start us, length us, event | category | flops | bytes accessed | tf_op | source)
XLA Modules:
  0.0 75.2 jit_solution(2372031496889351862)
XLA Ops:
  0.6 73.2 %shard_map.92 = (bf16[4,16,512]{2,1,0:T(8,128)(2,1)S(1)}, bf16[8,64,128]{2,1,0:T(8,128)(2,1)S(1)}, bf16[2,4,4,9,16,128]{5,4,3,2,1,0:T(8,128)(2,1)S(1)}, bf16[2,16,5,16,128]{4,3,2,1,0:T(8,128)(2,1)S(1)}) custom-call(bf16[8,64,128]{2,1,0:T(8,128)(2,1)} %level_in.1, bf16[3,384,128]{2,1,0:T(8,128)(2,1)} %bitcast.9, bf16[512,256]{1,0:T(8,128)(2,1)} %bitcast.10, ...), custom_call_target="tpu_custom_call" | custom-call | tf_op jit(solution)/shard_map/pallas_call | solution.py:527
  73.8 1.3 %shard_map.93 = (bf16[4,16,512]{2,1,0:T(8,128)(2,1)}, bf16[8,64,128]{2,1,0:T(8,128)(2,1)}, bf16[2,12,3,16,128]{4,3,2,1,0:T(8,128)(2,1)}, bf16[16,2,16,256]{3,2,1,0:T(8,128)(2,1)}, bf16[4,4,9,16,256]{4,3,2,1,0:T(8,128)(2,1)}) custom-call(bf16[4,16,512]{2,1,0:T(8,128)(2,1)S(1)} %get-tuple-element.14.strip, bf16[8,64,128]{2,1,0:T(8,128)(2,1)S(1)} %get-tuple-element.15.level, ...), custom_call_target="tpu_custom_call" | custom-call | tf_op jit(solution)/shard_map/pallas_call | solution.py:570

commit v6 on v5

--- a/solution.py
+++ b/solution.py
@@ -51,7 +51,7 @@
     a_pair_s, a_pair_r, a_work, near_a, near_b, far_a, far_b, a_piece, a_z, a_fin,
     b_pair_s, b_pair_r, b_work, b_xy, b_piece, b_z, b_fin,
     w_sem, e1_sem, cot_sem, ch_sem, no_sem, e4_sem,
-    pair_sem, xy_sem, z_sem, zb_sem, xyb_sem, near_sem, far_sem, back1_sem, back2_sem,
+    pair_sem, xy_sem, z_sem, zb_sem, xyb_sem, near_sem, far_sem, back1_sem, back2_sem, known,
 ):
     gy, gx = lax.axis_index("gy"), lax.axis_index("gx")
     z, core = gy // 2, gy % 2
@@ -81,7 +81,9 @@
     for load in loads[:2]:
         load.start()
     barrier = pltpu.get_barrier_semaphore()
-    peers = plane[1:] + [column((z + k) % 16) for k in range(1, 16)] + [side(dy, dx) for dy, dx in SIDES if dy != 0]
+    x_peer = [None] + [(gy, (x + k) % 4 * 4 + y) for k in range(1, 4)]
+    y_peer = [None] + [(gy, x * 4 + (y + k) % 4) for k in range(1, 4)]
+    peers = x_peer[1:] + y_peer[1:] + [side(dy, dx) for dy, dx in SIDES]
     for peer in peers:
         pl.semaphore_signal(barrier, inc=1, device_id=peer, device_id_type=MESH)
 
@@ -100,6 +102,12 @@
         return copies
 
     pl.semaphore_wait(barrier, len(peers))
+    def tell(n):
+        for dy in (-1, 1):
+            pl.semaphore_signal(known.at[n], inc=1, device_id=side(dy * 2 ** n, 0), device_id_type=MESH)
+
+    for k in range(1, 4):
+        pl.semaphore_signal(known.at[4], inc=1, device_id=y_peer[k], device_id_type=MESH)
     src_rows = {-1: slice(0, RIM), 0: slice(0, 8), 1: slice(8 - RIM, 8)}
     src_cols = {-1: slice(0, 16), 0: slice(0, 64), 1: slice(48, 64)}
     dst_rows = {-1: slice(RIM + 8, RIM + 8 + RIM), 0: slice(RIM, RIM + 8), 1: slice(0, RIM)}
@@ -109,6 +117,7 @@
         for n, (dy, dx) in enumerate(SIDES)
     ])
 
+    tell(0)
     loads[0].wait()
     for load in loads[2:]:
         load.start()
@@ -130,6 +139,7 @@
     left_ok = jnp.where(gx > 0, 1.0, 0.0).astype(F32)
     right_ok = jnp.where(gx < 15, 1.0, 0.0).astype(F32)
 
+    pl.semaphore_wait(known.at[4], 3)
     cot_copies = go([
         copy(cot_send.at[in_plane(k)], cot_recv.at[gx], cot_sem, k, plane[k]) for k in FAR_FIRST
     ])
@@ -139,6 +149,9 @@
     for r in range(8):
         start = 8 + (r + RIM) * WIDE + 16
         lf[start:start + 64] = level_own[r].astype(F32)
+
+    pl.semaphore_wait(known.at[0], 2)
+    tell(1)
 
     loads[2].wait()
     for ky in range(3):
@@ -158,6 +171,9 @@
     ct[0] = cf[NARROW:2 * NARROW].astype(BF16)
     ct[1] = cf[4 * NARROW:5 * NARROW].astype(BF16)
     ch = go([copy(ct.at[n], hr.at[n], ch_sem, n, side(2 * n - 1, 0)) for n in range(2)])
+
+    pl.semaphore_wait(known.at[1], 2)
+    tell(2)
 
     for c in e1:
         c.wait_recv()
@@ -226,6 +242,8 @@
         part = dot_tn(im_n[(1 + ky) * NARROW:(5 + ky) * NARROW], theirs)
         a_pair_s[48 * ky:48 * ky + 48] = part.astype(BF16).reshape(48, 16, 128)
     a_pair = go([copy(a_pair_s, a_pair_r, pair_sem, 0, pair_dev)])
+    pl.semaphore_wait(known.at[2], 2)
+    tell(3)
     mine = gate_own[:, half_lanes(core)]
     for ky in range(3):
         neck_own[48 * ky:48 * ky + 48] = dot_tn(im_n[(1 + ky) * NARROW:(5 + ky) * NARROW], mine).reshape(48, 16, 128)
@@ -240,8 +258,6 @@
     for n in range(16):
         part = slice(n * NECK_TILES, (n + 1) * NECK_TILES)
         a_work[n // 4, n % 4] = (neck_own[part] + a_pair_r[part].astype(F32)).astype(BF16)
-    x_peer = [None] + [(gy, (x + k) % 4 * 4 + y) for k in range(1, 4)]
-    y_peer = [None] + [(gy, x * 4 + (y + k) % 4) for k in range(1, 4)]
     near = []
     for k in (2, 1, 3):
         near.append(copy(a_work.at[(x + k) % 4, :, 0:ROUTE], near_a.at[k], near_sem, k, x_peer[k]))
@@ -367,6 +383,8 @@
                 part = pltpu.roll(pieces[j], (32 * (j - r)) % 128, 1) if r != j else pieces[j]
                 out = jnp.where(lane < 32 * (j + 1), part, out)
             neck_out[r, :, 128 * q:128 * q + 128] = out.astype(BF16)
+
+    pl.semaphore_wait(known.at[3], 2)
 
     def z_send(piece, buf, tiles, first, sems, offset):
         copies = []
@@ -554,6 +572,7 @@
             v(REST_TILES, 16, 128), v(16, 16, 128), v(REST_TILES, 16, 128),
             dma((5,)), dma((2, 8)), dma((2, 16)), dma((2, 8)), dma((2, 16)), dma((2, 8)),
             dma((2, 12)), dma((2, 32)), dma((2, 32)), dma((2, 32)), dma((2, 32)), dma((2, 8)), dma((2, 8)), dma((2, 8)), dma((2, 8)),
+            pltpu.SemaphoreType.REGULAR((5,)),
         ],
         compiler_params=pltpu.CompilerParams(
             collective_id=0, has_side_effects=True, vmem_limit_bytes=24 * 1024 * 1024

time: 75.7 us -> 71.5 us (0.945)
  Pallas kernels: 74.5 us -> 70.4 us
    pallas_call x1, Pallas kernels: 73.2 us -> 69.1 us  [local(): pl.pallas_call(functools.partial(kernel, (neck_scale, level_scale)), out_...]
where the time goes in v6:
time: 71.5 us; the launch traced here: 71 us
  Pallas kernels  70.4 us (98%)
    pallas_call x1, Pallas kernels, local(): pl.pallas_call(functools.partial(kernel, (neck_scale, level_scale)), out_...  69.1 us

profile of v6, /device:TPU:1, one launch (start us, length us, event | category | flops | bytes accessed | tf_op | source)
XLA Modules:
  0.0 71.0 jit_solution(10679061378951547834)
XLA Ops:
  0.6 69.1 %shard_map.92 = (bf16[4,16,512]{2,1,0:T(8,128)(2,1)S(1)}, bf16[8,64,128]{2,1,0:T(8,128)(2,1)S(1)}, bf16[2,4,4,9,16,128]{5,4,3,2,1,0:T(8,128)(2,1)S(1)}, bf16[2,16,5,16,128]{4,3,2,1,0:T(8,128)(2,1)S(1)}) custom-call(bf16[8,64,128]{2,1,0:T(8,128)(2,1)} %level_in.1, bf16[3,384,128]{2,1,0:T(8,128)(2,1)} %bitcast.9, bf16[512,256]{1,0:T(8,128)(2,1)} %bitcast.10, ...), custom_call_target="tpu_custom_call" | custom-call | tf_op jit(solution)/shard_map/pallas_call | solution.py:545
  69.7 1.3 %shard_map.93 = (bf16[4,16,512]{2,1,0:T(8,128)(2,1)}, bf16[8,64,128]{2,1,0:T(8,128)(2,1)}, bf16[2,12,3,16,128]{4,3,2,1,0:T(8,128)(2,1)}, bf16[16,2,16,256]{3,2,1,0:T(8,128)(2,1)}, bf16[4,4,9,16,256]{4,3,2,1,0:T(8,128)(2,1)}) custom-call(bf16[4,16,512]{2,1,0:T(8,128)(2,1)S(1)} %get-tuple-element.14.strip, bf16[8,64,128]{2,1,0:T(8,128)(2,1)S(1)} %get-tuple-element.15.level, ...), custom_call_target="tpu_custom_call" | custom-call | tf_op jit(solution)/shard_map/pallas_call | solution.py:589

commit v7 on v6

--- a/solution.py
+++ b/solution.py
@@ -264,14 +264,6 @@
         near.append(copy(a_work.at[:, (y + k) % 4, ROUTE:], near_b.at[k], near_sem, 4 + k, y_peer[k]))
     go(near)
 
-    rows = []
-    for r in range(4):
-        v = neck_pre[(r + 1) * NARROW + 8:(r + 1) * NARROW + 40]
-        rows.append(nf[8 + (r + 2) * NARROW + 8:8 + (r + 2) * NARROW + 40] + v * jax.nn.sigmoid(v))
-    no_send[...] = jnp.concatenate(rows, axis=0).T.astype(BF16).reshape(16, 16, 128)
-    no_recv[gx] = no_send[gx]
-    no_copies = go([copy(no_send.at[in_plane(k)], no_recv.at[gx], no_sem, k, plane[k]) for k in FAR_FIRST])
-
     for c in ch:
         c.wait_recv()
     for n, ok, rows in ((1, top_ok, slice(0, NARROW)), (0, bottom_ok, slice(5 * NARROW, 6 * NARROW))):
@@ -300,6 +292,33 @@
     for r in range(8):
         rows_r = slice(r * WIDE + 16, r * WIDE + 80)
         gp[r + 1, 16:80] = (lbf[rows_r] * slope_of(pre_l[rows_r])).astype(BF16)
+    own_gate = gp[1:9, 16:80].reshape(512, 128)
+    for ky in range(3):
+        window = jnp.concatenate(
+            [im_l[(4 + ky + r) * WIDE + 16:(4 + ky + r) * WIDE + 80] for r in range(8)], axis=0
+        )
+        level_acc[ky * 384:(ky + 1) * 384] = dot_tn(window, own_gate)
+    down_acc[...] = dot_tn(dn[2 * NARROW:6 * NARROW], ng[...])
+
+    def rest_terms(half):
+        down = down_acc[:, half_lanes(half)].reshape(16, 2, 16, 128)
+        level = level_acc[pl.ds(pl.multiple_of(half * 576, 576), 576), :].reshape(LEVEL_OWNERS, 3, 16, 128)
+        return down, level
+
+    down, level = rest_terms(other)
+    nothing = jnp.zeros((16 - LEVEL_OWNERS, 3, 16, 128), BF16)
+    b_pair_s[:, 0:2] = down.astype(BF16)
+    b_pair_s[0:LEVEL_OWNERS, 2:5] = level.astype(BF16)
+    b_pair_s[LEVEL_OWNERS:, 2:5] = nothing
+    b_pair = go([copy(b_pair_s, b_pair_r, pair_sem, 1, pair_dev)])
+
+    b_pair[0].wait_recv()
+    down, level = rest_terms(core)
+    b_work[:, 0:2] = (down + b_pair_r[:, 0:2].astype(F32)).astype(BF16)
+    b_work[0:LEVEL_OWNERS, 2:5] = (level + b_pair_r[0:LEVEL_OWNERS, 2:5].astype(F32)).astype(BF16)
+    b_work[LEVEL_OWNERS:, 2:5] = nothing
+    b_plane = plane_stage(b_piece_of, b_xy, xy_sem, 16)
+
     e4_src = {-1: slice(1, 2), 0: slice(1, 9), 1: slice(8, 9)}
     e4_dst = {-1: slice(9, 10), 0: slice(1, 9), 1: slice(0, 1)}
     e4_scol = {-1: slice(16, 32), 0: slice(16, 80), 1: slice(64, 80)}
@@ -308,33 +327,101 @@
         for n, (dy, dx) in enumerate(SIDES)
     ])
 
-    own_gate = gp[1:9, 16:80].reshape(512, 128)
-    for ky in range(3):
-        window = jnp.concatenate(
-            [im_l[(4 + ky + r) * WIDE + 16:(4 + ky + r) * WIDE + 80] for r in range(8)], axis=0
+    for c in near:
+        c.wait_recv()
+    for p in range(4):
+        via_x, via_y = a_work[x, p, 0:ROUTE].astype(F32), a_work[p, y, ROUTE:].astype(F32)
+        for k in range(1, 4):
+            via_x = via_x + near_a[k, p].astype(F32)
+            via_y = via_y + near_b[k, p].astype(F32)
+        near_a[0, p] = via_x.astype(BF16)
+        near_b[0, p] = via_y.astype(BF16)
+    far = []
+    for k in (2, 1, 3):
+        far.append(copy(near_a.at[0, (y + k) % 4], far_a.at[k], far_sem, k, y_peer[k]))
+        far.append(copy(near_b.at[0, (x + k) % 4], far_b.at[k], far_sem, 4 + k, x_peer[k]))
+    go(far)
+
+    rows = []
+    for r in range(4):
+        v = neck_pre[(r + 1) * NARROW + 8:(r + 1) * NARROW + 40]
+        rows.append(nf[8 + (r + 2) * NARROW + 8:8 + (r + 2) * NARROW + 40] + v * jax.nn.sigmoid(v))
+    no_send[...] = jnp.concatenate(rows, axis=0).T.astype(BF16).reshape(16, 16, 128)
+    no_recv[gx] = no_send[gx]
+    no_copies = go([copy(no_send.at[in_plane(k)], no_recv.at[gx], no_sem, k, plane[k]) for k in FAR_FIRST])
+
+    pl.semaphore_wait(known.at[3], 2)
+
+    def z_send(piece, buf, tiles, first, sems, offset):
+        copies = []
+        for k in Z_FAR_FIRST:
+            t = (z + k) % 16 - first
+            c = copy_z(piece.at[t], buf.at[z], sems, offset + k, offset + z, column((z + k) % 16))
+            copies.append(((t >= 0) & (t < tiles), c))
+        return copies
+
+    def copy_z(src, dst, sems, ks, kr, dev):
+        return pltpu.make_async_remote_copy(
+            src_ref=src, dst_ref=dst, send_sem=sems.at[0, ks], recv_sem=sems.at[1, kr],
+            device_id=dev, device_id_type=MESH,
         )
-        level_acc[ky * 384:(ky + 1) * 384] = dot_tn(window, own_gate)
-    down_acc[...] = dot_tn(dn[2 * NARROW:6 * NARROW], ng[...])
-
-    def rest_terms(half):
-        down = down_acc[:, half_lanes(half)].reshape(16, 2, 16, 128)
-        level = level_acc[pl.ds(pl.multiple_of(half * 576, 576), 576), :].reshape(LEVEL_OWNERS, 3, 16, 128)
-        return down, level
-
-    down, level = rest_terms(other)
-    nothing = jnp.zeros((16 - LEVEL_OWNERS, 3, 16, 128), BF16)
-    b_pair_s[:, 0:2] = down.astype(BF16)
-    b_pair_s[0:LEVEL_OWNERS, 2:5] = level.astype(BF16)
-    b_pair_s[LEVEL_OWNERS:, 2:5] = nothing
-    b_pair = go([copy(b_pair_s, b_pair_r, pair_sem, 1, pair_dev)])
-
-    b_pair[0].wait_recv()
-    down, level = rest_terms(core)
-    b_work[:, 0:2] = (down + b_pair_r[:, 0:2].astype(F32)).astype(BF16)
-    b_work[0:LEVEL_OWNERS, 2:5] = (level + b_pair_r[0:LEVEL_OWNERS, 2:5].astype(F32)).astype(BF16)
-    b_work[LEVEL_OWNERS:, 2:5] = nothing
-    b_plane = plane_stage(b_piece_of, b_xy, xy_sem, 16)
-
+
+    def start_all(copies):
+        for cond, c in copies:
+            pl.when(cond)(c.start)
+
+    def plane_sum(piece_of, buf, own_ref, copies, out):
+        for c in copies:
+            c.wait_recv()
+        total = own_ref[...].astype(F32)
+        for k in range(1, 16):
+            total = total + buf[k].astype(F32)
+        out[...] = total.astype(BF16)
+
+    def owns(first, tiles):
+        return (z >= first) & (z < first + tiles)
+
+    def z_sum(piece, buf, fin, tiles, first, sems, offset, scale):
+        @pl.when(owns(first, tiles))
+        def _():
+            mine = z - first
+            for s in range(16):
+                @pl.when(z != s)
+                def _(s=s):
+                    copy_z(piece.at[0], buf.at[s], sems, offset, offset + s, column(s)).wait_recv()
+            buf[z] = piece[mine]
+            total = buf[0].astype(F32)
+            for s in range(1, 16):
+                total = total + buf[s].astype(F32)
+            fin[mine] = (total * scale).astype(BF16)
+            for k in Z_FAR_FIRST:
+                copy_z(fin.at[mine], fin.at[mine], zb_sem, offset + k, offset + mine, column((z + k) % 16)).start()
+
+    def z_back(fin, tiles, first, offset):
+        for t in range(tiles):
+            @pl.when(z != first + t)
+            def _(t=t):
+                copy_z(fin.at[t], fin.at[t], zb_sem, offset, offset + t, column(first + t)).wait_recv()
+
+    def z_back_sent(fin, tiles, first, offset):
+        @pl.when(owns(first, tiles))
+        def _():
+            for k in Z_FAR_FIRST:
+                copy_z(fin.at[0], fin.at[0], zb_sem, offset + k, offset, column((z + k) % 16)).wait_send()
+
+    for c in far:
+        c.wait_recv()
+    via_x, via_y = near_a[0, y].astype(F32), near_b[0, x].astype(F32)
+    for k in range(1, 4):
+        via_x = via_x + far_a[k].astype(F32)
+        via_y = via_y + far_b[k].astype(F32)
+    a_piece[0:ROUTE] = via_x.astype(BF16)
+    a_piece[ROUTE:] = via_y.astype(BF16)
+    a_zs = z_send(a_piece, a_z, NECK_TILES, 0, z_sem, 0)
+    start_all(a_zs)
+    plane_sum(b_piece_of, b_xy, b_piece_of(gx), b_plane, b_piece)
+    b_zs = z_send(b_piece, b_z, REST_TILES, NECK_TILES, z_sem, 16)
+    start_all(b_zs)
     for c in e4:
         c.wait_recv()
     g2f[0:8] = jnp.zeros((8, 128), F32)
@@ -358,21 +445,6 @@
             total = total + dot(im_b[(4 * q + ky) * WIDE:(4 * q + ky + 4) * WIDE], wlt[ky])
         grad_input[4 * q:4 * q + 4] = total.reshape(4, WIDE, 128)[:, 16:80].astype(BF16)
 
-    for c in near:
-        c.wait_recv()
-    for p in range(4):
-        via_x, via_y = a_work[x, p, 0:ROUTE].astype(F32), a_work[p, y, ROUTE:].astype(F32)
-        for k in range(1, 4):
-            via_x = via_x + near_a[k, p].astype(F32)
-            via_y = via_y + near_b[k, p].astype(F32)
-        near_a[0, p] = via_x.astype(BF16)
-        near_b[0, p] = via_y.astype(BF16)
-    far = []
-    for k in (2, 1, 3):
-        far.append(copy(near_a.at[0, (y + k) % 4], far_a.at[k], far_sem, k, y_peer[k]))
-        far.append(copy(near_b.at[0, (x + k) % 4], far_b.at[k], far_sem, 4 + k, x_peer[k]))
-    go(far)
-
     for c in no_copies:
         c.wait_recv()
     for q in range(4):
@@ -384,77 +456,6 @@
                 out = jnp.where(lane < 32 * (j + 1), part, out)
             neck_out[r, :, 128 * q:128 * q + 128] = out.astype(BF16)
 
-    pl.semaphore_wait(known.at[3], 2)
-
-    def z_send(piece, buf, tiles, first, sems, offset):
-        copies = []
-        for t in range(tiles):
-            c = copy_z(piece.at[t], buf.at[z], sems, offset + t, offset + z, column(first + t))
-            copies.append((z != first + t, c))
-        return copies
-
-    def copy_z(src, dst, sems, ks, kr, dev):
-        return pltpu.make_async_remote_copy(
-            src_ref=src, dst_ref=dst, send_sem=sems.at[0, ks], recv_sem=sems.at[1, kr],
-            device_id=dev, device_id_type=MESH,
-        )
-
-    def start_all(copies):
-        for cond, c in copies:
-            pl.when(cond)(c.start)
-
-    def plane_sum(piece_of, buf, own_ref, copies, out):
-        for c in copies:
-            c.wait_recv()
-        total = own_ref[...].astype(F32)
-        for k in range(1, 16):
-            total = total + buf[k].astype(F32)
-        out[...] = total.astype(BF16)
-
-    def owns(first, tiles):
-        return (z >= first) & (z < first + tiles)
-
-    def z_sum(piece, buf, fin, tiles, first, sems, offset, scale):
-        @pl.when(owns(first, tiles))
-        def _():
-            mine = z - first
-            for s in range(16):
-                @pl.when(z != s)
-                def _(s=s):
-                    copy_z(piece.at[0], buf.at[s], sems, offset, offset + s, column(s)).wait_recv()
-            buf[z] = piece[mine]
-            total = buf[0].astype(F32)
-            for s in range(1, 16):
-                total = total + buf[s].astype(F32)
-            fin[mine] = (total * scale).astype(BF16)
-            for k in Z_FAR_FIRST:
-                copy_z(fin.at[mine], fin.at[mine], zb_sem, offset + k, offset + mine, column((z + k) % 16)).start()
-
-    def z_back(fin, tiles, first, offset):
-        for t in range(tiles):
-            @pl.when(z != first + t)
-            def _(t=t):
-                copy_z(fin.at[t], fin.at[t], zb_sem, offset, offset + t, column(first + t)).wait_recv()
-
-    def z_back_sent(fin, tiles, first, offset):
-        @pl.when(owns(first, tiles))
-        def _():
-            for k in Z_FAR_FIRST:
-                copy_z(fin.at[0], fin.at[0], zb_sem, offset + k, offset, column((z + k) % 16)).wait_send()
-
-    for c in far:
-        c.wait_recv()
-    via_x, via_y = near_a[0, y].astype(F32), near_b[0, x].astype(F32)
-    for k in range(1, 4):
-        via_x = via_x + far_a[k].astype(F32)
-        via_y = via_y + far_b[k].astype(F32)
-    a_piece[0:ROUTE] = via_x.astype(BF16)
-    a_piece[ROUTE:] = via_y.astype(BF16)
-    a_zs = z_send(a_piece, a_z, NECK_TILES, 0, z_sem, 0)
-    start_all(a_zs)
-    plane_sum(b_piece_of, b_xy, b_piece_of(gx), b_plane, b_piece)
-    b_zs = z_send(b_piece, b_z, REST_TILES, NECK_TILES, z_sem, 16)
-    start_all(b_zs)
     z_sum(a_piece, a_z, a_fin, NECK_TILES, 0, z_sem, 0, scales[0])
     z_sum(b_piece, b_z, b_fin, REST_TILES, NECK_TILES, z_sem, 16, jnp.where(z < NECK_TILES + 2, scales[0], scales[1]))
 

time: 71.5 us -> 69.8 us (0.976)
  Pallas kernels: 70.4 us -> 69 us
    pallas_call x1, Pallas kernels: 69.1 us -> 67.7 us  [local(): pl.pallas_call(functools.partial(kernel, (neck_scale, level_scale)), out_...]
where the time goes in v7:
time: 69.8 us; the launch traced here: 69.7 us
  Pallas kernels  69 us (99%)
    pallas_call x1, Pallas kernels, local(): pl.pallas_call(functools.partial(kernel, (neck_scale, level_scale)), out_...  67.7 us

profile of v7, /device:TPU:1, one launch (start us, length us, event | category | flops | bytes accessed | tf_op | source)
XLA Modules:
  0.0 69.7 jit_solution(5494834614045903124)
XLA Ops:
  0.6 67.7 %shard_map.92 = (bf16[4,16,512]{2,1,0:T(8,128)(2,1)S(1)}, bf16[8,64,128]{2,1,0:T(8,128)(2,1)S(1)}, bf16[2,4,4,9,16,128]{5,4,3,2,1,0:T(8,128)(2,1)S(1)}, bf16[2,16,5,16,128]{4,3,2,1,0:T(8,128)(2,1)S(1)}) custom-call(bf16[8,64,128]{2,1,0:T(8,128)(2,1)} %level_in.1, bf16[3,384,128]{2,1,0:T(8,128)(2,1)} %bitcast.9, bf16[512,256]{1,0:T(8,128)(2,1)} %bitcast.10, ...), custom_call_target="tpu_custom_call" | custom-call | tf_op jit(solution)/shard_map/pallas_call | solution.py:546
  68.4 1.3 %shard_map.93 = (bf16[4,16,512]{2,1,0:T(8,128)(2,1)}, bf16[8,64,128]{2,1,0:T(8,128)(2,1)}, bf16[2,12,3,16,128]{4,3,2,1,0:T(8,128)(2,1)}, bf16[16,2,16,256]{3,2,1,0:T(8,128)(2,1)}, bf16[4,4,9,16,256]{4,3,2,1,0:T(8,128)(2,1)}) custom-call(bf16[4,16,512]{2,1,0:T(8,128)(2,1)S(1)} %get-tuple-element.14.strip, bf16[8,64,128]{2,1,0:T(8,128)(2,1)S(1)} %get-tuple-element.15.level, ...), custom_call_target="tpu_custom_call" | custom-call | tf_op jit(solution)/shard_map/pallas_call | solution.py:590

commit v8 on v7

--- a/solution.py
+++ b/solution.py
@@ -106,17 +106,16 @@
         for dy in (-1, 1):
             pl.semaphore_signal(known.at[n], inc=1, device_id=side(dy * 2 ** n, 0), device_id_type=MESH)
 
-    for k in range(1, 4):
-        pl.semaphore_signal(known.at[4], inc=1, device_id=y_peer[k], device_id_type=MESH)
     src_rows = {-1: slice(0, RIM), 0: slice(0, 8), 1: slice(8 - RIM, 8)}
     src_cols = {-1: slice(0, 16), 0: slice(0, 64), 1: slice(48, 64)}
     dst_rows = {-1: slice(RIM + 8, RIM + 8 + RIM), 0: slice(RIM, RIM + 8), 1: slice(0, RIM)}
     dst_cols = {-1: slice(80, 96), 0: slice(16, 80), 1: slice(0, 16)}
     e1 = go([
         copy(level_in.at[src_rows[dy], src_cols[dx]], lp.at[dst_rows[dy], dst_cols[dx]], e1_sem, n, side(dy, dx))
-        for n, (dy, dx) in enumerate(SIDES)
+        for n, (dy, dx) in sorted(enumerate(SIDES), key=lambda e: -abs(e[1][0]) - abs(e[1][1]))
     ])
-
+    for k in range(1, 4):
+        pl.semaphore_signal(known.at[4], inc=1, device_id=y_peer[k], device_id_type=MESH)
     tell(0)
     loads[0].wait()
     for load in loads[2:]:
@@ -159,24 +158,10 @@
             w = wl[2 - ky, (2 - kx) * 128:(3 - kx) * 128, :].astype(F32)
             wlt[ky, kx * 128:(kx + 1) * 128, :] = w.T.astype(BF16)
 
-    for c in cot_copies:
-        c.wait_recv()
-    cot_tile = cot_recv[:, 0].reshape(256, 128).astype(F32).T
-    cot_beside = cot_recv[:, 1].reshape(256, 128).astype(F32).T
-    for r in range(4):
-        base = (r + 1) * NARROW
-        cf[base:base + 8] = cot_beside[32 * r + 24:32 * r + 32] * left_ok
-        cf[base + 8:base + 40] = cot_tile[32 * r:32 * r + 32]
-        cf[base + 40:base + 48] = cot_beside[32 * r:32 * r + 8] * right_ok
-    ct[0] = cf[NARROW:2 * NARROW].astype(BF16)
-    ct[1] = cf[4 * NARROW:5 * NARROW].astype(BF16)
-    ch = go([copy(ct.at[n], hr.at[n], ch_sem, n, side(2 * n - 1, 0)) for n in range(2)])
-
+    for c in e1:
+        c.wait_recv()
     pl.semaphore_wait(known.at[1], 2)
     tell(2)
-
-    for c in e1:
-        c.wait_recv()
     for r in range(18):
         row_ok = top_ok if r < RIM else bottom_ok if r >= RIM + 8 else None
         base = 8 + r * WIDE
@@ -200,6 +185,19 @@
         act[4 * q * WIDE:(4 * q + 4) * WIDE] = own + pre * jax.nn.sigmoid(pre)
         if q in (1, 2):
             pre_l[(q - 1) * 4 * WIDE:q * 4 * WIDE] = pre
+
+    for c in cot_copies:
+        c.wait_recv()
+    cot_tile = cot_recv[:, 0].reshape(256, 128).astype(F32).T
+    cot_beside = cot_recv[:, 1].reshape(256, 128).astype(F32).T
+    for r in range(4):
+        base = (r + 1) * NARROW
+        cf[base:base + 8] = cot_beside[32 * r + 24:32 * r + 32] * left_ok
+        cf[base + 8:base + 40] = cot_tile[32 * r:32 * r + 32]
+        cf[base + 40:base + 48] = cot_beside[32 * r:32 * r + 8] * right_ok
+    ct[0] = cf[NARROW:2 * NARROW].astype(BF16)
+    ct[1] = cf[4 * NARROW:5 * NARROW].astype(BF16)
+    ch = go([copy(ct.at[n], hr.at[n], ch_sem, n, side(2 * n - 1, 0)) for n in range(2)])
 
     for rr in range(16):
         for q in range(2):
@@ -238,12 +236,12 @@
         return pl.ds(pl.multiple_of(half * 128, 128), 128)
 
     theirs = gate_own[:, half_lanes(other)]
+    a_pair = []
     for ky in range(3):
         part = dot_tn(im_n[(1 + ky) * NARROW:(5 + ky) * NARROW], theirs)
-        a_pair_s[48 * ky:48 * ky + 48] = part.astype(BF16).reshape(48, 16, 128)
-    a_pair = go([copy(a_pair_s, a_pair_r, pair_sem, 0, pair_dev)])
-    pl.semaphore_wait(known.at[2], 2)
-    tell(3)
+        third = slice(48 * ky, 48 * ky + 48)
+        a_pair_s[third] = part.astype(BF16).reshape(48, 16, 128)
+        a_pair.extend(go([copy(a_pair_s.at[third], a_pair_r.at[third], pair_sem, (0, 2, 12)[ky], pair_dev)]))
     mine = gate_own[:, half_lanes(core)]
     for ky in range(3):
         neck_own[48 * ky:48 * ky + 48] = dot_tn(im_n[(1 + ky) * NARROW:(5 + ky) * NARROW], mine).reshape(48, 16, 128)
@@ -254,8 +252,9 @@
     def b_piece_of(o):
         return b_work.at[o]
 
-    a_pair[0].wait_recv()
     for n in range(16):
+        if n in (0, 5, 10):
+            a_pair[n // 5].wait_recv()
         part = slice(n * NECK_TILES, (n + 1) * NECK_TILES)
         a_work[n // 4, n % 4] = (neck_own[part] + a_pair_r[part].astype(F32)).astype(BF16)
     near = []
@@ -263,6 +262,8 @@
         near.append(copy(a_work.at[(x + k) % 4, :, 0:ROUTE], near_a.at[k], near_sem, k, x_peer[k]))
         near.append(copy(a_work.at[:, (y + k) % 4, ROUTE:], near_b.at[k], near_sem, 4 + k, y_peer[k]))
     go(near)
+    pl.semaphore_wait(known.at[2], 2)
+    tell(3)
 
     for c in ch:
         c.wait_recv()
@@ -572,7 +573,7 @@
             v(16, REST_TILES, 16, 128), v(16, REST_TILES, 16, 128), v(16, REST_TILES, 16, 128), v(16, REST_TILES, 16, 128),
             v(REST_TILES, 16, 128), v(16, 16, 128), v(REST_TILES, 16, 128),
             dma((5,)), dma((2, 8)), dma((2, 16)), dma((2, 8)), dma((2, 16)), dma((2, 8)),
-            dma((2, 12)), dma((2, 32)), dma((2, 32)), dma((2, 32)), dma((2, 32)), dma((2, 8)), dma((2, 8)), dma((2, 8)), dma((2, 8)),
+            dma((2, 13)), dma((2, 32)), dma((2, 32)), dma((2, 32)), dma((2, 32)), dma((2, 8)), dma((2, 8)), dma((2, 8)), dma((2, 8)),
             pltpu.SemaphoreType.REGULAR((5,)),
         ],
         compiler_params=pltpu.CompilerParams(

time: 69.8 us -> 69.8 us (level)
  no operation moved by 1% of the time
where the time goes in v8:
time: 69.8 us; the launch traced here: 69.6 us
  Pallas kernels  69 us (99%)
    pallas_call x1, Pallas kernels, local(): pl.pallas_call(functools.partial(kernel, (neck_scale, level_scale)), out_...  67.7 us

profile of v8, /device:TPU:1, one launch (start us, length us, event | category | flops | bytes accessed | tf_op | source)
XLA Modules:
  0.0 69.6 jit_solution(16955023528163399962)
XLA Ops:
  0.6 67.7 %shard_map.92 = (bf16[4,16,512]{2,1,0:T(8,128)(2,1)S(1)}, bf16[8,64,128]{2,1,0:T(8,128)(2,1)S(1)}, bf16[2,4,4,9,16,128]{5,4,3,2,1,0:T(8,128)(2,1)S(1)}, bf16[2,16,5,16,128]{4,3,2,1,0:T(8,128)(2,1)S(1)}) custom-call(bf16[8,64,128]{2,1,0:T(8,128)(2,1)} %level_in.1, bf16[3,384,128]{2,1,0:T(8,128)(2,1)} %bitcast.9, bf16[512,256]{1,0:T(8,128)(2,1)} %bitcast.10, ...), custom_call_target="tpu_custom_call" | custom-call | tf_op jit(solution)/shard_map/pallas_call | solution.py:547
  68.3 1.3 %shard_map.93 = (bf16[4,16,512]{2,1,0:T(8,128)(2,1)}, bf16[8,64,128]{2,1,0:T(8,128)(2,1)}, bf16[2,12,3,16,128]{4,3,2,1,0:T(8,128)(2,1)}, bf16[16,2,16,256]{3,2,1,0:T(8,128)(2,1)}, bf16[4,4,9,16,256]{4,3,2,1,0:T(8,128)(2,1)}) custom-call(bf16[4,16,512]{2,1,0:T(8,128)(2,1)S(1)} %get-tuple-element.14.strip, bf16[8,64,128]{2,1,0:T(8,128)(2,1)S(1)} %get-tuple-element.15.level, ...), custom_call_target="tpu_custom_call" | custom-call | tf_op jit(solution)/shard_map/pallas_call | solution.py:591

commit v9 on v8

--- a/solution.py
+++ b/solution.py
@@ -83,7 +83,8 @@
     barrier = pltpu.get_barrier_semaphore()
     x_peer = [None] + [(gy, (x + k) % 4 * 4 + y) for k in range(1, 4)]
     y_peer = [None] + [(gy, x * 4 + (y + k) % 4) for k in range(1, 4)]
-    peers = x_peer[1:] + y_peer[1:] + [side(dy, dx) for dy, dx in SIDES]
+    corners_first = sorted(SIDES, key=lambda e: -abs(e[0]) - abs(e[1]))
+    peers = [side(dy, dx) for dy, dx in corners_first] + x_peer[1:] + y_peer[1:]
     for peer in peers:
         pl.semaphore_signal(barrier, inc=1, device_id=peer, device_id_type=MESH)
 
@@ -245,12 +246,6 @@
     mine = gate_own[:, half_lanes(core)]
     for ky in range(3):
         neck_own[48 * ky:48 * ky + 48] = dot_tn(im_n[(1 + ky) * NARROW:(5 + ky) * NARROW], mine).reshape(48, 16, 128)
-
-    def plane_stage(work, buf, sems, first):
-        return go([copy(work(in_plane(k)), buf.at[k], sems, first + k, plane[k]) for k in FAR_FIRST])
-
-    def b_piece_of(o):
-        return b_work.at[o]
 
     for n in range(16):
         if n in (0, 5, 10):
@@ -318,7 +313,20 @@
     b_work[:, 0:2] = (down + b_pair_r[:, 0:2].astype(F32)).astype(BF16)
     b_work[0:LEVEL_OWNERS, 2:5] = (level + b_pair_r[0:LEVEL_OWNERS, 2:5].astype(F32)).astype(BF16)
     b_work[LEVEL_OWNERS:, 2:5] = nothing
-    b_plane = plane_stage(b_piece_of, b_xy, xy_sem, 16)
+    me_level = gx < LEVEL_OWNERS
+    b_plane = []
+    for k in FAR_FIRST:
+        o = in_plane(k)
+        full = copy(b_work.at[o], b_xy.at[k], xy_sem, 16 + k, plane[k])
+        short = copy(b_work.at[o, 0:2], b_xy.at[k, 0:2], xy_sem, 16 + k, plane[k])
+        b_plane.append((o < LEVEL_OWNERS, full, short))
+
+    def either(cond, one, two):
+        pl.when(cond)(one)
+        pl.when(jnp.logical_not(cond))(two)
+
+    for cond, full, short in b_plane:
+        either(cond, full.start, short.start)
 
     e4_src = {-1: slice(1, 2), 0: slice(1, 9), 1: slice(8, 9)}
     e4_dst = {-1: slice(9, 10), 0: slice(1, 9), 1: slice(0, 1)}
@@ -371,13 +379,11 @@
         for cond, c in copies:
             pl.when(cond)(c.start)
 
-    def plane_sum(piece_of, buf, own_ref, copies, out):
-        for c in copies:
-            c.wait_recv()
-        total = own_ref[...].astype(F32)
+    def b_sum(tiles):
+        total = b_work[gx, tiles].astype(F32)
         for k in range(1, 16):
-            total = total + buf[k].astype(F32)
-        out[...] = total.astype(BF16)
+            total = total + b_xy[k, tiles].astype(F32)
+        b_piece[tiles] = total.astype(BF16)
 
     def owns(first, tiles):
         return (z >= first) & (z < first + tiles)
@@ -420,7 +426,19 @@
     a_piece[ROUTE:] = via_y.astype(BF16)
     a_zs = z_send(a_piece, a_z, NECK_TILES, 0, z_sem, 0)
     start_all(a_zs)
-    plane_sum(b_piece_of, b_xy, b_piece_of(gx), b_plane, b_piece)
+    @pl.when(me_level)
+    def _():
+        for _, full, _ in b_plane:
+            full.wait_recv()
+        b_sum(slice(2, REST_TILES))
+
+    @pl.when(jnp.logical_not(me_level))
+    def _():
+        for _, _, short in b_plane:
+            short.wait_recv()
+        b_piece[2:] = nothing[0]
+
+    b_sum(slice(0, 2))
     b_zs = z_send(b_piece, b_z, REST_TILES, NECK_TILES, z_sem, 16)
     start_all(b_zs)
     for c in e4:
@@ -473,8 +491,21 @@
     go(leg1)
     z_back(b_fin, REST_TILES, NECK_TILES, 16)
     b_all[core, gx] = b_fin[...]
-    b_mine = b_slot(gx)
-    go([copy(b_mine, b_mine, xyb_sem, 16 + k, plane[k]) for k in FAR_FIRST])
+    b_back = []
+    for k in FAR_FIRST:
+        full, short = b_slot(gx), b_all.at[core, gx, 0:2]
+        b_back.append((copy(full, full, xyb_sem, 16 + k, plane[k]), copy(short, short, xyb_sem, 16 + k, plane[k])))
+
+    @pl.when(me_level)
+    def _():
+        for full, _ in b_back:
+            full.start()
+
+    @pl.when(jnp.logical_not(me_level))
+    def _():
+        for _, short in b_back:
+            short.start()
+
     for c in leg1:
         c.wait_recv()
 
@@ -496,15 +527,22 @@
 
     swap(0)
     for k in FAR_FIRST:
-        slot = b_slot(in_plane(k, -1))
-        copy(slot, slot, xyb_sem, 16 + k, plane[k]).wait_recv()
-    go([copy(b_all.at[core], b_all.at[core], pair_sem, 3, pair_dev)])
+        o = in_plane(k, -1)
+        full, short = b_slot(o), b_all.at[core, o, 0:2]
+        full, short = copy(full, full, xyb_sem, 16 + k, plane[k]), copy(short, short, xyb_sem, 16 + k, plane[k])
+        either(o < LEVEL_OWNERS, full.wait_recv, short.wait_recv)
+
+    def b_parts(c):
+        return b_all.at[c, 0:LEVEL_OWNERS], b_all.at[c, LEVEL_OWNERS:, 0:2]
+
+    go([copy(part, part, pair_sem, (3, 13)[n], pair_dev) for n, part in enumerate(b_parts(core))])
     for k in (1, 3, 2):
         bx, by = block_x(core, (x - k + 4) % 4), block_y(core, (y - k + 4) % 4)
         copy(bx, bx, back2_sem, k, x_peer[k]).wait_recv()
         copy(by, by, back2_sem, 4 + k, y_peer[k]).wait_recv()
         swap(k)
-    copy(b_all.at[other], b_all.at[other], pair_sem, 3, pair_dev).wait_recv()
+    for n, part in enumerate(b_parts(other)):
+        copy(part, part, pair_sem, (3, 13)[n], pair_dev).wait_recv()
     for k in range(4):
         bx, by = block_x(other, (x - k + 4) % 4), block_y(other, (y - k + 4) % 4)
         copy(bx, bx, pair_sem, 4 + k, pair_dev).wait_recv()
@@ -512,6 +550,9 @@
 
     for c in sent:
         c.wait_send()
+    for (cond, full, short), (back, back_short) in zip(b_plane, b_back):
+        either(cond, full.wait_send, short.wait_send)
+        either(me_level, back.wait_send, back_short.wait_send)
     for cond, c in a_zs + b_zs:
         pl.when(cond)(c.wait_send)
     z_back_sent(a_fin, NECK_TILES, 0, 0)
@@ -573,7 +614,7 @@
             v(16, REST_TILES, 16, 128), v(16, REST_TILES, 16, 128), v(16, REST_TILES, 16, 128), v(16, REST_TILES, 16, 128),
             v(REST_TILES, 16, 128), v(16, 16, 128), v(REST_TILES, 16, 128),
             dma((5,)), dma((2, 8)), dma((2, 16)), dma((2, 8)), dma((2, 16)), dma((2, 8)),
-            dma((2, 13)), dma((2, 32)), dma((2, 32)), dma((2, 32)), dma((2, 32)), dma((2, 8)), dma((2, 8)), dma((2, 8)), dma((2, 8)),
+            dma((2, 14)), dma((2, 32)), dma((2, 32)), dma((2, 32)), dma((2, 32)), dma((2, 8)), dma((2, 8)), dma((2, 8)), dma((2, 8)),
             pltpu.SemaphoreType.REGULAR((5,)),
         ],
         compiler_params=pltpu.CompilerParams(

time: 69.8 us -> 68.2 us (0.977)
  Pallas kernels: 69 us -> 67.5 us
    pallas_call x1, Pallas kernels: 67.7 us -> 66.1 us  [local(): pl.pallas_call(functools.partial(kernel, (neck_scale, level_scale)), out_...]
where the time goes in v9:
time: 68.2 us; the launch traced here: 68.1 us
  Pallas kernels  67.5 us (99%)
    pallas_call x1, Pallas kernels, local(): pl.pallas_call(functools.partial(kernel, (neck_scale, level_scale)), out_...  66.1 us

profile of v9, /device:TPU:1, one launch (start us, length us, event | category | flops | bytes accessed | tf_op | source)
XLA Modules:
  0.0 68.1 jit_solution(3563975223562508154)
XLA Ops:
  0.6 66.1 %shard_map.92 = (bf16[4,16,512]{2,1,0:T(8,128)(2,1)S(1)}, bf16[8,64,128]{2,1,0:T(8,128)(2,1)S(1)}, bf16[2,4,4,9,16,128]{5,4,3,2,1,0:T(8,128)(2,1)S(1)}, bf16[2,16,5,16,128]{4,3,2,1,0:T(8,128)(2,1)S(1)}) custom-call(bf16[8,64,128]{2,1,0:T(8,128)(2,1)} %level_in.1, bf16[3,384,128]{2,1,0:T(8,128)(2,1)} %bitcast.9, bf16[512,256]{1,0:T(8,128)(2,1)} %bitcast.10, ...), custom_call_target="tpu_custom_call" | custom-call | tf_op jit(solution)/shard_map/pallas_call | solution.py:588
  66.8 1.3 %shard_map.93 = (bf16[4,16,512]{2,1,0:T(8,128)(2,1)}, bf16[8,64,128]{2,1,0:T(8,128)(2,1)}, bf16[2,12,3,16,128]{4,3,2,1,0:T(8,128)(2,1)}, bf16[16,2,16,256]{3,2,1,0:T(8,128)(2,1)}, bf16[4,4,9,16,256]{4,3,2,1,0:T(8,128)(2,1)}) custom-call(bf16[4,16,512]{2,1,0:T(8,128)(2,1)S(1)} %get-tuple-element.14.strip, bf16[8,64,128]{2,1,0:T(8,128)(2,1)S(1)} %get-tuple-element.15.level, ...), custom_call_target="tpu_custom_call" | custom-call | tf_op jit(solution)/shard_map/pallas_call | solution.py:632

commit v10 on v9

--- a/solution.py
+++ b/solution.py
@@ -288,28 +288,29 @@
     for r in range(8):
         rows_r = slice(r * WIDE + 16, r * WIDE + 80)
         gp[r + 1, 16:80] = (lbf[rows_r] * slope_of(pre_l[rows_r])).astype(BF16)
+    def down_terms(half):
+        return down_acc[:, half_lanes(half)].reshape(16, 2, 16, 128)
+
+    def level_terms(half):
+        return level_acc[pl.ds(pl.multiple_of(half * 576, 576), 576), :].reshape(LEVEL_OWNERS, 3, 16, 128)
+
+    down_acc[...] = dot_tn(dn[2 * NARROW:6 * NARROW], ng[...])
+    b_pair_s[:, 0:2] = down_terms(other).astype(BF16)
+    b_pair = go([copy(b_pair_s.at[:, 0:2], b_pair_r.at[:, 0:2], pair_sem, 1, pair_dev)])
     own_gate = gp[1:9, 16:80].reshape(512, 128)
     for ky in range(3):
         window = jnp.concatenate(
             [im_l[(4 + ky + r) * WIDE + 16:(4 + ky + r) * WIDE + 80] for r in range(8)], axis=0
         )
         level_acc[ky * 384:(ky + 1) * 384] = dot_tn(window, own_gate)
-    down_acc[...] = dot_tn(dn[2 * NARROW:6 * NARROW], ng[...])
-
-    def rest_terms(half):
-        down = down_acc[:, half_lanes(half)].reshape(16, 2, 16, 128)
-        level = level_acc[pl.ds(pl.multiple_of(half * 576, 576), 576), :].reshape(LEVEL_OWNERS, 3, 16, 128)
-        return down, level
-
-    down, level = rest_terms(other)
     nothing = jnp.zeros((16 - LEVEL_OWNERS, 3, 16, 128), BF16)
-    b_pair_s[:, 0:2] = down.astype(BF16)
-    b_pair_s[0:LEVEL_OWNERS, 2:5] = level.astype(BF16)
-    b_pair_s[LEVEL_OWNERS:, 2:5] = nothing
-    b_pair = go([copy(b_pair_s, b_pair_r, pair_sem, 1, pair_dev)])
-
-    b_pair[0].wait_recv()
-    down, level = rest_terms(core)
+    b_pair_s[0:LEVEL_OWNERS, 2:5] = level_terms(other).astype(BF16)
+    with_level = b_pair_s.at[0:LEVEL_OWNERS, 2:5]
+    b_pair.extend(go([copy(with_level, b_pair_r.at[0:LEVEL_OWNERS, 2:5], pair_sem, 14, pair_dev)]))
+
+    for c in b_pair:
+        c.wait_recv()
+    down, level = down_terms(core), level_terms(core)
     b_work[:, 0:2] = (down + b_pair_r[:, 0:2].astype(F32)).astype(BF16)
     b_work[0:LEVEL_OWNERS, 2:5] = (level + b_pair_r[0:LEVEL_OWNERS, 2:5].astype(F32)).astype(BF16)
     b_work[LEVEL_OWNERS:, 2:5] = nothing
@@ -614,7 +615,7 @@
             v(16, REST_TILES, 16, 128), v(16, REST_TILES, 16, 128), v(16, REST_TILES, 16, 128), v(16, REST_TILES, 16, 128),
             v(REST_TILES, 16, 128), v(16, 16, 128), v(REST_TILES, 16, 128),
             dma((5,)), dma((2, 8)), dma((2, 16)), dma((2, 8)), dma((2, 16)), dma((2, 8)),
-            dma((2, 14)), dma((2, 32)), dma((2, 32)), dma((2, 32)), dma((2, 32)), dma((2, 8)), dma((2, 8)), dma((2, 8)), dma((2, 8)),
+            dma((2, 15)), dma((2, 32)), dma((2, 32)), dma((2, 32)), dma((2, 32)), dma((2, 8)), dma((2, 8)), dma((2, 8)), dma((2, 8)),
             pltpu.SemaphoreType.REGULAR((5,)),
         ],
         compiler_params=pltpu.CompilerParams(

time: 68.2 us -> 67.8 us (level)
  no operation moved by 1% of the time
where the time goes in v10:
time: 67.8 us; the launch traced here: 67.7 us
  Pallas kernels  67 us (99%)
    pallas_call x1, Pallas kernels, local(): pl.pallas_call(functools.partial(kernel, (neck_scale, level_scale)), out_...  65.7 us

profile of v10, /device:TPU:1, one launch (start us, length us, event | category | flops | bytes accessed | tf_op | source)
XLA Modules:
  0.0 67.7 jit_solution(5841015711754294360)
XLA Ops:
  0.6 65.7 %shard_map.92 = (bf16[4,16,512]{2,1,0:T(8,128)(2,1)S(1)}, bf16[8,64,128]{2,1,0:T(8,128)(2,1)S(1)}, bf16[2,4,4,9,16,128]{5,4,3,2,1,0:T(8,128)(2,1)S(1)}, bf16[2,16,5,16,128]{4,3,2,1,0:T(8,128)(2,1)S(1)}) custom-call(bf16[8,64,128]{2,1,0:T(8,128)(2,1)} %level_in.1, bf16[3,384,128]{2,1,0:T(8,128)(2,1)} %bitcast.9, bf16[512,256]{1,0:T(8,128)(2,1)} %bitcast.10, ...), custom_call_target="tpu_custom_call" | custom-call | tf_op jit(solution)/shard_map/pallas_call | solution.py:589
  66.3 1.3 %shard_map.93 = (bf16[4,16,512]{2,1,0:T(8,128)(2,1)}, bf16[8,64,128]{2,1,0:T(8,128)(2,1)}, bf16[2,12,3,16,128]{4,3,2,1,0:T(8,128)(2,1)}, bf16[16,2,16,256]{3,2,1,0:T(8,128)(2,1)}, bf16[4,4,9,16,256]{4,3,2,1,0:T(8,128)(2,1)}) custom-call(bf16[4,16,512]{2,1,0:T(8,128)(2,1)S(1)} %get-tuple-element.14.strip, bf16[8,64,128]{2,1,0:T(8,128)(2,1)S(1)} %get-tuple-element.15.level, ...), custom_call_target="tpu_custom_call" | custom-call | tf_op jit(solution)/shard_map/pallas_call | solution.py:633
